TPU v7x, 32 devices: a whole 2x2x4 slice. The times are simulated.
32 devices in a mesh: dp: 8 (over y, x, core), branch: 4 (over z).
Axes of the slice: x: 2, y: 2, z: 4, core: 2. Of those that a mesh axis runs over, the one named last changes fastest.
Arguments:
- tokens: bfloat16 [8192, 2048], P(('dp', 'branch')), may hold values from -6 to 6
- doc_ids: int32 [8192], P('dp'), may hold values from 0 to 15, as said below
- real_rows: int32 [8192], P('dp'), may hold values from 0 to 1, as said below
- cotangent: bfloat16 [8192, 2048], P(('dp', 'branch')), may hold values from -6 to 6
- norm_gain: float32 [2048], P(('dp', 'branch')), may hold values from 0.5 to 1.5
- norm_shift: float32 [2048], P(('dp', 'branch')), may hold values from -2 to 2
- out_bias: float32 [2048], P(('dp', 'branch')), may hold values from -2 to 2
- w_qkv: float32 [3, 2048, 2048], P(None, 'dp', 'branch'), may hold values from -0.125 to 0.125
- b_qkv: float32 [3, 32, 64], P(None, 'branch', 'dp'), may hold values from -3 to 3
- w_out: float32 [2048, 2048], P('branch', 'dp'), may hold values from -0.75 to 0.75
- w_up: float32 [2048, 8192], P('dp', 'branch'), may hold values from -0.125 to 0.125
- b_up: float32 [64, 128], P('branch', 'dp'), may hold values from -3 to 3
- w_down: float32 [8192, 2048], P('branch', 'dp'), may hold values from -0.0625 to 0.0625
Outputs:
- block_out: bfloat16 [8192, 2048], P(('dp', 'branch'))
- tokens_grad: bfloat16 [8192, 2048], P(('dp', 'branch'))
- norm_gain_grad: float32 [2048], P(('dp', 'branch'))
- norm_shift_grad: float32 [2048], P(('dp', 'branch'))
- out_bias_grad: float32 [2048], P(('dp', 'branch'))
- w_qkv_grad: float32 [3, 2048, 2048], P(None, 'dp', 'branch')
- b_qkv_grad: float32 [3, 32, 64], P(None, 'branch', 'dp')
- w_out_grad: float32 [2048, 2048], P('branch', 'dp')
- w_up_grad: float32 [2048, 8192], P('dp', 'branch')
- b_up_grad: float32 [64, 128], P('branch', 'dp')
- w_down_grad: float32 [8192, 2048], P('branch', 'dp')
Inputs may be any that keep to these rules, and one draw needn't show every extreme that they name: `doc_ids`: within each aligned block of 1024 slots the ids start at 0 and never fall; a sequence has 64 times a power of two slots, up to 1024; some sequence has exactly 1024; all padding slots of a block share the id 1024 // 64 - 1, which real slots of a block with padding never take; the last block ends in padding. `real_rows`: within each block, the slots of whole sequences come first and are 1; the rest of the block is 0; every block holds a sequence; the last block ends in padding.
All inputs are finite; a program needn't handle non-finite values.
Results may differ from a plain program's by a relative error of at most 0.014.
Values may be sent and summed in bfloat16 or wider, within the bound.
A program may use at most 192 MiB of HBM per device.

v0:
```python
import math

import jax
import jax.numpy as jnp
from jax import lax
from jax.sharding import PartitionSpec as P

HEAD_DIM = 64
ROT = 32


NORM_EPS = 1e-05
NEGATIVE = -1e30


def positions(doc_rows):
    row_count = doc_rows.shape[0]
    row_index = jnp.arange(row_count, dtype=jnp.int32)
    change = jnp.concatenate([jnp.ones((1,), dtype=bool), doc_rows[1:] != doc_rows[:-1]])
    begins = lax.cummax(jnp.where(change, row_index, jnp.zeros_like(row_index)), axis=0)
    return row_index - begins


def rotary_tables(doc_rows):
    places = positions(doc_rows).astype(jnp.float32)
    half_rot = ROT // 2
    frequency = 10000.0 ** (-2.0 * jnp.arange(half_rot, dtype=jnp.float32) / ROT)
    angles = places[:, None] * frequency[None, :]
    return (jnp.cos(angles), jnp.sin(angles))


def rotate(values, cosine, sine_tab):
    half_rot = ROT // 2
    first_half = values[..., :half_rot]
    second_half = values[..., half_rot : 2 * half_rot]
    remain = values[..., 2 * half_rot :]
    return jnp.concatenate(
        [
            first_half * cosine - second_half * sine_tab,
            second_half * cosine + first_half * sine_tab,
            remain,
        ],
        axis=-1,
    )


def unrotate(values, cosine, sine_tab):
    half_rot = ROT // 2
    first_half = values[..., :half_rot]
    second_half = values[..., half_rot : 2 * half_rot]
    remain = values[..., 2 * half_rot :]
    return jnp.concatenate(
        [
            first_half * cosine + second_half * sine_tab,
            second_half * cosine - first_half * sine_tab,
            remain,
        ],
        axis=-1,
    )


def gelu_tanh(values):
    return jax.nn.gelu(values, approximate=True)


def contract_rows(left, right):
    return lax.dot_general(
        left, right, (((0,), (0,)), ((), ())), preferred_element_type=jnp.float32
    )


def contract_cols(left, right):
    return lax.dot_general(
        left, right, (((1,), (1,)), ((), ())), preferred_element_type=jnp.float32
    )


def masked_scores(query_blk, keys_rot, doc_query, doc_rows, query_index, key_index, factor):
    scores = (
        jnp.einsum("hqd,hkd->hqk", query_blk, keys_rot, preferred_element_type=jnp.float32) * factor
    )
    allowed = (doc_query[:, None] == doc_rows[None, :]) & (
        key_index[None, :] <= query_index[:, None]
    )
    return jnp.where(allowed[None], scores, NEGATIVE)


def local(
    tokens,
    doc_ids,
    real_rows,
    cotangent,
    norm_gain,
    norm_shift,
    out_bias,
    w_qkv,
    b_qkv,
    w_out,
    w_up,
    b_up,
    w_down,
):
    member = lax.axis_index("branch")
    my_rows = tokens.shape[0]
    broadcast_gain, broadcast_shift, bias_full = (
        lax.all_gather(norm_gain.astype(jnp.bfloat16), ("dp", "branch"), axis=0, tiled=True),
        lax.all_gather(norm_shift.astype(jnp.bfloat16), ("dp", "branch"), axis=0, tiled=True),
        lax.all_gather(out_bias.astype(jnp.bfloat16), ("dp", "branch"), axis=0, tiled=True),
    )
    broadcast_gain = broadcast_gain.astype(jnp.float32)
    broadcast_shift = broadcast_shift.astype(jnp.float32)
    bias_full = bias_full.astype(jnp.float32)
    xfloat = tokens.astype(jnp.float32)
    mean_removed = xfloat - jnp.mean(xfloat, axis=-1, keepdims=True)
    inverse_deviation = lax.rsqrt(
        jnp.mean(mean_removed * mean_removed, axis=-1, keepdims=True) + NORM_EPS
    )
    standardized_input = mean_removed * inverse_deviation
    normed_input = (standardized_input * broadcast_gain + broadcast_shift).astype(jnp.bfloat16)
    gathered = lax.all_gather(normed_input, "branch", axis=0, tiled=True)
    row_count = gathered.shape[0]
    attn_w, attn_b, out_w = (
        lax.all_gather(w_qkv.astype(jnp.bfloat16), "dp", axis=1, tiled=True),
        lax.all_gather(b_qkv.astype(jnp.bfloat16), "dp", axis=2, tiled=True),
        lax.all_gather(w_out.astype(jnp.bfloat16), "dp", axis=1, tiled=True),
    )
    up_w, up_b, down_w = (
        lax.all_gather(w_up.astype(jnp.bfloat16), "dp", axis=0, tiled=True),
        lax.all_gather(b_up.astype(jnp.bfloat16), "dp", axis=1, tiled=True),
        lax.all_gather(w_down.astype(jnp.bfloat16), "dp", axis=1, tiled=True),
    )
    local_cols = attn_w.shape[2]
    local_heads = local_cols // HEAD_DIM
    project = jnp.einsum("td,cde->cte", gathered, attn_w, preferred_element_type=jnp.float32)
    project = project + attn_b.astype(jnp.float32).reshape(3, 1, local_cols)
    heads_view = project.reshape(3, row_count, local_heads, HEAD_DIM).transpose(0, 2, 1, 3)
    cosine, sine_tab = rotary_tables(doc_ids)
    queries = rotate(heads_view[0], cosine, sine_tab).astype(jnp.bfloat16)
    keys_rot = rotate(heads_view[1], cosine, sine_tab).astype(jnp.bfloat16)
    values_low = heads_view[2].astype(jnp.bfloat16)
    block_rows = min(512, row_count)
    blocks = row_count // block_rows
    row_index = jnp.arange(row_count, dtype=jnp.int32)
    factor = 1.0 / math.sqrt(HEAD_DIM)
    query_blocks = queries.reshape(local_heads, blocks, block_rows, HEAD_DIM).transpose(1, 0, 2, 3)
    doc_blocks = doc_ids.reshape(blocks, block_rows)
    index_blocks = row_index.reshape(blocks, block_rows)

    def forward_block(pieces):
        query_blk, doc_query, query_index = pieces
        masked = masked_scores(
            query_blk, keys_rot, doc_query, doc_ids, query_index, row_index, factor
        )
        row_top = jnp.max(masked, axis=-1, keepdims=True)
        weights_exp = jnp.exp(masked - row_top)
        row_total = jnp.sum(weights_exp, axis=-1, keepdims=True)
        probability = (weights_exp / row_total).astype(jnp.bfloat16)
        result = jnp.einsum(
            "hqk,hkd->hqd", probability, values_low, preferred_element_type=jnp.float32
        )
        return (result.astype(jnp.bfloat16), (row_top + jnp.log(row_total))[..., 0])

    attended, log_total = lax.map(forward_block, (query_blocks, doc_blocks, index_blocks))
    flat_out = attended.transpose(0, 2, 1, 3).reshape(row_count, local_cols)
    hidden_pre = jnp.dot(gathered, up_w, preferred_element_type=jnp.float32) + up_b.astype(
        jnp.float32
    ).reshape(-1)
    activated = gelu_tanh(hidden_pre).astype(jnp.bfloat16)
    partial_value = jnp.dot(flat_out, out_w, preferred_element_type=jnp.float32)
    partial_value = partial_value + jnp.dot(activated, down_w, preferred_element_type=jnp.float32)
    summed = lax.psum_scatter(
        partial_value.astype(jnp.bfloat16), "branch", scatter_dimension=0, tiled=True
    ).astype(jnp.float32)
    my_real = lax.dynamic_slice_in_dim(real_rows, member * my_rows, my_rows).astype(jnp.float32)
    block_out = (xfloat + my_real[:, None] * (summed + bias_full)).astype(jnp.bfloat16)
    masked_cot = (cotangent.astype(jnp.float32) * my_real[:, None]).astype(jnp.bfloat16)
    cot_all = lax.all_gather(masked_cot, "branch", axis=0, tiled=True)
    bias_part = jnp.sum(masked_cot, axis=0, dtype=jnp.float32)
    down_grad = contract_rows(activated, cot_all)
    hidden_grad = contract_cols(cot_all, down_w)
    gelu_value, gelu_pull = jax.vjp(gelu_tanh, hidden_pre)
    pre_grad = gelu_pull(hidden_grad)[0].astype(jnp.bfloat16)
    up_grad = contract_rows(gathered, pre_grad)
    up_bias_grad = jnp.sum(pre_grad, axis=0, dtype=jnp.float32).reshape(up_b.shape)
    normed_grad = contract_cols(pre_grad, up_w)
    out_grad_w = contract_rows(flat_out, cot_all)
    flat_dout = contract_cols(cot_all, out_w).astype(jnp.bfloat16)
    dout_blocks = flat_dout.reshape(blocks, block_rows, local_heads, HEAD_DIM).transpose(0, 2, 1, 3)

    def backward_block(running_acc, pieces):
        key_acc, value_acc = running_acc
        query_blk, dout_blk, log_blk, doc_query, query_index = pieces
        masked = masked_scores(
            query_blk, keys_rot, doc_query, doc_ids, query_index, row_index, factor
        )
        probability = jnp.exp(masked - log_blk[..., None])
        value_acc = value_acc + jnp.einsum(
            "hqk,hqd->hkd",
            probability.astype(jnp.bfloat16),
            dout_blk,
            preferred_element_type=jnp.float32,
        )
        prob_grad = jnp.einsum(
            "hqd,hkd->hqk", dout_blk, values_low, preferred_element_type=jnp.float32
        )
        score_grad = probability * (
            prob_grad - jnp.sum(probability * prob_grad, axis=-1, keepdims=True)
        )
        score_grad = score_grad.astype(jnp.bfloat16)
        query_grad = (
            jnp.einsum("hqk,hkd->hqd", score_grad, keys_rot, preferred_element_type=jnp.float32)
            * factor
        )
        key_acc = (
            key_acc
            + jnp.einsum("hqk,hqd->hkd", score_grad, query_blk, preferred_element_type=jnp.float32)
            * factor
        )
        return ((key_acc, value_acc), query_grad)

    zero_acc = jnp.zeros((local_heads, row_count, HEAD_DIM), jnp.float32)
    (key_grad, value_grad), query_grads = lax.scan(
        backward_block,
        (zero_acc, zero_acc),
        (query_blocks, dout_blocks, log_total, doc_blocks, index_blocks),
    )
    query_grad = query_grads.transpose(1, 0, 2, 3).reshape(local_heads, row_count, HEAD_DIM)
    stacked = jnp.stack(
        [unrotate(query_grad, cosine, sine_tab), unrotate(key_grad, cosine, sine_tab), value_grad]
    )
    qkv_grad = stacked.transpose(0, 2, 1, 3).reshape(3, row_count, local_cols).astype(jnp.bfloat16)
    attn_grad_w = jnp.einsum("td,cte->cde", gathered, qkv_grad, preferred_element_type=jnp.float32)
    attn_bias_grad = jnp.sum(qkv_grad, axis=1, dtype=jnp.float32).reshape(attn_b.shape)
    normed_grad = normed_grad + jnp.einsum(
        "cte,cde->td", qkv_grad, attn_w, preferred_element_type=jnp.float32
    )
    w_qkv_grad, b_qkv_grad, w_out_grad, w_up_grad, b_up_grad, w_down_grad = (
        lax.psum_scatter(
            attn_grad_w.astype(jnp.bfloat16), "dp", scatter_dimension=1, tiled=True
        ).astype(jnp.float32),
        lax.psum_scatter(
            attn_bias_grad.astype(jnp.bfloat16), "dp", scatter_dimension=2, tiled=True
        ).astype(jnp.float32),
        lax.psum_scatter(
            out_grad_w.astype(jnp.bfloat16), "dp", scatter_dimension=1, tiled=True
        ).astype(jnp.float32),
        lax.psum_scatter(
            up_grad.astype(jnp.bfloat16), "dp", scatter_dimension=0, tiled=True
        ).astype(jnp.float32),
        lax.psum_scatter(
            up_bias_grad.astype(jnp.bfloat16), "dp", scatter_dimension=1, tiled=True
        ).astype(jnp.float32),
        lax.psum_scatter(
            down_grad.astype(jnp.bfloat16), "dp", scatter_dimension=1, tiled=True
        ).astype(jnp.float32),
    )
    normed_total_sum = lax.psum_scatter(
        normed_grad.astype(jnp.bfloat16), "branch", scatter_dimension=0, tiled=True
    ).astype(jnp.float32)
    scaled_input = normed_total_sum * broadcast_gain
    input_grad = inverse_deviation * (
        scaled_input
        - jnp.mean(scaled_input, axis=-1, keepdims=True)
        - standardized_input * jnp.mean(scaled_input * standardized_input, axis=-1, keepdims=True)
    )
    tokens_grad = (cotangent.astype(jnp.float32) + input_grad).astype(jnp.bfloat16)
    gain_sums, shift_sums, bias_sums = (
        lax.psum_scatter(
            jnp.sum(normed_total_sum * standardized_input, axis=0),
            ("dp", "branch"),
            scatter_dimension=0,
            tiled=True,
        ),
        lax.psum_scatter(
            jnp.sum(normed_total_sum, axis=0), ("dp", "branch"), scatter_dimension=0, tiled=True
        ),
        lax.psum_scatter(bias_part, ("dp", "branch"), scatter_dimension=0, tiled=True),
    )
    return (
        block_out,
        tokens_grad,
        gain_sums,
        shift_sums,
        bias_sums,
        w_qkv_grad,
        b_qkv_grad,
        w_out_grad,
        w_up_grad,
        b_up_grad,
        w_down_grad,
    )


def solution(mesh):
    in_specs = (
        P(("dp", "branch"), None),
        P("dp"),
        P("dp"),
        P(("dp", "branch"), None),
        P(("dp", "branch")),
        P(("dp", "branch")),
        P(("dp", "branch")),
        P(None, "dp", "branch"),
        P(None, "branch", "dp"),
        P("branch", "dp"),
        P("dp", "branch"),
        P("branch", "dp"),
        P("branch", "dp"),
    )
    out_specs = (
        P(("dp", "branch"), None),
        P(("dp", "branch"), None),
        P(("dp", "branch")),
        P(("dp", "branch")),
        P(("dp", "branch")),
        P(None, "dp", "branch"),
        P(None, "branch", "dp"),
        P("branch", "dp"),
        P("dp", "branch"),
        P("branch", "dp"),
        P("branch", "dp"),
    )
    return jax.shard_map(local, mesh=mesh, in_specs=in_specs, out_specs=out_specs, check_vma=False)
```

profile of v0, /device:TPU:1, one launch (start us, length us, event | category | flops | bytes accessed | tf_op | source)
XLA Modules:
  0.0 864.7 jit_solution(15730923838003511770)
XLA Ops:
  10.5 3.1 convert_reduce_fusion.2
  14.5 41.5 %all-reduce.8 = (bf16[2048]{0:T(1024)(128)(2,1)S(1)}, bf16[2048]{0:T(1024)(128)(2,1)S(1)}, bf16[2048]{0:T(1024)(128)(2,1)}) all-reduce(bf16[2048]{0:T(1024)(128)(2,1)S(1)} %dynamic-update-slice.1, bf16[2048]{0:T(1024)(128)(2,1)S(1)} %dynamic-update-slice, ...), channel_id=1, replica_groups=mesh['dp'=8,'branch'=4] {'dp','branch'}, use_global_device_ids=true, to_apply=%add.1 | all-reduce | flops 6144 | bytes 24576
  65.9 10.9 %all_gather.37 = bf16[3,8,64]{1,0,2:T(4,128)(2,1)S(1)} all-gather(bf16[3,8,8]{1,0,2:T(4,128)(2,1)S(1)} %copy.73), channel_id=1, replica_groups=mesh['dp'=8,'branch'=4] {'dp'}, dimensions={2}, use_global_device_ids=true | all-gather | bytes 3456 | tf_op jit(solution)/shard_map/all_gather | solution.py:124
  77.7 8.1 all_gather.40
  86.8 37.1 %all-gather.17.cloned.1.call-done = bf16[1024,2048]{1,0:T(8,128)(2,1)} async-done(((bf16[256,2048]{1,0:T(8,128)(2,1)}), bf16[1024,2048]{1,0:T(8,128)(2,1)}) %all-gather.17.cloned.1.call-update) | async-done | bytes 4194320 | tf_op jit(solution)/shard_map/all_gather | solution.py:177
  124.0 5.2 convolution_convert_fusion.3
  131.9 73.5 %all-gather.7.cloned.1.call-done = bf16[1024,2048]{1,0:T(8,128)(2,1)} async-done(((bf16[256,2048]{1,0:T(8,128)(2,1)}), bf16[1024,2048]{1,0:T(8,128)(2,1)}) %all-gather.7.cloned.1.call-update) | async-done | bytes 4194320 | tf_op jit(solution)/shard_map/all_gather | solution.py:120
  205.4 47.4 %all-gather.9.cloned.1.call-done = bf16[3,2048,512]{1,2,0:T(8,128)(2,1)} async-done(((bf16[3,256,512]{1,2,0:T(8,128)(2,1)}), bf16[3,2048,512]{1,2,0:T(8,128)(2,1)}) %all-gather.9.cloned.1.call-update) | async-done | bytes 6291472 | tf_op jit(solution)/shard_map/all_gather | solution.py:123
  252.8 10.1 %broadcast_add_fusion = f32[1024,3,512]{0,2,1:T(8,128)S(1)} fusion(f32[3,512]{1,0:T(4,128)S(1)} %reshape.336, bf16[3,2048,512]{1,2,0:T(8,128)(2,1)} %all-gather.9.cloned.1.call-done, bf16[1024,2048]{1,0:T(8,128)(2,1)} %all-gather.7.cloned.1.call-done), kind=kOutput, calls=%fused_computation.73 | convolution fusion | flops 6444023808 | bytes 16783360 | tf_op jit(solution)/shard_map/td,cde->cte/dot_general | solution.py:134
  266.4 31.2 %while.28 = (s32[]{:T(128)}, bf16[2,8,512,64]{2,3,1,0:T(8,128)(2,1)S(1)}, f32[2,8,512]{2,1,0:T(8,128)}, s32[2,512]{1,0:T(2,128)S(1)}, s32[1024]{0:T(1024)S(1)}, ...) while((s32[]{:T(128)}, ...), condition=%wide.region_7.8_spmd.clone, body=%wide.region_4.7_spmd.clone.sunk | while | flops 1125904384 | bytes 55723116 | solution.py:163
  267.0 4.1 fusion.124
  271.1 4.2 fusion.125
  276.0 5.9 fusion.126
  282.5 4.3 fusion.124
  286.8 4.2 fusion.125
  291.7 5.9 fusion.126
  298.5 96.7 %while.29 = (s32[]{:T(128)}, f32[8,1024,64]{1,2,0:T(8,128)}, f32[8,1024,64]{1,2,0:T(8,128)}, f32[2,8,512,64]{2,3,1,0:T(8,128)}, s32[2,512]{1,0:T(2,128)S(1)}, /*...) while((s32[]{:T(128)}, f32[8,1024,64]{1,2,0:T(8,128)}, ...), condition=%wide.region_11.12_spmd.clone, body=%wide.region_9.11_spmd.clone.sunk | while | flops 2726555648 | bytes 229869888 | solution.py:222
  300.1 3.8 fusion.136
  304.5 11.4 %multiply_reduce_fusion.2 = (f32[8,512]{1,0:T(8,128)}, f32[8,512,1024]{2,1,0:T(8,128)}) fusion(f32[8,512,1024]{2,1,0:T(8,128)S(1)} %fusion.136, f32[8,512]{1,0:T(8,128)} %dynamic-slice_bitcast_fusion.2, bf16[8,1024,64]{1,2,0:T(8,128)(2,1)S(1)} %get-tuple-element.598, bf16[2,8,512,64]{2,3,1,0:T(8,128)(2,1)} %get-tuple-element.597, ...), kind=kOutput, calls=%fused_computation.23.clone.1 | convolution fusion | flops 557838336 | bytes 35684864 | tf_op jit(solution)/shard_map/while/body/eval_jaxpr/hqd,hkd->hqk/dot_general | solution.py:80
  316.0 10.8 %multiply_convert_fusion.5 = bf16[8,512,1024]{2,1,0:T(8,128)(2,1)} fusion(f32[8,512,1024]{2,1,0:T(8,128)} %get-tuple-element.530, f32[8,512,1024]{2,1,0:T(8,128)S(1)} %fusion.136, f32[8,512]{1,0:T(8,128)} %get-tuple-element.531), kind=kLoop, calls=%fused_computation.22.clone.1 | loop fusion | flops 12582912 | bytes 41959424 | tf_op jit(solution)/shard_map/while/body/eval_jaxpr/convert_element_type | solution.py:209
  326.8 7.2 fusion.138
  334.0 5.5 select_add_fusion.4
  339.5 4.5 copy-done
  344.2 2.9 select_add_fusion.5
  348.5 3.8 fusion.136
  352.9 11.5 %multiply_reduce_fusion.2 = (f32[8,512]{1,0:T(8,128)}, f32[8,512,1024]{2,1,0:T(8,128)}) fusion(f32[8,512,1024]{2,1,0:T(8,128)S(1)} %fusion.136, f32[8,512]{1,0:T(8,128)} %dynamic-slice_bitcast_fusion.2, bf16[8,1024,64]{1,2,0:T(8,128)(2,1)S(1)} %get-tuple-element.598, bf16[2,8,512,64]{2,3,1,0:T(8,128)(2,1)} %get-tuple-element.597, ...), kind=kOutput, calls=%fused_computation.23.clone.1 | convolution fusion | flops 557838336 | bytes 35684864 | tf_op jit(solution)/shard_map/while/body/eval_jaxpr/hqd,hkd->hqk/dot_general | solution.py:80
  364.4 9.4 %multiply_convert_fusion.5 = bf16[8,512,1024]{2,1,0:T(8,128)(2,1)} fusion(f32[8,512,1024]{2,1,0:T(8,128)} %get-tuple-element.530, f32[8,512,1024]{2,1,0:T(8,128)S(1)} %fusion.136, f32[8,512]{1,0:T(8,128)} %get-tuple-element.531), kind=kLoop, calls=%fused_computation.22.clone.1 | loop fusion | flops 12582912 | bytes 41959424 | tf_op jit(solution)/shard_map/while/body/eval_jaxpr/convert_element_type | solution.py:209
  373.7 7.3 fusion.138
  381.0 5.5 select_add_fusion.4
  386.5 3.6 copy-done
  390.3 4.5 select_add_fusion.5
  400.0 3.7 convolution_convert_fusion.2
  406.4 14.7 %fusion.74 = f32[1024,2048]{1,0:T(8,128)} fusion(bf16[1024,2048]{1,0:T(8,128)(2,1)} %all-gather.7.cloned.1.call-done, bf16[2048,2048]{1,0:T(8,128)(2,1)} %all-gather.13.cloned.1.call-done), kind=kOutput, calls=%fused_computation.140 | convolution fusion | flops 8589934592 | bytes 20971520 | tf_op jit(solution)/shard_map/dot_general | solution.py:165
  421.1 20.3 %fusion.70 = (bf16[2048]{0:T(1024)(128)(2,1)S(1)}, bf16[1024,2048]{1,0:T(8,128)(2,1)}) fusion(f32[1024,2048]{1,0:T(8,128)} %fusion.74, f32[2048]{0:T(1024)S(1)} %copy-done.32, bf16[1024,2048]{1,0:T(8,128)(2,1)} %all-gather.17.cloned.1.call-done, bf16[2048,2048]{1,0:T(8,128)(2,1)} %all-gather.15.cloned.1.call-done), kind=kOutput, calls=%fused_computation.138 | convolution fusion | flops 8636069888 | bytes 25178112 | tf_op jit(solution)/shard_map/dot_general | solution.py:73
  442.2 10.9 %convert_bitcast_fusion = bf16[3,2048,512]{1,2,0:T(8,128)(2,1)} fusion(bf16[3,1024,512]{1,2,0:T(8,128)(2,1)S(1)} %bitcast.179, bf16[1024,2048]{1,0:T(8,128)(2,1)} %all-gather.7.cloned.1.call-done), kind=kOutput, calls=%fused_computation.66 | convolution fusion | flops 6445596672 | bytes 13631488 | tf_op jit(solution)/shard_map/td,cte->cde/dot_general | solution.py:232
  453.2 12.6 %fusion.75 = f32[1024,2048]{1,0:T(8,128)S(1)} fusion(bf16[1024,2048]{1,0:T(8,128)(2,1)} %get-tuple-element.355, bf16[2048,2048]{1,0:T(8,128)(2,1)} %all-gather.13.cloned.1.call-done), kind=kOutput, calls=%fused_computation.141 | convolution fusion | flops 8589934592 | bytes 20971520 | tf_op jit(solution)/shard_map/dot_general | solution.py:73
  465.8 11.2 %fusion.44 = bf16[1024,2048]{1,0:T(8,128)(2,1)} fusion(f32[1024,2048]{1,0:T(8,128)S(1)} %fusion.75, bf16[3,1024,512]{1,2,0:T(8,128)(2,1)S(1)} %bitcast.180, bf16[3,2048,512]{1,2,0:T(8,128)(2,1)} %all-gather.9.cloned.1.call-done), kind=kOutput, calls=%fused_computation.60 | convolution fusion | flops 6446645248 | bytes 22020096 | tf_op jit(solution)/shard_map/cte,cde->td/dot_general | solution.py:234
  477.1 15.8 %fusion.69 = f32[1024,2048]{1,0:T(8,128)S(1)} fusion(bf16[2048,2048]{1,0:T(8,128)(2,1)} %all-gather.15.cloned.1.call-done, f32[1024,2048]{1,0:T(8,128)} %fusion.74, f32[2048]{0:T(1024)S(1)} %copy-done.32), kind=kOutput, calls=%fused_computation.137 | convolution fusion | flops 8610906112 | bytes 25174016 | tf_op jit(solution)/shard_map/dot_general | solution.py:170
  493.0 4.4 add_convert_fusion
  497.4 14.3 %convolution_convert_fusion.1 = bf16[2048,2048]{1,0:T(8,128)(2,1)} fusion(bf16[1024,2048]{1,0:T(8,128)(2,1)} %all-gather.7.cloned.1.call-done, bf16[1024,2048]{1,0:T(8,128)(2,1)} %get-tuple-element.355), kind=kOutput, calls=%fused_computation.64 | convolution fusion | flops 8594128896 | bytes 16777216 | tf_op jit(solution)/shard_map/dot_general | solution.py:67
  511.8 16.3 %convolution_convert_fusion = bf16[2048,2048]{1,0:T(8,128)(2,1)} fusion(bf16[1024,2048]{1,0:T(8,128)(2,1)} %all-gather.17.cloned.1.call-done, f32[1024,2048]{1,0:T(8,128)} %fusion.74, f32[2048]{0:T(1024)S(1)} %copy-done.32), kind=kOutput, calls=%fused_computation.63 | convolution fusion | flops 8615100416 | bytes 20979712 | tf_op jit(solution)/shard_map/dot_general | solution.py:67
  530.0 12.3 %all-reduce.6 = bf16[3,8,64]{2,1,0:T(8,128)(2,1)S(1)} all-reduce(bf16[3,8,64]{2,1,0:T(8,128)(2,1)S(1)} %copy-done.25), channel_id=8, replica_groups=mesh['dp'=8,'branch'=4] {'dp'}, use_global_device_ids=true, to_apply=%region_23.24.clone | all-reduce | flops 1536 | bytes 6144
  548.7 75.5 %reduce-scatter.13.cloned.1.call-done = bf16[256,2048]{1,0:T(8,128)(2,1)} async-done(((bf16[1024,2048]{1,0:T(8,128)(2,1)}), bf16[256,2048]{1,0:T(8,128)(2,1)}) %reduce-scatter.13.cloned.1.call-update) | async-done | bytes 1048592 | tf_op jit(solution)/shard_map/reduce_scatter | solution.py:257
  626.4 46.3 %all-reduce.7 = (f32[2048]{0:T(1024)S(1)}, f32[2048]{0:T(1024)S(1)}, f32[2048]{0:T(1024)S(1)}) all-reduce(f32[2048]{0:T(1024)S(1)} %get-tuple-element.302, f32[2048]{0:T(1024)S(1)} %get-tuple-element.305, f32[2048]{0:T(1024)S(1)} %copy-done.22), channel_id=4, replica_groups=mesh['dp'=8,'branch'=4] {'dp','branch'}, use_global_device_ids=true, to_apply=%region_16.17.clone | all-reduce | flops 6144 | bytes 49152
  674.5 30.3 %reduce-scatter.11.cloned.1.call-done = bf16[256,2048]{1,0:T(8,128)(2,1)} async-done(((bf16[1024,2048]{1,0:T(8,128)(2,1)}), bf16[256,2048]{1,0:T(8,128)(2,1)}) %reduce-scatter.11.cloned.1.call-update) | async-done | bytes 1048592 | tf_op jit(solution)/shard_map/reduce_scatter | solution.py:171
  704.8 4.0 fusion.63
  708.8 71.5 %reduce-scatter.19.cloned.1.call-done = bf16[256,2048]{1,0:T(8,128)(2,1)} async-done(((bf16[2048,2048]{1,0:T(8,128)(2,1)}), bf16[256,2048]{1,0:T(8,128)(2,1)}) %reduce-scatter.19.cloned.1.call-update) | async-done | bytes 1048592 | tf_op jit(solution)/shard_map/reduce_scatter | solution.py:247
  783.1 72.0 %reduce-scatter.21.cloned.1.call-done = bf16[2048,256]{1,0:T(8,128)(2,1)} async-done(((bf16[2048,2048]{1,0:T(8,128)(2,1)}), bf16[2048,256]{1,0:T(8,128)(2,1)}) %reduce-scatter.21.cloned.1.call-update) | async-done | bytes 1048592 | tf_op jit(solution)/shard_map/reduce_scatter | solution.py:253
  (213 shorter events, 55.2 us)
Async XLA Ops:
  7.2 6.5 copy-start.36
  7.2 6.5 copy-start.37
  7.2 6.5 copy-start.38
  7.2 48.8 %copy-start.5 = (bf16[256,2048]{1,0:T(8,128)(2,1)S(1)}, bf16[256,2048]{1,0:T(8,128)(2,1)}, u32[]{:S(2)}) copy-start(bf16[256,2048]{1,0:T(8,128)(2,1)} %param.17) | copy-start | bytes 3145732
  7.2 79.6 %all-gather.11.cloned.1.call-start = ((), (), s32[]{:S(2)}) async-start(), calls=%async_computation.9 | async-start | bytes 2359296 | tf_op jit(solution)/shard_map/all_gather | solution.py:125
  9.1 114.8 %all-gather.17.cloned.1.call-start = ((), (), s32[]{:S(2)}) async-start(), calls=%async_computation.13 | async-start | bytes 5242880 | tf_op jit(solution)/shard_map/all_gather | solution.py:177
  13.6 191.8 %all-gather.7.cloned.1.call-start = ((), (), s32[]{:S(2)}) async-start(), calls=%async_computation.7 | async-start | bytes 5242880 | tf_op jit(solution)/shard_map/all_gather | solution.py:120
  56.0 5.6 copy-start.8
  58.9 193.9 %all-gather.9.cloned.1.call-start = ((), (), s32[]{:S(2)}) async-start(), calls=%async_computation.8 | async-start | bytes 7077888 | tf_op jit(solution)/shard_map/all_gather | solution.py:123
  61.6 4.1 copy-start.14
  61.6 4.2 copy-start.28
  61.6 16.0 %copy-start.31 = (f32[16,16]{1,0:T(8,128)S(1)}, f32[16,16]{1,0:T(8,128)}, u32[]{:S(2)}) copy-start(f32[16,16]{1,0:T(8,128)} %param.28) | copy-start | bytes 3076
  61.6 344.8 %all-gather.13.cloned.1.call-start = ((), (), s32[]{:S(2)}) async-start(), calls=%async_computation.10 | async-start | bytes 9437184 | tf_op jit(solution)/shard_map/all_gather | solution.py:128
  62.8 358.3 %all-gather.15.cloned.1.call-start = ((), (), s32[]{:S(2)}) async-start(), calls=%async_computation.11 | async-start | bytes 9437184 | tf_op jit(solution)/shard_map/all_gather | solution.py:130
  65.6 477.4 %reduce-scatter.17.cloned.1.call-start = ((), (), s32[]{:S(2)}) async-start(), calls=%async_computation.16 | async-start | bytes 2359296 | tf_op jit(solution)/shard_map/reduce_scatter | solution.py:244
  86.8 178.1 %copy-start.15 = (f32[1024,16]{0,1:T(8,128)}, f32[1024,16]{0,1:T(8,128)S(1)}, u32[]{:S(2)}) copy-start(f32[1024,16]{0,1:T(8,128)S(1)} %get-tuple-element.384) | copy-start | bytes 196612
  86.8 178.1 %copy-start.17 = (f32[1024,16]{0,1:T(8,128)}, f32[1024,16]{0,1:T(8,128)S(1)}, u32[]{:S(2)}) copy-start(f32[1024,16]{0,1:T(8,128)S(1)} %get-tuple-element.385) | copy-start | bytes 196612
  300.1 3.8 copy-start.19
  326.8 7.2 copy-start.1
  334.0 10.0 %copy-start = (f32[8,512,1024]{2,1,0:T(8,128)S(1)}, f32[8,512,1024]{2,1,0:T(8,128)}, u32[]{:S(2)}) copy-start(f32[8,512,1024]{2,1,0:T(8,128)} %get-tuple-element.530) | copy-start | bytes 50331652 | tf_op jit(solution)/shard_map/while
  334.0 10.3 %copy-start.4 = (bf16[2,8,512,64]{2,3,1,0:T(8,128)(2,1)S(1)}, bf16[2,8,512,64]{2,3,1,0:T(8,128)(2,1)}, u32[]{:S(2)}) copy-start(bf16[2,8,512,64]{2,3,1,0:T(8,128)(2,1)} %get-tuple-element.600) | copy-start | bytes 3145732 | tf_op jit(solution)/shard_map/while
  339.5 7.7 copy-start.2
  348.5 3.8 copy-start.19
  373.7 7.3 copy-start.1
  381.0 9.1 %copy-start = (f32[8,512,1024]{2,1,0:T(8,128)S(1)}, f32[8,512,1024]{2,1,0:T(8,128)}, u32[]{:S(2)}) copy-start(f32[8,512,1024]{2,1,0:T(8,128)} %get-tuple-element.530) | copy-start | bytes 50331652 | tf_op jit(solution)/shard_map/while
  381.0 9.3 %copy-start.4 = (bf16[2,8,512,64]{2,3,1,0:T(8,128)(2,1)S(1)}, bf16[2,8,512,64]{2,3,1,0:T(8,128)(2,1)}, u32[]{:S(2)}) copy-start(bf16[2,8,512,64]{2,3,1,0:T(8,128)(2,1)} %get-tuple-element.600) | copy-start | bytes 3145732 | tf_op jit(solution)/shard_map/while
  386.5 8.3 copy-start.2
  395.2 2.2 copy-start.3
  395.2 2.5 copy-start.11
  397.2 1.9 copy-start.16
  397.4 2.6 copy-start.34
  403.7 141.0 %reduce-scatter.23.cloned.1.call-start = ((), (), s32[]{:S(2)}) async-start(), calls=%async_computation.19 | async-start | bytes 36864
  406.4 14.7 %copy-start.32 = (f32[2048]{0:T(1024)S(1)}, f32[2048]{0:T(1024)}, u32[]{:S(2)}) copy-start(f32[2048]{0:T(1024)} %bitcast_convert_fusion) | copy-start | bytes 24580
  442.2 103.9 %reduce-scatter.15.cloned.1.call-start = ((), (), s32[]{:S(2)}) async-start(), calls=%async_computation.15 | async-start | bytes 7077888 | tf_op jit(solution)/shard_map/reduce_scatter | solution.py:238
  453.2 171.0 %reduce-scatter.13.cloned.1.call-start = ((), (), s32[]{:S(2)}) async-start(), calls=%async_computation.14 | async-start | bytes 5242880 | tf_op jit(solution)/shard_map/reduce_scatter | solution.py:257
  477.0 15.9 %copy-start.13 = (bf16[64,8,2,512]{3,1,2,0:T(8,128)(2,1)S(1)}, bf16[64,8,2,512]{3,1,2,0:T(8,128)(2,1)}, u32[]{:S(2)}) copy-start(bf16[64,8,2,512]{3,1,2,0:T(8,128)(2,1)} %copy-done.12) | copy-start | bytes 3145732
  477.1 15.9 %copy-start.35 = (bf16[512,2048]{1,0:T(8,128)(2,1)S(1)}, bf16[512,2048]{1,0:T(8,128)(2,1)}, u32[]{:S(2)}) copy-start(bf16[512,2048]{1,0:T(8,128)(2,1)} %all-gather.11.cloned.1.call-done) | copy-start | bytes 6291460
  477.1 227.7 %reduce-scatter.11.cloned.1.call-start = ((), (), s32[]{:S(2)}) async-start(), calls=%async_computation.12 | async-start | bytes 5242880 | tf_op jit(solution)/shard_map/reduce_scatter | solution.py:171
  497.4 282.9 %reduce-scatter.19.cloned.1.call-start = ((), (), s32[]{:S(2)}) async-start(), calls=%async_computation.17 | async-start | bytes 9437184 | tf_op jit(solution)/shard_map/reduce_scatter | solution.py:247
  511.7 343.4 %reduce-scatter.21.cloned.1.call-start = ((), (), s32[]{:S(2)}) async-start(), calls=%async_computation.18 | async-start | bytes 9437184 | tf_op jit(solution)/shard_map/reduce_scatter | solution.py:253
  528.1 1.9 copy-start.25
  528.1 96.1 %copy-start.6 = (bf16[256,2048]{1,0:T(8,128)(2,1)S(1)}, bf16[256,2048]{1,0:T(8,128)(2,1)}, u32[]{:S(2)}) copy-start(bf16[256,2048]{1,0:T(8,128)(2,1)} %param.17) | copy-start | bytes 3145732
  528.1 96.1 %copy-start.21 = (f32[2048]{0:T(1024)S(1)}, f32[2048]{0:T(1024)}, u32[]{:S(2)}) copy-start(f32[2048]{0:T(1024)} %copy-done.20) | copy-start | bytes 24580
  528.1 96.1 %copy-start.24 = (f32[256]{0:T(256)S(1)}, f32[256]{0:T(256)}, u32[]{:S(2)}) copy-start(f32[256]{0:T(256)} %copy-done.23) | copy-start | bytes 3076
  528.1 96.0 %copy-start.27 = (f32[256]{0:T(256)S(1)}, f32[256]{0:T(256)}, u32[]{:S(2)}) copy-start(f32[256]{0:T(256)} %copy-done.26) | copy-start | bytes 3076
  528.1 98.3 %copy-start.22 = (f32[2048]{0:T(1024)S(1)}, f32[2048]{0:T(1024)}, u32[]{:S(2)}) copy-start(f32[2048]{0:T(1024)} %get-tuple-element.358) | copy-start | bytes 24580
  528.1 176.7 %copy-start.7 = (bf16[256,2048]{1,0:T(8,128)(2,1)S(1)}, bf16[256,2048]{1,0:T(8,128)(2,1)}, u32[]{:S(2)}) copy-start(bf16[256,2048]{1,0:T(8,128)(2,1)} %param.20) | copy-start | bytes 3145732
  528.1 176.7 %copy-start.30 = (f32[256]{0:T(256)S(1)}, f32[256]{0:T(256)}, u32[]{:S(2)}) copy-start(f32[256]{0:T(256)} %copy-done.29) | copy-start | bytes 3076
  (10 other events, 9.1 us)
Sparse Core Ops, SparseCore 0:
  10.5 30.8 all-gather.10
  43.6 80.3 all-gather.16
  126.1 79.2 all-gather.6
  207.2 45.5 all-gather.8
  255.1 54.4 all-gather.12
  311.3 55.9 all-gather.14
  403.9 40.4 reduce-scatter.16
  448.2 30.7 reduce-scatter.22
  482.4 62.6 reduce-scatter.14
  547.3 76.7 reduce-scatter.12
  626.4 78.3 reduce-scatter.10
  708.5 71.7 reduce-scatter.18
  783.8 71.2 reduce-scatter.20
where the time goes:
time: 872 us; the launch traced here: 865 us
  waiting for transfers between devices  408 us (47%)
  matrix products  223 us (26%)
  blocking collectives  119 us (14%)
  other arithmetic  66.1 us (8%)
  local copies, waits for them, and re-layouts  32.2 us (4%)
  between operations  15.7 us (2%)
    unnamed x3, blocking collectives  100 us
    reduce_scatter x1, waiting for transfers between devices, local(): lax.psum_scatter(normed_grad.astype(jnp.bfloat16), 'branch', scatter_dime...  75.5 us
    all_gather x1, waiting for transfers between devices, local(): gathered = lax.all_gather(normed_input, 'branch', axis=0, tiled=True)  73.5 us
    reduce_scatter x1, waiting for transfers between devices, local(): lax.psum_scatter(down_grad.astype(jnp.bfloat16), 'dp', scatter_dimension=...  72 us
    reduce_scatter x1, waiting for transfers between devices, local(): lax.psum_scatter(up_grad.astype(jnp.bfloat16), 'dp', scatter_dimension=0,...  71.5 us
    all_gather x1, waiting for transfers between devices, local(): lax.all_gather(w_qkv.astype(jnp.bfloat16), 'dp', axis=1, tiled=True)  47.4 us
    dot_general x3, matrix products, contract_cols(): lax.dot_general(left, right, (((1,), (1,)), ((), ())), preferred_element_...  38.1 us
    all_gather x1, waiting for transfers between devices, local(): cot_all = lax.all_gather(masked_cot, 'branch', axis=0, tiled=True)  37.1 us
  transfers between devices with their start and end apart: 13, of which 7 were waited for; matrix products, arithmetic and copies ran while one was open for 35% of the time, Pallas kernels for 0%

commit v1 on v0

v1 whole, which is shorter than its diff:
```python
import functools
import math

import jax
import jax.numpy as jnp
from jax import lax
from jax.experimental import pallas as pl
from jax.experimental.pallas import tpu as pltpu
from jax.sharding import PartitionSpec as P

HEAD_DIM = 64
ROT = 32
NORM_EPS = 1e-05
NEGATIVE = -1e30
BF = jnp.bfloat16
F32 = jnp.float32
MESH = pl.DeviceIdType.MESH
VMEM_LIMIT = 60 * 2**20
GATHER_VMEM = 32 * 2**20


def ring_place(group):
    row = group // 2
    return 2 * row + (group + row) % 2


def ring_group(place):
    row = place // 2
    return 2 * row + (place + row) % 2


def chunk_rows(group, half, rows):
    return pl.ds(pl.multiple_of((2 * group + half) * rows, rows), rows)


class Links:
    def __init__(self, dp_size, branch_size):
        self.groups = dp_size // 2
        self.branches = branch_size
        dp = lax.axis_index("dp")
        self.core = dp % 2
        self.other = 1 - self.core
        self.group = dp // 2
        self.place = ring_place(self.group)
        self.branch = lax.axis_index("branch")
        self.sibling = {"dp": 2 * self.group + self.other}
        right = ring_group((self.place + 1) % self.groups)
        left = ring_group((self.place + self.groups - 1) % self.groups)
        self.ring = ({"dp": 2 * right + self.core}, {"dp": 2 * left + self.core})
        self.has_up = self.branch < self.branches - 1
        self.has_down = self.branch > 0
        self.peers = [{"branch": (self.branch + k) % branch_size} for k in range(1, branch_size)]
        self.up = {"branch": self.branch + 1}
        self.down = {"branch": self.branch - 1}

    def meet(self):
        barrier = pltpu.get_barrier_semaphore()

        def greet(device):
            pl.semaphore_signal(barrier, 1, device_id=device, device_id_type=MESH)

        greet(self.sibling)
        greet(self.ring[0])
        greet(self.ring[1])
        for device in self.peers:
            greet(device)
        pl.semaphore_wait(barrier, 3 + len(self.peers))


def remote(src, dst, send, recv, device):
    return pltpu.make_async_remote_copy(
        src_ref=src, dst_ref=dst, send_sem=send, recv_sem=recv, device_id=device, device_id_type=MESH
    )


def gather_kernel(dp_size, branch_size, n_w, *refs):
    rows_refs = refs[:2]
    w_refs = refs[2 : 2 + n_w]
    full_refs = refs[2 + n_w : 4 + n_w]
    wf_refs = refs[4 + n_w : 4 + 2 * n_w]
    small_out = refs[4 + 2 * n_w]
    (z_send, z_recv, s_send, s_recv, l_sem, w_send, w_recv, ws_send, ws_recv, wl_sem, p_send, p_recv, p_local) = refs[
        5 + 2 * n_w :
    ]
    at = Links(dp_size, branch_size)
    at.meet()
    rows = rows_refs[0].shape[0]
    waits = []

    def piece(block, branch):
        start = (block * branch_size + branch) * rows
        return pl.ds(pl.multiple_of(start, rows), rows)

    for a in range(2):
        mine = piece(at.core, at.branch)
        for cond, way, device in ((at.has_up, 0, at.up), (at.has_down, 1, at.down)):
            copy = remote(
                rows_refs[a], full_refs[a].at[mine], z_send.at[a, way, 0], z_recv.at[a, at.branch], device
            )
            if a == 0:
                pl.when(cond)(copy.start)
            waits.append((cond, copy.wait_send))
        copy = remote(
            rows_refs[a], full_refs[a].at[mine], s_send.at[a, at.branch], s_recv.at[a, at.branch], at.sibling
        )
        copy.start()
        waits.append((None, copy.wait_send))
        own = pltpu.make_async_copy(rows_refs[a], full_refs[a].at[mine], l_sem.at[a])
        own.start()
        waits.append((None, own.wait))
    for w in range(n_w):
        here = chunk_rows(at.group, at.core, w_refs[w].shape[1])
        copy = remote(
            w_refs[w].at[at.other], wf_refs[w].at[here], ws_send.at[w], ws_recv.at[w], at.sibling
        )
        copy.start()
        waits.append((None, copy.wait_send))
        own = pltpu.make_async_copy(w_refs[w].at[at.core], wf_refs[w].at[here], wl_sem.at[w])
        own.start()

    def ring_copy(w, half, step):
        shift = step if half == 0 else -step
        source = ring_group((at.place - shift + at.groups) % at.groups)
        part = wf_refs[w].at[chunk_rows(source, half, w_refs[w].shape[1])]
        return remote(part, part, w_send.at[w, half, step], w_recv.at[w, half, step], at.ring[half])

    def ring_step(w, step):
        if step == 0:
            here = wf_refs[w].at[chunk_rows(at.group, at.core, w_refs[w].shape[1])]
            pltpu.make_async_copy(w_refs[w].at[at.core], here, wl_sem.at[w]).wait()
            there = wf_refs[w].at[chunk_rows(at.group, at.other, w_refs[w].shape[1])]
            remote(there, there, ws_send.at[w], ws_recv.at[w], at.sibling).wait_recv()
        for half in range(2):
            if step > 0:
                shift = step if half == 0 else -step
                source = ring_group((at.place - shift + at.groups) % at.groups)
                part = wf_refs[w].at[chunk_rows(source, half, w_refs[w].shape[1])]
                remote(
                    part, part, w_send.at[w, half, step - 1], w_recv.at[w, half, step - 1], at.ring[half]
                ).wait_recv()
            if step < at.groups - 1:
                copy = ring_copy(w, half, step)
                copy.start()
                waits.append((None, copy.wait_send))

    def line_step(a, step):
        for way in range(2):
            source = at.branch - step if way == 0 else at.branch + step
            inside = source >= 0 if way == 0 else source < branch_size
            part = full_refs[a].at[piece(at.core, jnp.clip(source, 0, branch_size - 1))]
            onward = at.branch < branch_size - 1 if way == 0 else at.branch > 0
            device = at.up if way == 0 else at.down
            source = jnp.clip(source, 0, branch_size - 1)
            arrived = remote(part, part, z_send.at[a, way, 0], z_recv.at[a, source], device)
            forward = remote(part, part, z_send.at[a, way, step], z_recv.at[a, source], device)
            across = remote(part, part, s_send.at[a, source], s_recv.at[a, source], at.sibling)

            @pl.when(inside)
            def _():
                arrived.wait_recv()
                pl.when(onward)(forward.start)
                across.start()

            def both(inside=inside, onward=onward, forward=forward, across=across):
                @pl.when(inside)
                def _():
                    pl.when(onward)(forward.wait_send)
                    across.wait_send()

            waits.append((None, both))

    def begin_second():
        mine = piece(at.core, at.branch)
        for cond, way, device in ((at.has_up, 0, at.up), (at.has_down, 1, at.down)):
            copy = remote(
                rows_refs[1], full_refs[1].at[mine], z_send.at[1, way, 0], z_recv.at[1, at.branch], device
            )
            pl.when(cond)(copy.start)

    for w in range(n_w):
        ring_step(w, 0)
    line_steps = [(0, s) for s in range(1, branch_size)] + [(1, s) for s in range(1, branch_size)]
    ring_steps = [(w, s) for s in range(1, at.groups) for w in range(n_w)]
    events = [((i + 1.0) / len(line_steps) * 137.0, 0, e) for i, e in enumerate(line_steps)]
    events += [((i + 1.0) / len(ring_steps) * 103.0, 1, e) for i, e in enumerate(ring_steps)]
    for _, kind, event in sorted(events):
        if kind == 0:
            line_step(*event)
            if event == (0, branch_size - 2 if branch_size > 2 else 1):
                begin_second()
        else:
            ring_step(*event)
    params = wf_refs[n_w - 1]
    own = pltpu.make_async_copy(params, small_out.at[at.branch], p_local)
    own.start()
    waits.append((None, own.wait))
    for k in range(1, branch_size):
        copy = remote(params, small_out.at[at.branch], p_send.at[k], p_recv.at[k], at.peers[k - 1])
        copy.start()
        waits.append((None, copy.wait_send))
    for k in range(1, branch_size):
        slot = small_out.at[(at.branch - k + branch_size) % branch_size]
        remote(slot, slot, p_send.at[k], p_recv.at[k], at.peers[k - 1]).wait_recv()
    for a in range(2):
        for branch in range(branch_size):
            part = full_refs[a].at[piece(at.other, branch)]
            remote(part, part, s_send.at[a, branch], s_recv.at[a, branch], at.sibling).wait_recv()
    for cond, wait in waits:
        if cond is None:
            wait()
        else:
            pl.when(cond)(wait)


def gather_all(dp_size, branch_size, arrays, weights):
    rows, width = arrays[0].shape
    n_w = len(weights)
    groups = dp_size // 2
    out_shape = [jax.ShapeDtypeStruct((2 * branch_size * rows, width), BF)] * 2
    out_shape += [jax.ShapeDtypeStruct((dp_size * w.shape[1], w.shape[2]), BF) for w in weights]
    out_shape += [jax.ShapeDtypeStruct((branch_size, dp_size * weights[-1].shape[1], weights[-1].shape[2]), BF)]
    dma = pltpu.SemaphoreType.DMA
    return pl.pallas_call(
        functools.partial(gather_kernel, dp_size, branch_size, n_w),
        out_shape=out_shape,
        in_specs=[pl.BlockSpec(memory_space=pl.ANY)] * (2 + n_w),
        out_specs=[pl.BlockSpec(memory_space=pl.ANY)] * (3 + n_w),
        scratch_shapes=[
            dma((2, 2, branch_size)),
            dma((2, branch_size)),
            dma((2, branch_size)),
            dma((2, branch_size)),
            dma((2,)),
            dma((n_w, 2, groups)),
            dma((n_w, 2, groups)),
            dma((n_w,)),
            dma((n_w,)),
            dma((n_w,)),
            dma((branch_size,)),
            dma((branch_size,)),
            dma,
        ],
        compiler_params=pltpu.CompilerParams(
            collective_id=0, has_side_effects=True, vmem_limit_bytes=GATHER_VMEM
        ),
        name="gather_all",
    )(*arrays, *weights)


def scatter_kernel(dp_size, branch_size, *refs):
    (h_ref, gm_ref, dqkv_ref, dz_ref, o_ref, u_ref, dh_ref, sums_ref) = refs[:8]
    g_refs = refs[8:12]
    tok_out, sum_out, sib_land = refs[12:15]
    slots = refs[15:19]
    firsts = refs[19:23]
    gots = refs[23:27]
    (own_buf, sib_buf, line_slot, w_send, w_recv, ws_send, ws_recv, z_send, z_recv, s_send, s_recv,
     l_sem, left_buf, x_sem, sum_slot, sum_first, sum_got, sum_peer, p_send, p_recv) = refs[27:]
    at = Links(dp_size, branch_size)
    at.meet()
    rows = own_buf.shape[0]
    toks = branch_size * rows
    w_rows = firsts[0].shape[1]
    block = left_buf.shape[3]
    lefts = (gm_ref, h_ref)
    rights = (u_ref, o_ref, dz_ref, dqkv_ref)
    last = at.groups - 1
    waits = []
    first_sent = {}

    sib_copy = remote(
        dh_ref.at[pl.ds(at.other * toks, toks)], sib_land, s_send, s_recv, at.sibling
    )
    sib_copy.start()

    def left_copy(a, half, step):
        shift = step + 1 if half == 0 else -step - 1
        dest = ring_group((at.place - shift + 2 * at.groups) % at.groups)
        start = (2 * dest + half) * w_rows if block == w_rows else dest * block
        start = pl.multiple_of(start, block)
        return pltpu.make_async_copy(lefts[a].at[:, pl.ds(start, block)], left_buf.at[a, half], x_sem.at[a, half])

    def ring_step(a, step):
        for half in range(2):
            left_copy(a, half, step).wait()
            for w in (2 * a, 2 * a + 1):
                total = lax.dot_general(
                    left_buf[a, half, :, pl.ds(half * (block - w_rows), w_rows)], rights[w][...], (((0,), (0,)), ((), ())), preferred_element_type=F32
                )
                if step > 0:
                    slot = slots[w].at[half, step - 1]
                    remote(
                        slot, slot, w_send.at[w, half, step - 1], w_recv.at[w, half, step - 1], at.ring[half]
                    ).wait_recv()
                    total = total + slot[...].astype(F32)
                if step < last:
                    out = firsts[w].at[half] if step == 0 else slots[w].at[half, step - 1]
                    out[...] = total.astype(BF)
                    copy = remote(
                        out, slots[w].at[half, step], w_send.at[w, half, step], w_recv.at[w, half, step], at.ring[half]
                    )
                    copy.start()
                    if step == 0:
                        first_sent[w, half] = copy
                    else:
                        waits.append(copy.wait_send)
                else:
                    out = firsts[w].at[half]
                    first_sent[w, half].wait_send()
                    copy = remote(out, gots[w], ws_send.at[w], ws_recv.at[w], at.sibling)

                    @pl.when(at.core == half)
                    def _():
                        g_refs[w][half] = total

                    @pl.when(at.core != half)
                    def _():
                        out[...] = total.astype(BF)
                        copy.start()

                    waits.append(lambda copy=copy, half=half: pl.when(at.core != half)(copy.wait_send))

            if step < last:
                left_copy(a, half, step + 1).start()

    n_w = 4

    def sum_step(step):
        for half in range(2):
            shift = step + 1 if half == 0 else -step - 1
            dest = ring_group((at.place - shift + 2 * at.groups) % at.groups)
            total = sums_ref[chunk_rows(dest, half, 8)]
            if step > 0:
                slot = sum_slot.at[half, step - 1]
                remote(
                    slot, slot, w_send.at[n_w, half, step - 1], w_recv.at[n_w, half, step - 1], at.ring[half]
                ).wait_recv()
                total = total + slot[...]
            out = sum_first.at[step, half]
            out[...] = total
            if step < last:
                copy = remote(
                    out, sum_slot.at[half, step], w_send.at[n_w, half, step], w_recv.at[n_w, half, step], at.ring[half]
                )
                copy.start()
                waits.append(copy.wait_send)
        if step == last:
            copy = remote(
                sum_first.at[last, at.other], sum_got, ws_send.at[n_w], ws_recv.at[n_w], at.sibling
            )
            copy.start()
            copy.wait()
            mine = sum_peer.at[0]
            mine[...] = sum_first[last, at.core] + sum_got[...]
            sum_out[at.core] = sum_first[last, at.core]
            sum_out[at.other] = sum_got[...]
            for k in range(1, branch_size):
                copy = remote(mine, sum_peer.at[k], p_send.at[k], p_recv.at[k], at.peers[k - 1])
                copy.start()
                waits.append(copy.wait_send)

    def sum_end():
        total = sum_peer[0]
        for k in range(1, branch_size):
            remote(sum_peer.at[0], sum_peer.at[k], p_send.at[k], p_recv.at[k], at.peers[k - 1]).wait_recv()
            total = total + sum_peer[k]
        sum_out[2] = total

    def load_own(k, d):
        own = pltpu.make_async_copy(dh_ref.at[pl.ds(at.core * toks + d * rows, rows)], own_buf, l_sem.at[0])
        sib = pltpu.make_async_copy(sib_land.at[pl.ds(d * rows, rows)], sib_buf, l_sem.at[1])
        own.start()
        sib.start()
        own.wait()
        sib.wait()

    def line_step(k):
        for way in range(2):
            d = branch_size - 1 - k if way == 0 else k
            going = at.branch < d if way == 0 else at.branch > d
            more = at.branch > 0 if way == 0 else at.branch < branch_size - 1
            device = at.up if way == 0 else at.down
            slot = line_slot.at[way, d - 1 + way]
            sent = remote(slot, slot, z_send.at[way, d], z_recv.at[way, d], device)

            @pl.when(going)
            def _():
                load_own(k, d)
                total = own_buf[...].astype(F32) + sib_buf[...].astype(F32)

                @pl.when(more)
                def _():
                    sent.wait_recv()
                    slot[...] = (total + slot[...].astype(F32)).astype(BF)

                @pl.when(jnp.logical_not(more))
                def _():
                    slot[...] = total.astype(BF)

                sent.start()

            waits.append(lambda going=going, sent=sent: pl.when(going)(sent.wait_send))

    def line_end():
        d = at.branch
        load_own(0, d)
        tok_out[...] = own_buf[...].astype(F32) + sib_buf[...].astype(F32)
        for way in range(2):
            more = at.branch > 0 if way == 0 else at.branch < branch_size - 1
            slot = line_slot.at[way, d - 1 + way]
            device = at.up if way == 0 else at.down

            @pl.when(more)
            def _():
                remote(slot, slot, z_send.at[way, d], z_recv.at[way, d], device).wait_recv()
                tok_out[...] += slot[...].astype(F32)

    for a in range(2):
        for half in range(2):
            left_copy(a, half, 0).start()
    sum_step(0)
    ring_step(0, 0)
    sib_copy.wait_recv()
    line_step(0)
    ring_step(1, 0)
    for k in range(1, branch_size - 1):
        line_step(k)
    events = []
    for s in range(1, at.groups):
        for a in range(2):
            ring_step(a, s)
        sum_step(s)
        if s == 2:
            line_end()
    if at.groups < 3:
        line_end()
    for w in range(n_w):
        remote(firsts[w].at[0], gots[w], ws_send.at[w], ws_recv.at[w], at.sibling).wait_recv()
        g_refs[w][at.other] = gots[w][...].astype(F32)
    sum_end()
    sib_copy.wait_send()
    for wait in waits:
        wait()


def scatter_all(dp_size, branch_size, h, gm, dqkv, dz, o, u, dh, sums):
    widths = [u.shape[1], o.shape[1], dz.shape[1], dqkv.shape[1]]
    width = h.shape[1]
    w_rows = width // dp_size
    groups = dp_size // 2
    toks = h.shape[0] // 2
    rows = toks // branch_size
    n_w = 4
    dma = pltpu.SemaphoreType.DMA
    vm = pl.BlockSpec(memory_space=pltpu.VMEM)
    hb = pl.BlockSpec(memory_space=pl.ANY)
    out_shape = [jax.ShapeDtypeStruct((2, w_rows, n), F32) for n in widths]
    out_shape += [jax.ShapeDtypeStruct((rows, width), F32), jax.ShapeDtypeStruct((3, 8, 128), F32)]
    out_shape += [jax.ShapeDtypeStruct((toks, width), BF)]
    out = pl.pallas_call(
        functools.partial(scatter_kernel, dp_size, branch_size),
        out_shape=out_shape,
        in_specs=[hb] * 2 + [vm] * 4 + [hb, vm],
        out_specs=[vm] * 6 + [hb],
        scratch_shapes=[pltpu.VMEM((2, groups - 1, w_rows, n), BF) for n in widths]
        + [pltpu.VMEM((2, w_rows, n), BF) for n in widths]
        + [pltpu.VMEM((w_rows, n), BF) for n in widths]
        + [
            pltpu.VMEM((rows, width), BF),
            pltpu.VMEM((rows, width), BF),
            pltpu.VMEM((2, branch_size - 1, rows, width), BF),
            dma((n_w + 1, 2, groups)),
            dma((n_w + 1, 2, groups)),
            dma((n_w + 1,)),
            dma((n_w + 1,)),
            dma((2, branch_size)),
            dma((2, branch_size)),
            dma(()),
            dma(()),
            dma((2,)),
            pltpu.VMEM((2, 2, 2 * toks, w_rows if w_rows % 128 == 0 else 2 * w_rows), BF),
            dma((2, 2)),
            pltpu.VMEM((2, groups - 1, 8, 128), F32),
            pltpu.VMEM((groups, 2, 8, 128), F32),
            pltpu.VMEM((8, 128), F32),
            pltpu.VMEM((branch_size, 8, 128), F32),
            dma((branch_size,)),
            dma((branch_size,)),
        ],
        compiler_params=pltpu.CompilerParams(
            collective_id=1, has_side_effects=True, vmem_limit_bytes=VMEM_LIMIT
        ),
        name="scatter_all",
    )(h, gm, dqkv, dz, o, u, dh, sums)
    return out[:6]


def turn(values, tables, sign):
    fixed, from_low, from_high = tables
    half = ROT // 2
    return (
        values * fixed
        + sign * (pltpu.roll(values, half, 1) * from_low + pltpu.roll(values, 2 * HEAD_DIM - half, 1) * from_high)
    )


def score_tile(keys, queries, begins, first, q_tile):
    scores = lax.dot_general(keys, queries, (((1,), (1,)), ((), ())), preferred_element_type=F32)
    key_at = lax.broadcasted_iota(jnp.int32, scores.shape, 0)
    query_at = first + lax.broadcasted_iota(jnp.int32, scores.shape, 1)
    allowed = jnp.logical_and(key_at >= begins, key_at <= query_at)
    return jnp.where(allowed, scores, NEGATIVE)


def attend_kernel(q_tile, q_ref, k_ref, v_ref, begin_ref, table_ref, qr_ref, kr_ref, vr_ref, o_ref, lse_ref):
    tables = tuple(table_ref[0, i] for i in range(3))
    qr_ref[...] = (turn(q_ref[...], tables, 1.0) * (HEAD_DIM**-0.5)).astype(BF)
    kr_ref[...] = turn(k_ref[...], tables, 1.0).astype(BF)
    vr_ref[...] = v_ref[...].astype(BF)
    toks = q_ref.shape[0]
    for first in range(0, toks, q_tile):
        span = first + q_tile
        begins = begin_ref[0, 0:1, first:span]
        outs = []
        for head in range(2):
            lanes = slice(head * HEAD_DIM, (head + 1) * HEAD_DIM)
            scores = score_tile(kr_ref[:span, lanes], qr_ref[first:span, lanes], begins, first, q_tile)
            top = jnp.max(scores, axis=0, keepdims=True)
            weights = jnp.exp(scores - top)
            total = jnp.sum(weights, axis=0, keepdims=True)
            lse_ref[0, 0, head : head + 1, first:span] = top + jnp.log(total)
            mixed = lax.dot_general(
                vr_ref[:span, lanes], weights.astype(BF), (((0,), (0,)), ((), ())), preferred_element_type=F32
            )
            outs.append(mixed / total)
        o_ref[first:span, :] = jnp.concatenate(outs, axis=0).T.astype(BF)


def attend_back_kernel(
    q_tile, qr_ref, kr_ref, vr_ref, o_ref, do_ref, lse_ref, begin_ref, table_ref, dq_ref, dk_ref, dv_ref, k_acc, v_acc
):
    tables = tuple(table_ref[0, i] for i in range(3))
    toks = qr_ref.shape[0]
    k_acc[...] = jnp.zeros_like(k_acc)
    v_acc[...] = jnp.zeros_like(v_acc)
    for first in range(0, toks, q_tile):
        span = first + q_tile
        begins = begin_ref[0, 0:1, first:span]
        both = (do_ref[first:span, :].astype(F32) * o_ref[first:span, :].astype(F32)).T
        turned = []
        for head in range(2):
            lanes = slice(head * HEAD_DIM, (head + 1) * HEAD_DIM)
            delta = jnp.sum(both[lanes], axis=0, keepdims=True)
            queries = qr_ref[first:span, lanes]
            grads = do_ref[first:span, lanes]
            keys = kr_ref[:span, lanes]
            scores = score_tile(keys, queries, begins, first, q_tile)
            prob = jnp.exp(scores - lse_ref[0, 0, head : head + 1, first:span])
            v_acc[head, :span, :] += jnp.dot(prob.astype(BF), grads, preferred_element_type=F32)
            dprob = lax.dot_general(
                vr_ref[:span, lanes], grads, (((1,), (1,)), ((), ())), preferred_element_type=F32
            )
            ds = (prob * (dprob - delta)).astype(BF)
            k_acc[head, :span, :] += jnp.dot(ds, queries, preferred_element_type=F32)
            turned.append(
                lax.dot_general(keys, ds, (((0,), (0,)), ((), ())), preferred_element_type=F32)
            )
        dq = jnp.concatenate(turned, axis=0).T * (HEAD_DIM**-0.5)
        dq_ref[first:span, :] = turn(dq, tuple(t[first:span] for t in tables), -1.0).astype(BF)
    dk = jnp.concatenate([k_acc[0], k_acc[1]], axis=1)
    dk_ref[...] = turn(dk, tables, -1.0).astype(BF)
    dv_ref[...] = jnp.concatenate([v_acc[0], v_acc[1]], axis=1).astype(BF)


def attention_specs(toks, pairs):
    wide = 2 * HEAD_DIM

    def cols(shift):
        return pl.BlockSpec((toks, wide), lambda i, j: (i, j + shift * pairs))

    begin = pl.BlockSpec((1, 8, toks), lambda i, j: (i, 0, 0))
    table = pl.BlockSpec((1, 3, toks, wide), lambda i, j: (i, 0, 0, 0))
    lse = pl.BlockSpec((1, 1, 2, toks), lambda i, j: (i, j, 0, 0))
    return cols, begin, table, lse


def attend(project, begins, tables):
    blocks, _, toks = begins.shape
    pairs = project.shape[1] // (6 * HEAD_DIM)
    cols, begin, table, lse = attention_specs(toks, pairs)
    narrow = jax.ShapeDtypeStruct((blocks * toks, pairs * 2 * HEAD_DIM), BF)
    return pl.pallas_call(
        functools.partial(attend_kernel, min(256, toks)),
        grid=(blocks, pairs),
        in_specs=[cols(0), cols(1), cols(2), begin, table],
        out_specs=[cols(0)] * 4 + [lse],
        out_shape=[narrow] * 4 + [jax.ShapeDtypeStruct((blocks, pairs, 2, toks), F32)],
        compiler_params=pltpu.CompilerParams(vmem_limit_bytes=GATHER_VMEM),
        name="attend",
    )(project, project, project, begins, tables)


def attend_back(queries, keys, values, o, do, lse_rows, begins, tables):
    blocks, _, toks = begins.shape
    pairs = queries.shape[1] // (2 * HEAD_DIM)
    cols, begin, table, lse = attention_specs(toks, pairs)
    narrow = jax.ShapeDtypeStruct(queries.shape, BF)
    acc = pltpu.VMEM((2, toks, HEAD_DIM), F32)
    return pl.pallas_call(
        functools.partial(attend_back_kernel, min(256, toks)),
        grid=(blocks, pairs),
        in_specs=[cols(0)] * 5 + [lse, begin, table],
        out_specs=[cols(0)] * 3,
        out_shape=[narrow] * 3,
        scratch_shapes=[acc, acc],
        compiler_params=pltpu.CompilerParams(vmem_limit_bytes=GATHER_VMEM),
        name="attend_back",
    )(queries, keys, values, o, do, lse_rows, begins, tables)


def rotary_tables(doc_rows):
    row_count = doc_rows.shape[0]
    row_index = jnp.arange(row_count, dtype=jnp.int32)
    same = doc_rows[:, None] == doc_rows[None, :]
    begins = jnp.min(jnp.where(same, row_index[:, None], row_count), axis=0)
    places = (row_index - begins).astype(F32)
    half = ROT // 2
    frequency = 10000.0 ** (-2.0 * jnp.arange(half, dtype=F32) / ROT)
    angles = places[:, None] * frequency[None, :]
    cosine, sine = jnp.cos(angles), jnp.sin(angles)
    none = jnp.zeros((row_count, HEAD_DIM - ROT), F32)
    blank = jnp.zeros_like(sine)
    fixed = jnp.concatenate([cosine, cosine, none + 1.0], axis=1)
    from_low = jnp.concatenate([blank, sine, none], axis=1)
    from_high = jnp.concatenate([-sine, blank, none], axis=1)
    tables = jnp.stack([jnp.tile(t, (1, 2)) for t in (fixed, from_low, from_high)])
    return jnp.broadcast_to(begins[None], (8, row_count)), tables


def contract_cols(left, right):
    return lax.dot_general(left, right, (((1,), (1,)), ((), ())), preferred_element_type=F32)


def gelu_tanh(values):
    return jax.nn.gelu(values, approximate=True)


def local(
    dp_size, branch_size, tokens, doc_ids, real_rows, cotangent, norm_gain, norm_shift, out_bias,
    w_qkv, b_qkv, w_out, w_up, b_up, w_down,
):
    dp = lax.axis_index("dp")
    branch = lax.axis_index("branch")
    core = dp % 2
    my_rows, width = tokens.shape
    toks = doc_ids.shape[0]
    w_rows = w_qkv.shape[1]
    cols = w_qkv.shape[2] // 2
    hid = w_up.shape[1] // 2
    heads = cols // HEAD_DIM

    my_real = lax.dynamic_slice_in_dim(real_rows, branch * my_rows, my_rows).astype(F32)
    masked_cot = (cotangent.astype(F32) * my_real[:, None]).astype(BF)
    qkv_l = w_qkv.astype(BF).reshape(3, w_rows, 2, cols).transpose(2, 1, 0, 3).reshape(2, w_rows, 3 * cols)
    up_l = w_up.astype(BF).reshape(w_rows, 2, hid).transpose(1, 0, 2)
    out_l = w_out.astype(BF).T.reshape(w_rows, 2, cols).transpose(1, 0, 2)
    down_l = w_down.astype(BF).T.reshape(w_rows, 2, hid).transpose(1, 0, 2)

    small = jnp.concatenate([v.reshape(-1) for v in (norm_gain, norm_shift, out_bias, b_qkv, b_up)]).astype(BF)
    small = jnp.pad(small, (0, -small.size % 128))
    small = jnp.broadcast_to(small[None, None], (2, 16, small.size))

    tok_all, gm, wqkv, wup, wot, wdt, _, params = gather_all(
        dp_size, branch_size, (tokens, masked_cot), (qkv_l, up_l, out_l, down_l, small)
    )
    params = params.reshape(branch_size, dp_size, 16, -1)[:, :, 0].astype(F32)
    sizes = [norm_gain.size, norm_shift.size, out_bias.size, b_qkv.size, b_up.size]
    stops = [sum(sizes[: i + 1]) for i in range(5)]
    gain, shift, bias_full = (
        params[:, :, stops[i] - sizes[i] : stops[i]].transpose(1, 0, 2).reshape(width) for i in range(3)
    )
    mine = lax.dynamic_index_in_dim(params, branch, 0, keepdims=False)
    qkv_b = mine[:, stops[2] : stops[3]].reshape((dp_size,) + b_qkv.shape).transpose(1, 2, 0, 3)
    qkv_b = qkv_b.reshape(3, 2, cols)
    qkv_b = lax.dynamic_index_in_dim(qkv_b, core, 1, keepdims=False).reshape(3 * cols)
    up_b = mine[:, stops[3] : stops[4]].reshape((dp_size,) + b_up.shape).transpose(1, 0, 2).reshape(2, hid)
    up_b = lax.dynamic_index_in_dim(up_b, core, 0, keepdims=False)
    swap = [(i, i + 1 - 2 * (i % 2)) for i in range(dp_size)]
    other_ids = lax.ppermute(doc_ids, "dp", swap)
    ids = jnp.where(core == 0, jnp.stack([doc_ids, other_ids]), jnp.stack([other_ids, doc_ids]))

    def normed(values):
        xfloat = values.astype(F32)
        removed = xfloat - jnp.mean(xfloat, axis=-1, keepdims=True)
        inverse = lax.rsqrt(jnp.mean(removed * removed, axis=-1, keepdims=True) + NORM_EPS)
        return removed * inverse, inverse

    xhat_all = normed(tok_all)[0]
    h = (xhat_all * gain + shift).astype(BF)
    project = jnp.dot(h, wqkv, preferred_element_type=F32) + qkv_b
    found = [rotary_tables(ids[i]) for i in range(2)]
    begins = jnp.stack([t[0] for t in found])
    tables = jnp.stack([t[1] for t in found])
    queries, keys, values, o, lse_rows = attend(project, begins, tables)
    hidden = jnp.dot(h, wup, preferred_element_type=F32) + up_b
    u = gelu_tanh(hidden).astype(BF)
    br = (contract_cols(o, wot) + contract_cols(u, wdt)).astype(BF).reshape(2, toks, width)
    give = lax.dynamic_index_in_dim(br, 1 - core, 0, keepdims=False)
    keep = lax.dynamic_index_in_dim(br, core, 0, keepdims=False)
    br = (keep.astype(F32) + lax.ppermute(give, "dp", swap).astype(F32)).astype(BF)
    summed = lax.psum_scatter(br, "branch", scatter_dimension=0, tiled=True).astype(F32)
    xfloat = tokens.astype(F32)

    dact = jnp.dot(gm, wdt, preferred_element_type=F32)
    dz = jax.vjp(gelu_tanh, hidden)[1](dact)[0].astype(BF)
    do = jnp.dot(gm, wot, preferred_element_type=F32).astype(BF)
    dqkv = jnp.concatenate(attend_back(queries, keys, values, o, do, lse_rows, begins, tables), axis=1)
    dh_part = contract_cols(dz, wup) + contract_cols(dqkv, wqkv)
    dh = dh_part.astype(BF)

    part = norm_gain.shape[0]
    vectors = jnp.stack(
        [jnp.sum(dh_part * xhat_all, axis=0), jnp.sum(dh_part, axis=0), jnp.sum(masked_cot, axis=0, dtype=F32)]
    )
    vectors = vectors.reshape(3, dp_size, branch_size * part).transpose(1, 0, 2).reshape(dp_size, -1)
    q_sum = jnp.sum(dqkv, axis=0, dtype=F32).reshape(3, heads, dp_size, -1).transpose(2, 0, 1, 3).reshape(dp_size, -1)
    u_sum = jnp.sum(dz, axis=0, dtype=F32).reshape(b_up.shape[0] // 2, dp_size, -1).transpose(1, 0, 2)
    u_sum = u_sum.reshape(dp_size, -1)
    sums = jnp.concatenate([vectors, q_sum, u_sum], axis=1)
    ends = (vectors.shape[1], vectors.shape[1] + q_sum.shape[1], sums.shape[1])
    sums = jnp.pad(sums, ((0, 0), (0, 1024 - sums.shape[1]))).reshape(8 * dp_size, 128)
    sums, summed = lax.optimization_barrier((sums, summed))

    g_down, g_out, g_up, g_qkv, dh_mine, total = scatter_all(dp_size, branch_size, h, gm, dqkv, dz, o, u, dh, sums)
    total = total.reshape(3, 1024)
    block_out = (xfloat + my_real[:, None] * (summed + bias_full)).astype(BF)
    xhat, inverse = normed(tokens)
    scaled = dh_mine * gain
    input_grad = inverse * (
        scaled
        - jnp.mean(scaled, axis=-1, keepdims=True)
        - xhat * jnp.mean(scaled * xhat, axis=-1, keepdims=True)
    )
    tokens_grad = (cotangent.astype(F32) + input_grad).astype(BF)

    gain_g, shift_g, bias_g = lax.dynamic_slice_in_dim(
        total[2, : ends[0]].reshape(3, branch_size * part), branch * part, part, axis=1
    )
    b_q = total[:2, ends[0] : ends[1]].reshape(2, 3, heads, -1).transpose(1, 0, 2, 3).reshape(b_qkv.shape)
    b_u = total[:2, ends[1] : ends[2]].reshape(b_up.shape)
    g_qkv = g_qkv.reshape(2, w_rows, 3, cols).transpose(2, 1, 0, 3).reshape(w_qkv.shape)
    g_up = g_up.transpose(1, 0, 2).reshape(w_up.shape)
    g_out = g_out.transpose(0, 2, 1).reshape(w_out.shape)
    g_down = g_down.transpose(0, 2, 1).reshape(w_down.shape)
    return (block_out, tokens_grad, gain_g, shift_g, bias_g, g_qkv, b_q, g_out, g_up, b_u, g_down)


def solution(mesh):
    in_specs = (
        P(("dp", "branch"), None),
        P("dp"),
        P("dp"),
        P(("dp", "branch"), None),
        P(("dp", "branch")),
        P(("dp", "branch")),
        P(("dp", "branch")),
        P(None, "dp", "branch"),
        P(None, "branch", "dp"),
        P("branch", "dp"),
        P("dp", "branch"),
        P("branch", "dp"),
        P("branch", "dp"),
    )
    out_specs = (
        P(("dp", "branch"), None),
        P(("dp", "branch"), None),
        P(("dp", "branch")),
        P(("dp", "branch")),
        P(("dp", "branch")),
        P(None, "dp", "branch"),
        P(None, "branch", "dp"),
        P("branch", "dp"),
        P("dp", "branch"),
        P("branch", "dp"),
        P("branch", "dp"),
    )
    body = functools.partial(local, mesh.shape["dp"], mesh.shape["branch"])
    return jax.shard_map(body, mesh=mesh, in_specs=in_specs, out_specs=out_specs, check_vma=False)
```

time: 872 us -> 641 us (0.74)
  Pallas kernels: 0 us -> 396 us
  waiting for transfers between devices: 408 us -> 15.3 us
  matrix products: 223 us -> 104 us
  blocking collectives: 119 us -> 0 us
  other arithmetic: 66.1 us -> 45.7 us
  local copies, waits for them, and re-layouts: 32.2 us -> 50.3 us
    pallas_call x0 -> x4, Pallas kernels: none -> 396 us  [the longest x1 196 us: scatter_all(): pl.pallas_call(functools.partial(scatter_kernel, dp_size, branch_size), o...]
    reduce_scatter x6 -> x1, waiting for transfers between devices: 249 us -> 8.54 us  [local(): lax.psum_scatter(br, 'branch', scatter_dimension=0, tiled=True).astype(F32)]
    all_gather x6 -> x0, waiting for transfers between devices: 158 us -> none  [the longest x1 73.5 us: local(): gathered = lax.all_gather(normed_input, 'branch', axis=0, tiled=True)]
    dot_general x23 -> x4, matrix products: 185 us -> 45.5 us  [the longest x1 19 us: local(): dact = jnp.dot(gm, wdt, preferred_element_type=F32)]
    unnamed x3 -> x0, blocking collectives: 100 us -> none
    dot_general x3 -> x4, matrix products: 38.1 us -> 58.8 us  [contract_cols(): lax.dot_general(left, right, (((1,), (1,)), ((), ())), preferred_element_...]
    all_gather x2 -> x0, blocking collectives: 19 us -> none  [the longest x1 10.9 us: local(): lax.all_gather(b_qkv.astype(jnp.bfloat16), 'dp', axis=2, tiled=True)]
    convert_element_type x21 -> x10, other arithmetic: 40.7 us -> 22.5 us  [the longest x1 6.66 us: local(): h = (xhat_all * gain + shift).astype(BF)]
  transfers between devices with their start and end apart: 13 -> 3, of which waited for: 7 -> 2; matrix products, arithmetic and copies ran while one was open for 35% -> 21% of each run, Pallas kernels for 0% -> 29%
where the time goes in v1:
time: 641 us; the launch traced here: 631 us
  Pallas kernels  396 us (62%)
  matrix products  104 us (16%)
  local copies, waits for them, and re-layouts  50.3 us (8%)
  other arithmetic  45.7 us (7%)
  waiting for transfers between devices  15.3 us (2%)
  between operations  15.2 us (2%)
    pallas_call x1, Pallas kernels, scatter_all(): pl.pallas_call(functools.partial(scatter_kernel, dp_size, branch_size), o...  196 us
    pallas_call x1, Pallas kernels, gather_all(): pl.pallas_call(functools.partial(gather_kernel, dp_size, branch_size, n_w...  159 us
    dot_general x4, matrix products, contract_cols(): lax.dot_general(left, right, (((1,), (1,)), ((), ())), preferred_element_...  58.8 us
    unnamed x82, local copies, waits for them, and re-layouts  26.3 us
    pallas_call x1, Pallas kernels, attend_back(): pl.pallas_call(functools.partial(attend_back_kernel, min(256, toks)), gri...  21.8 us
    dot_general x1, matrix products, local(): dact = jnp.dot(gm, wdt, preferred_element_type=F32)  19 us
    pallas_call x1, Pallas kernels, attend(): pl.pallas_call(functools.partial(attend_kernel, min(256, toks)), grid=(bl...  18.8 us
  transfers between devices with their start and end apart: 3, of which 2 were waited for; matrix products, arithmetic and copies ran while one was open for 21% of the time, Pallas kernels for 29%

profile of v1, /device:TPU:1, one launch (start us, length us, event | category | flops | bytes accessed | tf_op | source)
XLA Modules:
  0.0 630.6 jit_solution(6988605983098680908)
XLA Ops:
  10.9 1.1 convert_element_type.110
  12.1 1.7 copy.71
  13.9 1.2 copy.77.refs_2_
  15.0 1.8 copy.73
  17.4 2.8 convert_element_type.111
  20.1 1.5 copy.76
  22.4 2.5 convert_reduce_fusion.4
  25.0 1.2 copy-done.4
  26.2 1.1 copy-done.5
  27.3 159.5 %gather_all.1 = (bf16[2048,2048]{1,0:T(8,128)(2,1)}, bf16[2048,2048]{1,0:T(8,128)(2,1)}, bf16[2048,768]{1,0:T(8,128)(2,1)S(1)}, bf16[2048,1024]{1,0:T(8,128)(2,1...) custom-call(bf16[256,2048]{1,0:T(8,128)(2,1)S(1)} %copy-done, ...), custom_call_target="tpu_custom_call" | custom-call | tf_op jit(solution)/shard_map/gather_all/pallas_call | solution.py:223
  187.8 2.1 copy-done.14
  189.8 1.9 copy-done.16
  191.8 1.7 copy-done.18
  193.7 4.7 convert_reduce_fusion
  198.4 1.1 copy-done.21
  199.5 2.3 fusion.7
  203.7 6.7 %fusion.5.refs_0_ = bf16[2048,2048]{1,0:T(8,128)(2,1)S(1)} fusion(bf16[2048,2048]{1,0:T(8,128)(2,1)} %get-tuple-element.36, f32[2048]{0:T(1024)S(1)} %add.119, f32[2048]{0:T(1024)S(1)} %mul.162, f32[2048]{0:T(1024)S(1)} %add_rsqrt_fusion, f32[2048]{0:T(1024)S(1)} %broadcast_multiply_fusion), kind=kLoop, calls=%fused_computation.7 | loop fusion | flops 25165824 | bytes 16809984 | tf_op jit(solution)/shard_map/convert_element_type | solution.py:699
  210.4 11.0 %fusion.37 = f32[2048,1024]{1,0:T(8,128)} fusion(bf16[2048,2048]{1,0:T(8,128)(2,1)S(1)} %fusion.5.refs_0_, bf16[2048,1024]{1,0:T(8,128)(2,1)S(1)} %copy-done.15), kind=kOutput, calls=%fused_computation.103 | convolution fusion | flops 8589934592 | bytes 20971520 | tf_op jit(solution)/shard_map/dot_general | solution.py:705
  221.4 19.0 %convert_reduce_fusion.1 = (f32[1024]{0:T(1024)}, bf16[2048,1024]{1,0:T(8,128)(2,1)}, bf16[2048,1024]{1,0:T(8,128)(2,1)}) fusion(f32[2048,1024]{1,0:T(8,128)} %fusion.37, f32[1024]{0:T(1024)} %bitcast.138, bf16[2048,2048]{1,0:T(8,128)(2,1)S(1)} %bitcast.105, bf16[2048,1024]{1,0:T(8,128)(2,1)S(1)} %copy-done.17), kind=kOutput, calls=%fused_computation.23 | convolution fusion | flops 8642362368 | bytes 29368320 | tf_op jit(solution)/shard_map/dot_general | solution.py:714
  240.5 14.2 %fusion.39 = f32[2048,2048]{1,0:T(8,128)} fusion(bf16[2048,1024]{1,0:T(8,128)(2,1)} %get-tuple-element.99.refs_5_, bf16[2048,1024]{1,0:T(8,128)(2,1)S(1)} %copy-done.17), kind=kOutput, calls=%fused_computation.105 | convolution fusion | flops 8589934592 | bytes 25165824 | tf_op jit(solution)/shard_map/dot_general | solution.py:641
  254.7 8.9 %broadcast_add_fusion.q_ref.k_ref.v_ref = f32[2048,768]{1,0:T(8,128)} fusion(f32[768]{0:T(1024)S(1)} %copy-done.31, bf16[2048,2048]{1,0:T(8,128)(2,1)S(1)} %fusion.5.refs_0_, bf16[2048,768]{1,0:T(8,128)(2,1)S(1)} %copy-done.19), kind=kOutput, calls=%fused_computation.30 | convolution fusion | flops 6444023808 | bytes 17828864 | tf_op jit(solution)/shard_map/dot_general | solution.py:700
  268.0 1.0 copy.81
  269.1 1.3 maximum_bitcast_fusion
  272.0 18.8 %attend.1 = (bf16[2048,256]{1,0:T(8,128)(2,1)S(1)}, bf16[2048,256]{1,0:T(8,128)(2,1)S(1)}, bf16[2048,256]{1,0:T(8,128)(2,1)S(1)}, bf16[2048,256]{1,0:T(8,128)(2,1)S(1)}, f32[2,2,2,1024]{3,2,1,0:T(2,128)S(1)}) custom-call(f32[2048,768]{1,0:T(8,128)S(1)} %bitcast.96, f32[2048,768]{1,0:T(8,128)S(1)} %bitcast.96, f32[2048,768]{1,0:T(8,128)S(1)} %bitcast.96, ...), custom_call_target="tpu_custom_call" | custom-call | tf_op jit(solution)/shard_map/attend/pallas_call | solution.py:592
  293.7 11.8 %add_convert_fusion = bf16[2048,2048]{1,0:T(8,128)(2,1)} fusion(f32[2048,2048]{1,0:T(8,128)} %fusion.39, bf16[2048,256]{1,0:T(8,128)(2,1)S(1)} %get-tuple-element.43.o_ref.refs_4_, bf16[2048,256]{1,0:T(8,128)(2,1)S(1)} %copy-done.13), kind=kOutput, calls=%fused_computation.10 | convolution fusion | flops 2155872256 | bytes 27262976 | tf_op jit(solution)/shard_map/dot_general | solution.py:641
  305.5 2.7 dynamic-slice_bitcast_fusion
  308.2 3.4 collective-permute-start.1
  311.6 6.8 %collective-permute-done.1 = bf16[1024,2048]{1,0:T(8,128)(2,1)S(1)} collective-permute-done((bf16[1024,2048]{1,0:T(8,128)(2,1)S(1)}, bf16[1024,2048]{1,0:T(8,128)(2,1)S(1)}, u32[]{:S(2)}, u32[]{:S(2)}) %collective-permute-start.1) | collective-permute-done | bytes 4194336 | tf_op jit(solution)/shard_map/ppermute | solution.py:710
  318.4 4.1 fusion.15
  323.3 1.4 convert_reduce_fusion.3
  324.7 1.6 fusion.23
  326.4 6.6 %convolution_convert_fusion.do_ref = bf16[2048,256]{1,0:T(8,128)(2,1)S(1)} fusion(bf16[2048,2048]{1,0:T(8,128)(2,1)} %get-tuple-element.34.refs_1_, bf16[2048,256]{1,0:T(8,128)(2,1)} %copy-done.12), kind=kOutput, calls=%fused_computation.36 | convolution fusion | flops 2148007936 | bytes 10485760 | tf_op jit(solution)/shard_map/dot_general | solution.py:716
  333.1 21.8 %attend_back.1 = (bf16[2048,256]{1,0:T(8,128)(2,1)S(1)}, bf16[2048,256]{1,0:T(8,128)(2,1)S(1)}, bf16[2048,256]{1,0:T(8,128)(2,1)S(1)}) custom-call(bf16[2048,256]{1,0:T(8,128)(2,1)S(1)} %copy-done.7, bf16[2048,256]{1,0:T(8,128)(2,1)S(1)} %copy-done.9, bf16[2048,256]{1,0:T(8,128)(2,1)S(1)} %copy-done.11, bf16[2048,256]{1,0:T(8,128)(2,1)S(1)} %copy-done.3, ...), custom_call_target="tpu_custom_call" | custom-call | tf_op jit(solution)/shard_map/attend_back/pallas_call | solution.py:609
  355.2 1.6 copy-done.24
  358.0 12.4 %fusion.38 = f32[2048,2048]{1,0:T(8,128)} fusion(bf16[2048,768]{1,0:T(8,128)(2,1)} %copy-done.24, bf16[2048,768]{1,0:T(8,128)(2,1)S(1)} %copy-done.20), kind=kOutput, calls=%fused_computation.104 | convolution fusion | flops 6442450944 | bytes 23068672 | tf_op jit(solution)/shard_map/dot_general | solution.py:641
  370.4 20.4 %fusion.6 = (f32[2048]{0:T(1024)S(1)}, f32[2048]{0:T(1024)S(1)}, bf16[2048,2048]{1,0:T(8,128)(2,1)}) fusion(bf16[2048,2048]{1,0:T(8,128)(2,1)} %get-tuple-element.36, f32[2048]{0:T(1024)S(1)} %add_rsqrt_fusion, f32[2048]{0:T(1024)S(1)} %broadcast_multiply_fusion, f32[2048,2048]{1,0:T(8,128)} %fusion.38, bf16[2048,1024]{1,0:T(8,128)(2,1)} %get-tuple-element.97.refs_3_, ...), kind=kOutput, calls=%fused_computation.8 | convolution fusion | flops 8623484928 | bytes 41975808 | tf_op jit(solution)/shard_map/dot_general | solution.py:641
  391.5 8.5 %reduce-scatter.2.cloned.1.call-done = bf16[256,2048]{1,0:T(8,128)(2,1)} async-done(((bf16[1024,2048]{1,0:T(8,128)(2,1)}), bf16[256,2048]{1,0:T(8,128)(2,1)}) %reduce-scatter.2.cloned.1.call-update) | async-done | bytes 1048592 | tf_op jit(solution)/shard_map/reduce_scatter | solution.py:711
  400.1 2.8 convert_element_type.129
  402.9 196.1 %scatter_all.1 = (f32[2,256,1024]{2,1,0:T(8,128)}, f32[2,256,256]{2,1,0:T(8,128)}, f32[2,256,1024]{2,1,0:T(8,128)}, f32[2,256,768]{2,1,0:T(8,128)}, f32[256,2048...) custom-call(bf16[2048,2048]{1,0:T(8,128)(2,1)} %copy-done.23, ...), custom_call_target="tpu_custom_call" | custom-call | tf_op jit(solution)/shard_map/scatter_all/pallas_call | solution.py:460
  599.8 2.2 multiply_reduce_fusion
  604.1 2.0 copy.92
  606.1 1.9 copy.89
  608.0 1.2 copy.90
  609.2 3.0 copy.95
  612.2 1.9 copy.93
  614.2 1.8 copy.96
  616.0 3.0 copy.94
  619.0 4.3 fusion.25
  (167 shorter events, 23.1 us)
Async XLA Ops:
  7.2 392.9 %reduce-scatter.2.cloned.1.call-start = ((), (), s32[]{:S(2)}) async-start(), calls=%async_computation.1 | async-start | bytes 5242880 | tf_op jit(solution)/shard_map/reduce_scatter | solution.py:711
  7.2 256.6 %collective-permute-start = (s32[1024]{0:T(1024)}, s32[1024]{0:T(1024)}, u32[]{:S(2)}, u32[]{:S(2)}) collective-permute-start(s32[1024]{0:T(1024)} %param.14), channel_id=1, source_target_pairs={{0,4},{4,0},{8,12},{12,8},{16,20},{20,16},{24,28},{28,24},{1,5},{5... | collective-permute-start | bytes 12296 | tf_op jit(solution)/shard_map/ppermute | solution.py:689
  17.3 7.6 %copy-start = (bf16[256,2048]{1,0:T(8,128)(2,1)S(1)}, bf16[256,2048]{1,0:T(8,128)(2,1)}, u32[]{:S(2)}) copy-start(bf16[256,2048]{1,0:T(8,128)(2,1)} %refs_0_.1) | copy-start | bytes 3145732
  22.4 176.0 %copy-start.28 = (f32[256]{0:T(256)}, f32[256]{0:T(256)S(1)}, u32[]{:S(2)}) copy-start(f32[256]{0:T(256)S(1)} %dynamic-slice_convert_fusion) | copy-start | bytes 3076
  25.0 1.2 copy-start.4
  26.2 1.1 copy-start.5
  186.8 1.0 copy-start.12
  187.8 2.1 copy-start.14
  189.8 1.9 copy-start.16
  191.8 1.7 copy-start.18
  193.7 5.8 copy-start.21
  201.9 8.4 %copy-start.26 = (f32[2048]{0:T(1024)}, f32[2048]{0:T(1024)S(1)}, u32[]{:S(2)}) copy-start(f32[2048]{0:T(1024)S(1)} %mul.162) | copy-start | bytes 24580
  203.7 6.7 %copy-start.15 = (bf16[2048,1024]{1,0:T(8,128)(2,1)S(1)}, bf16[2048,1024]{1,0:T(8,128)(2,1)}, u32[]{:S(2)}) copy-start(bf16[2048,1024]{1,0:T(8,128)(2,1)} %copy-done.14) | copy-start | bytes 12582916
  203.7 17.7 %slice-start.2 = ((s8[8388608]{0:T(1024)(128)(4,1)}), s8[4194304]{0:T(1024)(128)(4,1)S(1)}, s32[]{:S(2)}) async-start(s8[8388608]{0:T(1024)(128)(4,1)} %bitcast.104), calls=%async_computation.4 | async-start | bytes 8388608
  210.4 44.3 %copy-start.23 = (bf16[2048,2048]{1,0:T(8,128)(2,1)}, bf16[2048,2048]{1,0:T(8,128)(2,1)S(1)}, u32[]{:S(2)}) copy-start(bf16[2048,2048]{1,0:T(8,128)(2,1)S(1)} %fusion.5.refs_0_) | copy-start | bytes 25165828
  210.4 11.0 %copy-start.17 = (bf16[2048,1024]{1,0:T(8,128)(2,1)S(1)}, bf16[2048,1024]{1,0:T(8,128)(2,1)}, u32[]{:S(2)}) copy-start(bf16[2048,1024]{1,0:T(8,128)(2,1)} %copy-done.16) | copy-start | bytes 12582916
  210.4 11.0 %slice-start.3 = ((s8[8388608]{0:T(1024)(128)(4,1)}), s8[4194304]{0:T(1024)(128)(4,1)S(1)}, s32[]{:S(2)}) async-start(s8[8388608]{0:T(1024)(128)(4,1)} %bitcast.104), calls=%async_computation.5 | async-start | bytes 8388608
  240.5 14.2 %copy-start.19 = (bf16[2048,768]{1,0:T(8,128)(2,1)S(1)}, bf16[2048,768]{1,0:T(8,128)(2,1)}, u32[]{:S(2)}) copy-start(bf16[2048,768]{1,0:T(8,128)(2,1)} %copy-done.18) | copy-start | bytes 9437188
  240.5 14.2 %copy-start.31 = (f32[768]{0:T(1024)S(1)}, f32[768]{0:T(1024)}, u32[]{:S(2)}) copy-start(f32[768]{0:T(1024)} %add.130) | copy-start | bytes 9220
  254.7 9.1 %copy-start.32 = (s32[1024]{0:T(1024)S(1)}, s32[1024]{0:T(1024)}, u32[]{:S(2)}) copy-start(s32[1024]{0:T(1024)} %param.14) | copy-start | bytes 12292
  269.0 2.3 slice-start
  269.1 2.9 slice-start.1
  272.0 21.7 %copy-start.13 = (bf16[2048,256]{1,0:T(8,128)(2,1)S(1)}, bf16[2048,256]{1,0:T(8,128)(2,1)}, u32[]{:S(2)}) copy-start(bf16[2048,256]{1,0:T(8,128)(2,1)} %copy-done.12) | copy-start | bytes 3145732
  290.8 1.0 copy-start.6
  291.8 1.0 copy-start.8
  292.7 1.0 copy-start.10
  293.7 11.8 %copy-start.2 = (bf16[2048,256]{1,0:T(8,128)(2,1)}, bf16[2048,256]{1,0:T(8,128)(2,1)S(1)}, u32[]{:S(2)}) copy-start(bf16[2048,256]{1,0:T(8,128)(2,1)S(1)} %get-tuple-element.43.o_ref.refs_4_) | copy-start | bytes 3145732
  305.5 12.8 %copy-start.22 = (bf16[2048,2048]{1,0:T(8,128)(2,1)S(1)}, bf16[2048,2048]{1,0:T(8,128)(2,1)}, u32[]{:S(2)}) copy-start(bf16[2048,2048]{1,0:T(8,128)(2,1)} %add_convert_fusion) | copy-start | bytes 25165828
  308.2 10.2 %collective-permute-start.1 = (bf16[1024,2048]{1,0:T(8,128)(2,1)S(1)}, bf16[1024,2048]{1,0:T(8,128)(2,1)S(1)}, u32[]{:S(2)}, u32[]{:S(2)}) collective-permute-start(bf16[1024,2048]{1,0:T(8,128)(2,1)S(1)} %dynamic-slice_bitcast_fusion), channel_id=1, source_target_pairs={{0,4},{4,0},{8,12},{12,8},{16,20},{20,16},{24,28},{28,24},{1,5},{5... | collective-permute-start | bytes 12582920 | tf_op jit(solution)/shard_map/ppermute | solution.py:710
  322.4 0.7 copy-start.30
  326.4 6.7 %copy-start.3 = (bf16[2048,256]{1,0:T(8,128)(2,1)S(1)}, bf16[2048,256]{1,0:T(8,128)(2,1)}, u32[]{:S(2)}) copy-start(bf16[2048,256]{1,0:T(8,128)(2,1)} %copy-done.2) | copy-start | bytes 3145732
  326.4 6.7 %copy-start.7 = (bf16[2048,256]{1,0:T(8,128)(2,1)S(1)}, bf16[2048,256]{1,0:T(8,128)(2,1)}, u32[]{:S(2)}) copy-start(bf16[2048,256]{1,0:T(8,128)(2,1)} %copy-done.6) | copy-start | bytes 3145732
  326.4 6.7 %copy-start.9 = (bf16[2048,256]{1,0:T(8,128)(2,1)S(1)}, bf16[2048,256]{1,0:T(8,128)(2,1)}, u32[]{:S(2)}) copy-start(bf16[2048,256]{1,0:T(8,128)(2,1)} %copy-done.8) | copy-start | bytes 3145732
  326.4 6.7 %copy-start.11 = (bf16[2048,256]{1,0:T(8,128)(2,1)S(1)}, bf16[2048,256]{1,0:T(8,128)(2,1)}, u32[]{:S(2)}) copy-start(bf16[2048,256]{1,0:T(8,128)(2,1)} %copy-done.10) | copy-start | bytes 3145732
  355.0 3.0 copy-start.20
  355.2 1.6 copy-start.24
  402.9 196.9 %copy-start.1 = (bf16[256,2048]{1,0:T(8,128)(2,1)S(1)}, bf16[256,2048]{1,0:T(8,128)(2,1)}, u32[]{:S(2)}) copy-start(bf16[256,2048]{1,0:T(8,128)(2,1)} %refs_0_.1) | copy-start | bytes 3145732
  402.9 196.9 %copy-start.27 = (f32[2048]{0:T(1024)S(1)}, f32[2048]{0:T(1024)}, u32[]{:S(2)}) copy-start(f32[2048]{0:T(1024)} %copy-done.26) | copy-start | bytes 24580
  614.2 4.9 copy-start.29
  616.0 3.0 copy-start.25
Sparse Core Ops, SparseCore 0:
  322.6 77.4 reduce-scatter.1

commit v2 on v1

v2 whole, which is shorter than its diff:
```python
import functools
import math

import jax
import jax.numpy as jnp
import numpy as np
from jax import lax
from jax.experimental import pallas as pl
from jax.experimental.pallas import tpu as pltpu
from jax.sharding import PartitionSpec as P

HEAD_DIM = 64
ROT = 32
NORM_EPS = 1e-05
NEGATIVE = -1e30
BF = jnp.bfloat16
F32 = jnp.float32
MESH = pl.DeviceIdType.MESH
VMEM_LIMIT = 48 * 2**20
ROW_TILE = 256
GATHER_VMEM = 32 * 2**20


def ring_place(group):
    row = group // 2
    return 2 * row + (group + row) % 2


def ring_group(place):
    row = place // 2
    return 2 * row + (place + row) % 2


def chunk_rows(group, half, rows):
    return pl.ds(pl.multiple_of((2 * group + half) * rows, rows), rows)


class Links:
    def __init__(self, dp_size, branch_size):
        self.groups = dp_size // 2
        self.branches = branch_size
        dp = lax.axis_index("dp")
        self.core = dp % 2
        self.other = 1 - self.core
        self.group = dp // 2
        self.place = ring_place(self.group)
        self.branch = lax.axis_index("branch")
        self.sibling = {"dp": 2 * self.group + self.other}
        right = ring_group((self.place + 1) % self.groups)
        left = ring_group((self.place + self.groups - 1) % self.groups)
        self.ring = ({"dp": 2 * right + self.core}, {"dp": 2 * left + self.core})
        self.has_up = self.branch < self.branches - 1
        self.has_down = self.branch > 0
        self.peers = [{"branch": (self.branch + k) % branch_size} for k in range(1, branch_size)]
        self.up = {"branch": self.branch + 1}
        self.down = {"branch": self.branch - 1}

    def meet(self):
        barrier = pltpu.get_barrier_semaphore()

        def greet(device):
            pl.semaphore_signal(barrier, 1, device_id=device, device_id_type=MESH)

        greet(self.sibling)
        greet(self.ring[0])
        greet(self.ring[1])
        for device in self.peers:
            greet(device)
        pl.semaphore_wait(barrier, 3 + len(self.peers))


def remote(src, dst, send, recv, device):
    return pltpu.make_async_remote_copy(
        src_ref=src, dst_ref=dst, send_sem=send, recv_sem=recv, device_id=device, device_id_type=MESH
    )


def gather_kernel(dp_size, branch_size, n_w, *refs):
    rows_ref = refs[0]
    w_refs = refs[1 : 1 + n_w]
    full_ref = refs[1 + n_w]
    wf_refs = refs[2 + n_w : 2 + 2 * n_w]
    small_out = refs[2 + 2 * n_w]
    (z_send, z_recv, s_send, s_recv, l_sem, w_send, w_recv, ws_send, ws_recv, wl_sem, p_send, p_recv, p_local) = refs[
        3 + 2 * n_w :
    ]
    at = Links(dp_size, branch_size)
    at.meet()
    rows = rows_ref.shape[0]
    waits = []

    def piece(block, branch):
        start = (block * branch_size + branch) * rows
        return full_ref.at[pl.ds(pl.multiple_of(start, rows), rows)]

    for cond, way, device in ((at.has_up, 0, at.up), (at.has_down, 1, at.down)):
        copy = remote(rows_ref, piece(0, at.branch), z_send.at[way, 0], z_recv.at[at.branch], device)
        pl.when(cond)(copy.start)
        waits.append((cond, copy.wait_send))
    copy = remote(rows_ref, piece(1, at.branch), s_send.at[at.branch], s_recv.at[at.branch], at.sibling)
    copy.start()
    waits.append((None, copy.wait_send))
    own = pltpu.make_async_copy(rows_ref, piece(0, at.branch), l_sem)
    own.start()
    waits.append((None, own.wait))
    for w in range(n_w):
        here = chunk_rows(at.group, at.core, w_refs[w].shape[1])
        copy = remote(
            w_refs[w].at[at.other], wf_refs[w].at[here], ws_send.at[w], ws_recv.at[w], at.sibling
        )
        copy.start()
        waits.append((None, copy.wait_send))
        own = pltpu.make_async_copy(w_refs[w].at[at.core], wf_refs[w].at[here], wl_sem.at[w])
        own.start()

    def ring_copy(w, half, step):
        shift = step if half == 0 else -step
        source = ring_group((at.place - shift + at.groups) % at.groups)
        part = wf_refs[w].at[chunk_rows(source, half, w_refs[w].shape[1])]
        return remote(part, part, w_send.at[w, half, step], w_recv.at[w, half, step], at.ring[half])

    def ring_step(w, step):
        if step == 0:
            here = wf_refs[w].at[chunk_rows(at.group, at.core, w_refs[w].shape[1])]
            pltpu.make_async_copy(w_refs[w].at[at.core], here, wl_sem.at[w]).wait()
            there = wf_refs[w].at[chunk_rows(at.group, at.other, w_refs[w].shape[1])]
            remote(there, there, ws_send.at[w], ws_recv.at[w], at.sibling).wait_recv()
        for half in range(2):
            if step > 0:
                shift = step if half == 0 else -step
                source = ring_group((at.place - shift + at.groups) % at.groups)
                part = wf_refs[w].at[chunk_rows(source, half, w_refs[w].shape[1])]
                remote(
                    part, part, w_send.at[w, half, step - 1], w_recv.at[w, half, step - 1], at.ring[half]
                ).wait_recv()
            if step < at.groups - 1:
                copy = ring_copy(w, half, step)
                copy.start()
                waits.append((None, copy.wait_send))

    def line_step(step):
        for way in range(2):
            source = at.branch - step if way == 0 else at.branch + step
            inside = source >= 0 if way == 0 else source < branch_size
            onward = at.has_up if way == 0 else at.has_down
            device = at.up if way == 0 else at.down
            source = jnp.clip(source, 0, branch_size - 1)
            part = piece(0, source)
            forward = remote(part, part, z_send.at[way, step], z_recv.at[source], device)
            across = remote(part, piece(1, source), s_send.at[source], s_recv.at[source], at.sibling)

            @pl.when(inside)
            def _():
                forward.wait_recv()
                pl.when(onward)(forward.start)
                across.start()

            def both(inside=inside, onward=onward, forward=forward, across=across):
                @pl.when(inside)
                def _():
                    pl.when(onward)(forward.wait_send)
                    across.wait_send()

            waits.append((None, both))

    for w in range(n_w):
        ring_step(w, 0)
    line_steps = list(range(1, branch_size))
    ring_steps = [(w, s) for s in range(1, at.groups) for w in range(n_w)]
    events = [(23.0 * e, 0, e) for e in line_steps]
    events += [((i + 1.0) / len(ring_steps) * 103.0, 1, e) for i, e in enumerate(ring_steps)]
    for _, kind, event in sorted(events, key=lambda e: e[:2]):
        if kind == 0:
            line_step(event)
        else:
            ring_step(*event)
    params = wf_refs[n_w - 1]
    own = pltpu.make_async_copy(params, small_out.at[at.branch], p_local)
    own.start()
    waits.append((None, own.wait))
    for k in range(1, branch_size):
        copy = remote(params, small_out.at[at.branch], p_send.at[k], p_recv.at[k], at.peers[k - 1])
        copy.start()
        waits.append((None, copy.wait_send))
    for k in range(1, branch_size):
        slot = small_out.at[(at.branch - k + branch_size) % branch_size]
        remote(slot, slot, p_send.at[k], p_recv.at[k], at.peers[k - 1]).wait_recv()
    for branch in range(branch_size):
        part = piece(1, branch)
        remote(part, part, s_send.at[branch], s_recv.at[branch], at.sibling).wait_recv()
    for cond, wait in waits:
        if cond is None:
            wait()
        else:
            pl.when(cond)(wait)


def gather_all(dp_size, branch_size, array, weights):
    rows, width = array.shape
    n_w = len(weights)
    groups = dp_size // 2
    out_shape = [jax.ShapeDtypeStruct((2 * branch_size * rows, width), BF)]
    out_shape += [jax.ShapeDtypeStruct((dp_size * w.shape[1], w.shape[2]), BF) for w in weights]
    out_shape += [jax.ShapeDtypeStruct((branch_size, dp_size * weights[-1].shape[1], weights[-1].shape[2]), BF)]
    dma = pltpu.SemaphoreType.DMA
    return pl.pallas_call(
        functools.partial(gather_kernel, dp_size, branch_size, n_w),
        out_shape=out_shape,
        in_specs=[pl.BlockSpec(memory_space=pl.ANY)] * (1 + n_w),
        out_specs=[pl.BlockSpec(memory_space=pl.ANY)] * (2 + n_w),
        scratch_shapes=[
            dma((2, branch_size)),
            dma((branch_size,)),
            dma((branch_size,)),
            dma((branch_size,)),
            dma,
            dma((n_w, 2, groups)),
            dma((n_w, 2, groups)),
            dma((n_w,)),
            dma((n_w,)),
            dma((n_w,)),
            dma((branch_size,)),
            dma((branch_size,)),
            dma,
        ],
        compiler_params=pltpu.CompilerParams(
            collective_id=0, has_side_effects=True, vmem_limit_bytes=GATHER_VMEM
        ),
        cost_estimate=pl.CostEstimate(
            flops=100 * 4 * rows * width * width, bytes_accessed=2 * rows * width, transcendentals=0
        ),
        name="gather_all",
    )(array, *weights)


def scatter_kernel(dp_size, branch_size, *refs):
    n_w = 4
    (h_ref, gm_ref, other_ref, dqkv_ref, dz_ref, o_ref, u_ref, dh_ref, sums_ref) = refs[:9]
    g_refs = refs[9:13]
    tok_out, sum_out, sib_land = refs[13:16]
    slots = refs[16:20]
    got_refs = refs[20:24]
    outs = refs[24:28]
    ins = refs[28:32]
    (own_buf, sib_buf, line_slot, w_send, w_recv, ws_send, ws_recv, z_send, z_recv, s_send, s_recv,
     l_sem, left_buf, x_sem, i_sem, sum_slot, sum_first, sum_got, sum_peer, p_send, p_recv) = refs[32:]
    at = Links(dp_size, branch_size)
    at.meet()
    rows = own_buf.shape[0]
    toks = branch_size * rows
    w_rows = outs[2].shape[2]
    cols = dqkv_ref.shape[2]
    block = left_buf.shape[3]
    lefts = ((gm_ref, other_ref), (h_ref,))
    rights = (u_ref, o_ref, dz_ref, dqkv_ref)
    last = at.groups - 1
    waits = []
    sent = {}

    sib_copy = remote(dh_ref.at[pl.ds(toks, toks)], sib_land, s_send, s_recv, at.sibling)
    sib_copy.start()

    def ring_dest(half, step):
        shift = step + 1 if half == 0 else -step - 1
        return ring_group((at.place - shift + 2 * at.groups) % at.groups)

    def left_copy(a, half, step):
        dest = ring_dest(half, step)
        start = (2 * dest + half) * w_rows if block == w_rows else dest * block
        start = pl.multiple_of(start, block)
        size = left_buf.shape[2] // len(lefts[a])
        return [
            pltpu.make_async_copy(
                ref.at[:, pl.ds(start, block)], left_buf.at[a, half, pl.ds(i * size, size)], x_sem.at[a, half, i]
            )
            for i, ref in enumerate(lefts[a])
        ]

    def product(a, half, w):
        left = left_buf[a, half, :, pl.ds(half * (block - w_rows), w_rows)]

        def dot(right, flip=False):
            pair = (right, left) if flip else (left, right)
            return lax.dot_general(*pair, (((0,), (0,)), ((), ())), preferred_element_type=F32)

        if w < 3:
            return dot(rights[w][...], w < 2)
        return jnp.concatenate([dot(rights[w][c]) for c in range(3)], axis=1)

    def finish(w, values, core):
        if w < 2:
            size = values.shape[0]
            g_refs[w][pl.ds(pl.multiple_of(core * size, size), size), :] = values
        elif w == 2:
            size = values.shape[1]
            g_refs[w][:, pl.ds(pl.multiple_of(core * size, size), size)] = values
        else:
            for c in range(3):
                g_refs[w][c, :, pl.ds(pl.multiple_of(core * cols, cols), cols)] = values[:, c * cols : (c + 1) * cols]

    def ring_piece(a, half, i, step):
        w = 2 * a + i
        if i == 0:
            for load in left_copy(a, half, step):
                load.wait()
        total = product(a, half, w)
        if step > 0:
            slot = slots[w].at[half, step - 1]
            remote(
                slot, slot, w_send.at[w, half, step - 1], w_recv.at[w, half, step - 1], at.ring[half]
            ).wait_recv()
            load = pltpu.make_async_copy(slot, ins[w], i_sem)
            load.start()
            load.wait()
            total = total + ins[w][...].astype(F32)
        if step > 1:
            sent.pop((w, half, step - 2)).wait_send()
        out = outs[w].at[step % 2, half]
        if step < last:
            out[...] = total.astype(BF)
            copy = remote(
                out, slots[w].at[half, step], w_send.at[w, half, step], w_recv.at[w, half, step], at.ring[half]
            )
            copy.start()
            sent[w, half, step] = copy
        else:
            copy = remote(out, got_refs[w], ws_send.at[w], ws_recv.at[w], at.sibling)

            @pl.when(at.core == half)
            def _():
                finish(w, total, at.core)

            @pl.when(at.core != half)
            def _():
                out[...] = total.astype(BF)
                copy.start()

            waits.append(lambda copy=copy, half=half: pl.when(at.core != half)(copy.wait_send))
        if i == 1 and step < last:
            for load in left_copy(a, half, step + 1):
                load.start()

    def sum_step(step):
        for half in range(2):
            total = sums_ref[chunk_rows(ring_dest(half, step), half, 8)]
            if step > 0:
                slot = sum_slot.at[half, step - 1]
                remote(
                    slot, slot, w_send.at[n_w, half, step - 1], w_recv.at[n_w, half, step - 1], at.ring[half]
                ).wait_recv()
                total = total + slot[...]
            out = sum_first.at[step, half]
            out[...] = total
            if step < last:
                copy = remote(
                    out, sum_slot.at[half, step], w_send.at[n_w, half, step], w_recv.at[n_w, half, step], at.ring[half]
                )
                copy.start()
                waits.append(copy.wait_send)
        if step == last:
            copy = remote(sum_first.at[last, at.other], sum_got, ws_send.at[n_w], ws_recv.at[n_w], at.sibling)
            copy.start()
            copy.wait()
            mine = sum_peer.at[0]
            mine[...] = sum_first[last, at.core] + sum_got[...]
            sum_out[at.core] = sum_first[last, at.core]
            sum_out[at.other] = sum_got[...]
            for k in range(1, branch_size):
                copy = remote(mine, sum_peer.at[k], p_send.at[k], p_recv.at[k], at.peers[k - 1])
                copy.start()
                waits.append(copy.wait_send)

    def sum_end():
        total = sum_peer[0]
        for k in range(1, branch_size):
            remote(sum_peer.at[0], sum_peer.at[k], p_send.at[k], p_recv.at[k], at.peers[k - 1]).wait_recv()
            total = total + sum_peer[k]
        sum_out[2] = total

    def load_own(d):
        own = pltpu.make_async_copy(dh_ref.at[pl.ds(d * rows, rows)], own_buf, l_sem.at[0])
        sib = pltpu.make_async_copy(sib_land.at[pl.ds(d * rows, rows)], sib_buf, l_sem.at[1])
        own.start()
        sib.start()
        own.wait()
        sib.wait()

    def line_step(slot_time):
        far = branch_size - 1 - slot_time
        for way in range(2):
            d = at.branch + far if way == 0 else at.branch - far
            going = d < branch_size if way == 0 else d >= 0
            more = at.has_down if way == 0 else at.has_up
            device = at.up if way == 0 else at.down
            slot = line_slot.at[way, d - 1 + way]
            passing = remote(slot, slot, z_send.at[way, d], z_recv.at[way, d], device)

            @pl.when(going)
            def _():
                load_own(d)
                total = own_buf[...].astype(F32) + sib_buf[...].astype(F32)

                @pl.when(more)
                def _():
                    passing.wait_recv()
                    slot[...] = (total + slot[...].astype(F32)).astype(BF)

                @pl.when(jnp.logical_not(more))
                def _():
                    slot[...] = total.astype(BF)

                passing.start()

            waits.append(lambda going=going, passing=passing: pl.when(going)(passing.wait_send))

    def line_end():
        d = at.branch
        load_own(d)
        for way in range(2):
            more = at.has_down if way == 0 else at.has_up
            slot = line_slot.at[way, d - 1 + way]
            device = at.up if way == 0 else at.down

            @pl.when(more)
            def _():
                remote(slot, slot, z_send.at[way, d], z_recv.at[way, d], device).wait_recv()

        below, above = (
            jnp.where(at.has_down, line_slot[0, jnp.maximum(d - 1, 0)].astype(F32), 0.0),
            jnp.where(at.has_up, line_slot[1, jnp.minimum(d, branch_size - 2)].astype(F32), 0.0),
        )
        tok_out[...] = (own_buf[...].astype(F32) + sib_buf[...].astype(F32) + below + above).astype(BF)

    for a in range(2):
        for half in range(2):
            for load in left_copy(a, half, 0):
                load.start()
    sum_step(0)
    pieces = [(a, half, i) for a in range(2) for half in range(2) for i in range(2)]
    size = [rights[2 * a + i].shape[-1] * (1 + a * i * 2) for a, half, i in pieces]
    due = [sum(size[: i + 1]) / sum(size) for i in range(len(pieces))]
    period = 34.0
    events = [(period * (s - 1 + f) + 4.0, 1, (*p, s)) for s in range(1, at.groups) for p, f in zip(pieces, due)]
    events += [(2.0 * i, 1, (*p, 0)) for i, p in enumerate(pieces)]
    events += [(9.0 + 24.0 * k, 0, k) for k in range(branch_size)]
    events += [(10.0 + 12.0 * s, 2, s) for s in range(1, at.groups)]
    events += [(18.0 + 12.0 * at.groups, 3, 0)]
    for _, kind, event in sorted(events, key=lambda e: e[:2]):
        if kind == 0 and event == 0:
            sib_copy.wait_recv()
        if kind == 0 and event == branch_size - 1:
            line_end()
        elif kind == 0:
            line_step(event)
        elif kind == 1:
            ring_piece(*event)
        elif kind == 2:
            sum_step(event)
        else:
            sum_end()
    for w in range(n_w):
        remote(outs[w].at[0, 0], got_refs[w], ws_send.at[w], ws_recv.at[w], at.sibling).wait_recv()
        finish(w, got_refs[w][...].astype(F32), at.other)
    sib_copy.wait_send()
    for copy in sent.values():
        copy.wait_send()
    for wait in waits:
        wait()


def scatter_all(dp_size, branch_size, h, gm, gm_other, dqkv, dz, o, u, dh, sums):
    widths = [u.shape[1], o.shape[1], dz.shape[1], 3 * dqkv.shape[2]]
    width = h.shape[1]
    w_rows = width // dp_size
    groups = dp_size // 2
    toks = h.shape[0] // 2
    rows = toks // branch_size
    n_w = 4
    dma = pltpu.SemaphoreType.DMA
    vm = pl.BlockSpec(memory_space=pltpu.VMEM)
    hb = pl.BlockSpec(memory_space=pl.ANY)
    shapes = [(widths[0], w_rows), (widths[1], w_rows), (w_rows, widths[2]), (w_rows, widths[3])]
    out_shape = [
        jax.ShapeDtypeStruct((2 * widths[0], w_rows), F32),
        jax.ShapeDtypeStruct((2 * widths[1], w_rows), F32),
        jax.ShapeDtypeStruct((w_rows, 2 * widths[2]), F32),
        jax.ShapeDtypeStruct((3, w_rows, 2 * dqkv.shape[2]), F32),
    ]
    out_shape += [jax.ShapeDtypeStruct((rows, width), BF), jax.ShapeDtypeStruct((3, 8, 128), F32)]
    out_shape += [jax.ShapeDtypeStruct((toks, width), BF)]
    out_shape += [jax.ShapeDtypeStruct((2, groups - 1) + shape, BF) for shape in shapes]
    out = pl.pallas_call(
        functools.partial(scatter_kernel, dp_size, branch_size),
        out_shape=out_shape,
        in_specs=[hb] * 3 + [vm] * 4 + [hb, vm],
        out_specs=[vm] * 6 + [hb] * 5,
        scratch_shapes=[pltpu.VMEM(shape, BF) for shape in shapes]
        + [pltpu.VMEM((2, 2) + shape, BF) for shape in shapes]
        + [pltpu.VMEM(shape, BF) for shape in shapes]
        + [
            pltpu.VMEM((rows, width), BF),
            pltpu.VMEM((rows, width), BF),
            pltpu.VMEM((2, branch_size - 1, rows, width), BF),
            dma((n_w + 1, 2, groups)),
            dma((n_w + 1, 2, groups)),
            dma((n_w + 1,)),
            dma((n_w + 1,)),
            dma((2, branch_size)),
            dma((2, branch_size)),
            dma(()),
            dma(()),
            dma((2,)),
            pltpu.VMEM((2, 2, 2 * toks, w_rows if w_rows % 128 == 0 else 2 * w_rows), BF),
            dma((2, 2, 2)),
            dma(()),
            pltpu.VMEM((2, groups - 1, 8, 128), F32),
            pltpu.VMEM((groups, 2, 8, 128), F32),
            pltpu.VMEM((8, 128), F32),
            pltpu.VMEM((branch_size, 8, 128), F32),
            dma((branch_size,)),
            dma((branch_size,)),
        ],
        compiler_params=pltpu.CompilerParams(
            collective_id=1, has_side_effects=True, vmem_limit_bytes=VMEM_LIMIT
        ),
        cost_estimate=pl.CostEstimate(
            flops=4 * toks * width * sum(widths), bytes_accessed=2 * toks * width, transcendentals=0
        ),
        name="scatter_all",
    )(h, gm, gm_other, dqkv, dz, o, u, dh, sums)
    return out[:4], out[4], out[5]


def turn(values, tables, sign):
    fixed, from_low, from_high = tables
    half = ROT // 2
    return (
        values * fixed
        + sign * (pltpu.roll(values, half, 1) * from_low + pltpu.roll(values, 2 * HEAD_DIM - half, 1) * from_high)
    )


def score_tile(keys, queries, begins, first, q_tile):
    scores = lax.dot_general(keys, queries, (((1,), (1,)), ((), ())), preferred_element_type=F32)
    key_at = lax.broadcasted_iota(jnp.int32, scores.shape, 0)
    query_at = first + lax.broadcasted_iota(jnp.int32, scores.shape, 1)
    allowed = jnp.logical_and(key_at >= begins, key_at <= query_at)
    return jnp.where(allowed, scores, NEGATIVE)


def attend_kernel(q_tile, q_ref, k_ref, v_ref, begin_ref, fixed_ref, low_ref, high_ref, qr_ref, kr_ref, vr_ref, o_ref, lse_ref):
    tables = (fixed_ref[0], low_ref[0], high_ref[0])
    qr_ref[...] = (turn(q_ref[...], tables, 1.0) * (HEAD_DIM**-0.5)).astype(BF)
    kr_ref[...] = turn(k_ref[...], tables, 1.0).astype(BF)
    vr_ref[...] = v_ref[...].astype(BF)
    toks = q_ref.shape[0]
    for first in range(0, toks, q_tile):
        span = first + q_tile
        begins = begin_ref[0, 0:1, first:span]
        outs = []
        for head in range(2):
            lanes = slice(head * HEAD_DIM, (head + 1) * HEAD_DIM)
            scores = score_tile(kr_ref[:span, lanes], qr_ref[first:span, lanes], begins, first, q_tile)
            top = jnp.max(scores, axis=0, keepdims=True)
            weights = jnp.exp(scores - top)
            total = jnp.sum(weights, axis=0, keepdims=True)
            lse_ref[0, 0, head : head + 1, first:span] = top + jnp.log(total)
            mixed = lax.dot_general(
                vr_ref[:span, lanes], weights.astype(BF), (((0,), (0,)), ((), ())), preferred_element_type=F32
            )
            outs.append(mixed / total)
        o_ref[first:span, :] = jnp.concatenate(outs, axis=0).T.astype(BF)


def attend_back_kernel(
    q_tile, qr_ref, kr_ref, vr_ref, o_ref, do_ref, lse_ref, begin_ref, fixed_ref, low_ref, high_ref, grad_ref, k_acc, v_acc
):
    tables = (fixed_ref[0], low_ref[0], high_ref[0])
    toks = qr_ref.shape[0]
    k_acc[...] = jnp.zeros_like(k_acc)
    v_acc[...] = jnp.zeros_like(v_acc)
    for first in range(0, toks, q_tile):
        span = first + q_tile
        begins = begin_ref[0, 0:1, first:span]
        both = (do_ref[first:span, :].astype(F32) * o_ref[first:span, :].astype(F32)).T
        turned = []
        for head in range(2):
            lanes = slice(head * HEAD_DIM, (head + 1) * HEAD_DIM)
            delta = jnp.sum(both[lanes], axis=0, keepdims=True)
            queries = qr_ref[first:span, lanes]
            grads = do_ref[first:span, lanes]
            keys = kr_ref[:span, lanes]
            scores = score_tile(keys, queries, begins, first, q_tile)
            prob = jnp.exp(scores - lse_ref[0, 0, head : head + 1, first:span])
            v_acc[head, :span, :] += jnp.dot(prob.astype(BF), grads, preferred_element_type=F32)
            dprob = lax.dot_general(
                vr_ref[:span, lanes], grads, (((1,), (1,)), ((), ())), preferred_element_type=F32
            )
            ds = (prob * (dprob - delta)).astype(BF)
            k_acc[head, :span, :] += jnp.dot(ds, queries, preferred_element_type=F32)
            turned.append(
                lax.dot_general(keys, ds, (((0,), (0,)), ((), ())), preferred_element_type=F32)
            )
        dq = jnp.concatenate(turned, axis=0).T * (HEAD_DIM**-0.5)
        grad_ref[0, first:span, :] = turn(dq, tuple(t[first:span] for t in tables), -1.0).astype(BF)
    dk = jnp.concatenate([k_acc[0], k_acc[1]], axis=1)
    grad_ref[1] = turn(dk, tables, -1.0).astype(BF)
    grad_ref[2] = jnp.concatenate([v_acc[0], v_acc[1]], axis=1).astype(BF)


def attention_specs(toks, pairs):
    wide = 2 * HEAD_DIM

    def cols(shift):
        return pl.BlockSpec((toks, wide), lambda i, j: (i, j + shift * pairs))

    begin = pl.BlockSpec((1, 8, toks), lambda i, j: (i, 0, 0))
    table = pl.BlockSpec((1, toks, wide), lambda i, j: (i, 0, 0))
    lse = pl.BlockSpec((1, 1, 2, toks), lambda i, j: (i, j, 0, 0))
    return cols, begin, table, lse


def attend(project, begins, tables):
    blocks, _, toks = begins.shape
    pairs = project.shape[1] // (6 * HEAD_DIM)
    cols, begin, table, lse = attention_specs(toks, pairs)
    narrow = jax.ShapeDtypeStruct((blocks * toks, pairs * 2 * HEAD_DIM), BF)
    return pl.pallas_call(
        functools.partial(attend_kernel, min(256, toks)),
        grid=(blocks, pairs),
        in_specs=[cols(0), cols(1), cols(2), begin] + [table] * 3,
        out_specs=[cols(0)] * 4 + [lse],
        out_shape=[narrow] * 4 + [jax.ShapeDtypeStruct((blocks, pairs, 2, toks), F32)],
        compiler_params=pltpu.CompilerParams(vmem_limit_bytes=GATHER_VMEM),
        name="attend",
    )(project, project, project, begins, *tables)


def attend_back(queries, keys, values, o, do, lse_rows, begins, tables):
    blocks, _, toks = begins.shape
    pairs = queries.shape[1] // (2 * HEAD_DIM)
    cols, begin, table, lse = attention_specs(toks, pairs)
    acc = pltpu.VMEM((2, toks, HEAD_DIM), F32)
    return pl.pallas_call(
        functools.partial(attend_back_kernel, min(256, toks)),
        grid=(blocks, pairs),
        in_specs=[cols(0)] * 5 + [lse, begin] + [table] * 3,
        out_specs=pl.BlockSpec((3, toks, 2 * HEAD_DIM), lambda i, j: (0, i, j)),
        out_shape=jax.ShapeDtypeStruct((3,) + queries.shape, BF),
        scratch_shapes=[acc, acc],
        compiler_params=pltpu.CompilerParams(vmem_limit_bytes=GATHER_VMEM),
        name="attend_back",
    )(queries, keys, values, o, do, lse_rows, begins, *tables)


def rotary_tables(doc_rows):
    row_count = doc_rows.shape[0]
    row_index = jnp.arange(row_count, dtype=jnp.int32)
    same = doc_rows[:, None] == doc_rows[None, :]
    begins = jnp.min(jnp.where(same, row_index[:, None], row_count), axis=0)
    places = (row_index - begins).astype(F32)
    half = ROT // 2
    lane = np.arange(2 * HEAD_DIM) % HEAD_DIM
    turning = lane < ROT
    frequency = np.where(turning, 10000.0 ** (-2.0 * (lane % half) / ROT), 0.0).astype(np.float32)
    angles = places[:, None] * frequency[None, :]
    sine = jnp.sin(angles)
    from_low = sine * np.where(turning & (lane >= half), 1.0, 0.0).astype(np.float32)
    from_high = sine * np.where(lane < half, -1.0, 0.0).astype(np.float32)
    return jnp.broadcast_to(begins[None], (8, row_count)), (jnp.cos(angles), from_low, from_high)


def dot_nt(left, right):
    return lax.dot_general(left, right, (((1,), (1,)), ((), ())), preferred_element_type=F32)


def standardized(rows):
    xfloat = rows.astype(F32)
    removed = xfloat - jnp.mean(xfloat, axis=-1, keepdims=True)
    inverse = lax.rsqrt(jnp.mean(removed * removed, axis=-1, keepdims=True) + NORM_EPS)
    return removed * inverse, inverse


def enter_kernel(tok_ref, gain_ref, shift_ref, wq_ref, qb_ref, wu_ref, ub_ref, h_ref, project_ref, u_ref, slope_ref):
    h = (standardized(tok_ref[...])[0] * gain_ref[0:1] + shift_ref[0:1]).astype(BF)
    h_ref[...] = h
    project_ref[...] = jnp.dot(h, wq_ref[...], preferred_element_type=F32) + qb_ref[0:1]
    z = jnp.dot(h, wu_ref[...], preferred_element_type=F32) + ub_ref[0:1]
    scale, cubic = math.sqrt(2.0 / math.pi), 0.044715
    square = z * z
    bent = jnp.tanh(scale * z * (1.0 + cubic * square))
    half = 0.5 * (1.0 + bent)
    u_ref[...] = (z * half).astype(BF)
    slope = half + 0.5 * z * (1.0 - bent * bent) * (scale * (1.0 + 3.0 * cubic * square))
    slope_ref[...] = slope.astype(BF)


def branch_kernel(o_ref, u_ref, wo_ref, wd_ref, br_ref):
    br_ref[...] = (dot_nt(o_ref[...], wo_ref[...]) + dot_nt(u_ref[...], wd_ref[...])).astype(BF)


def grad_kernel(gm_ref, other_ref, slope_ref, wo_ref, wd_ref, do_ref, dz_ref, sum_ref):
    step = pl.program_id(0)

    @pl.when(step == 0)
    def _():
        sum_ref[...] = jnp.zeros_like(sum_ref)

    def use(rows_ref):
        gm = rows_ref[...]
        do_ref[...] = jnp.dot(gm, wo_ref[...], preferred_element_type=F32).astype(BF)
        dz = jnp.dot(gm, wd_ref[...], preferred_element_type=F32) * slope_ref[...].astype(F32)
        dz = dz.astype(BF)
        dz_ref[...] = dz
        sum_ref[0:1] += jnp.sum(dz.astype(F32), axis=0, keepdims=True)

    own = step < pl.num_programs(0) // 2
    pl.when(own)(lambda: use(gm_ref))
    pl.when(jnp.logical_not(own))(lambda: use(other_ref))


def leave_kernel(tok_ref, grad_ref, dz_ref, wq_ref, wu_ref, dh_ref, sum_ref, q_sum_ref):
    @pl.when(pl.program_id(0) == 0)
    def _():
        sum_ref[...] = jnp.zeros_like(sum_ref)
        q_sum_ref[...] = jnp.zeros_like(q_sum_ref)

    cols = grad_ref.shape[2]
    grads = jnp.concatenate([grad_ref[c] for c in range(3)], axis=1)
    dh = dot_nt(dz_ref[...], wu_ref[...]) + dot_nt(grads, wq_ref[...])
    dh_ref[...] = dh.astype(BF)
    xhat = standardized(tok_ref[...])[0]
    sum_ref[0:1] += jnp.sum(dh * xhat, axis=0, keepdims=True)
    sum_ref[1:2] += jnp.sum(dh, axis=0, keepdims=True)
    q_sum_ref[0:1] += jnp.sum(grads.astype(F32), axis=0, keepdims=True)


def row_call(kernel, name, tiles, tiled, whole, outs, sums):
    tile = ROW_TILE

    def spec(width):
        return pl.BlockSpec((tile, width), lambda i: (i, 0))

    in_specs = [s if s is not None else spec(x.shape[1]) for x, s in tiled]
    in_specs += [pl.BlockSpec(x.shape, lambda i: (0, 0)) for x in whole]
    flops = 2 * tiles * tile * sum(x.size for x in whole)
    traffic = 2 * sum(x.size for x in whole) + 2 * sum(x.size for x, _ in tiled) + 4 * tiles * tile * sum(w for w, _ in outs)
    return pl.pallas_call(
        kernel,
        grid=(tiles,),
        in_specs=in_specs,
        out_specs=[spec(w) for w, _ in outs] + [pl.BlockSpec((8, w), lambda i: (0, 0)) for w in sums],
        out_shape=[jax.ShapeDtypeStruct((tiles * tile, w), t) for w, t in outs]
        + [jax.ShapeDtypeStruct((8, w), F32) for w in sums],
        compiler_params=pltpu.CompilerParams(vmem_limit_bytes=VMEM_LIMIT),
        cost_estimate=pl.CostEstimate(flops=flops, bytes_accessed=traffic, transcendentals=0),
        name=name,
    )(*[x for x, _ in tiled], *whole)


def local(
    dp_size, branch_size, tokens, doc_ids, real_rows, cotangent, norm_gain, norm_shift, out_bias,
    w_qkv, b_qkv, w_out, w_up, b_up, w_down,
):
    dp = lax.axis_index("dp")
    branch = lax.axis_index("branch")
    core = dp % 2
    my_rows, width = tokens.shape
    toks = doc_ids.shape[0]
    w_rows = w_qkv.shape[1]
    cols = w_qkv.shape[2] // 2
    hid = w_up.shape[1] // 2
    heads = cols // HEAD_DIM

    my_real = lax.dynamic_slice_in_dim(real_rows, branch * my_rows, my_rows).astype(F32)
    masked_cot = (cotangent.astype(F32) * my_real[:, None]).astype(BF)
    qkv_l = w_qkv.astype(BF).reshape(3, w_rows, 2, cols).transpose(2, 1, 0, 3).reshape(2, w_rows, 3 * cols)
    up_l = w_up.astype(BF).reshape(w_rows, 2, hid).transpose(1, 0, 2)
    out_l = w_out.astype(BF).T.reshape(w_rows, 2, cols).transpose(1, 0, 2)
    down_l = w_down.astype(BF).T.reshape(w_rows, 2, hid).transpose(1, 0, 2)

    small = jnp.concatenate([v.reshape(-1) for v in (norm_gain, norm_shift, out_bias, b_qkv, b_up)]).astype(BF)
    small = jnp.pad(small, (0, -small.size % 128))
    small = jnp.broadcast_to(small[None, None], (2, 16, small.size))

    tok_all, wqkv, wup, wot, wdt, _, params = gather_all(
        dp_size, branch_size, tokens, (qkv_l, up_l, out_l, down_l, small)
    )
    swap = [(i, i + 1 - 2 * (i % 2)) for i in range(dp_size)]
    late_cot, tok_all = lax.optimization_barrier((masked_cot, tok_all))
    gm_own = lax.all_gather(late_cot, "branch", axis=0, tiled=True)
    params = params.reshape(branch_size, dp_size, 16, -1)[:, :, 0].astype(F32)
    sizes = [norm_gain.size, norm_shift.size, out_bias.size, b_qkv.size, b_up.size]
    stops = [sum(sizes[: i + 1]) for i in range(5)]
    gain, shift, bias_full = (
        params[:, :, stops[i] - sizes[i] : stops[i]].transpose(1, 0, 2).reshape(width) for i in range(3)
    )
    mine = lax.dynamic_index_in_dim(params, branch, 0, keepdims=False)
    qkv_b = mine[:, stops[2] : stops[3]].reshape((dp_size,) + b_qkv.shape).transpose(1, 2, 0, 3)
    qkv_b = qkv_b.reshape(3, 2, cols)
    qkv_b = lax.dynamic_index_in_dim(qkv_b, core, 1, keepdims=False).reshape(3 * cols)
    up_b = mine[:, stops[3] : stops[4]].reshape((dp_size,) + b_up.shape).transpose(1, 0, 2).reshape(2, hid)
    up_b = lax.dynamic_index_in_dim(up_b, core, 0, keepdims=False)
    ids = jnp.stack([doc_ids, lax.ppermute(doc_ids, "dp", swap)])

    def row(values):
        return jnp.broadcast_to(values[None], (8, values.size))

    tiles = 2 * toks // ROW_TILE
    h, project, u, slope = row_call(
        enter_kernel, "enter", tiles, [(tok_all, None)], [row(gain), row(shift), wqkv, row(qkv_b), wup, row(up_b)],
        [(width, BF), (3 * cols, F32), (hid, BF), (hid, BF)], [],
    )
    found = [rotary_tables(ids[i]) for i in range(2)]
    begins = jnp.stack([t[0] for t in found])
    tables = [jnp.stack([t[1][i] for t in found]) for i in range(3)]
    queries, keys, values, o, lse_rows = attend(project, begins, tables)
    gm_own, _ = lax.optimization_barrier((gm_own, o))
    gm_other = lax.ppermute(gm_own, "dp", swap)
    half_tiles = tiles // 2

    def branch_out(first):
        def later(width):
            return pl.BlockSpec((ROW_TILE, width), lambda i: (i + first, 0))

        return row_call(
            branch_kernel, "branch_out", half_tiles, [(o, later(cols)), (u, later(hid))], [wot, wdt], [(width, BF)], []
        )[0]

    given = lax.ppermute(branch_out(half_tiles), "dp", swap)
    br = (branch_out(0).astype(F32) + given.astype(F32)).astype(BF)
    xfloat = tokens.astype(F32)

    near = pl.BlockSpec((ROW_TILE, width), lambda i: (jnp.minimum(i, half_tiles - 1), 0))
    far = pl.BlockSpec((ROW_TILE, width), lambda i: (jnp.maximum(i - half_tiles, 0), 0))
    do, dz, up_sums = row_call(
        grad_kernel, "branch_grad", tiles, [(gm_own, near), (gm_other, far), (slope, None)], [wot, wdt],
        [(cols, BF), (hid, BF)], [hid],
    )
    do, br = lax.optimization_barrier((do, br))
    summed = lax.psum_scatter(br, "branch", scatter_dimension=0, tiled=True).astype(F32)
    dqkv = attend_back(queries, keys, values, o, do, lse_rows, begins, tables)
    three = pl.BlockSpec((3, ROW_TILE, cols), lambda i: (0, i, 0))
    dh, token_sums, q_sums = row_call(
        leave_kernel, "leave", tiles, [(tok_all, None), (dqkv, three), (dz, None)], [wqkv, wup],
        [(width, BF)], [width, 3 * cols],
    )

    part = norm_gain.shape[0]
    vectors = jnp.stack(
        [token_sums[0], token_sums[1], jnp.sum(masked_cot, axis=0, dtype=F32)]
    )
    vectors = vectors.reshape(3, dp_size, branch_size * part).transpose(1, 0, 2).reshape(dp_size, -1)
    q_sum = q_sums[0].reshape(3, heads, dp_size, -1).transpose(2, 0, 1, 3).reshape(dp_size, -1)
    u_sum = up_sums[0].reshape(b_up.shape[0] // 2, dp_size, -1).transpose(1, 0, 2)
    u_sum = u_sum.reshape(dp_size, -1)
    sums = jnp.concatenate([vectors, q_sum, u_sum], axis=1)
    ends = (vectors.shape[1], vectors.shape[1] + q_sum.shape[1], sums.shape[1])
    sums = jnp.pad(sums, ((0, 0), (0, 1024 - sums.shape[1]))).reshape(8 * dp_size, 128)

    (g_down, g_out, g_up, g_qkv), dh_mine, total = scatter_all(
        dp_size, branch_size, h, gm_own, gm_other, dqkv, dz, o, u, dh, sums
    )
    dh_mine = dh_mine.astype(F32)
    total = total.reshape(3, 1024)
    block_out = (xfloat + my_real[:, None] * (summed + bias_full)).astype(BF)
    xhat, inverse = standardized(tokens)
    scaled = dh_mine * gain
    input_grad = inverse * (
        scaled
        - jnp.mean(scaled, axis=-1, keepdims=True)
        - xhat * jnp.mean(scaled * xhat, axis=-1, keepdims=True)
    )
    tokens_grad = (cotangent.astype(F32) + input_grad).astype(BF)

    gain_g, shift_g, bias_g = lax.dynamic_slice_in_dim(
        total[2, : ends[0]].reshape(3, branch_size * part), branch * part, part, axis=1
    )
    b_q = total[:2, ends[0] : ends[1]].reshape(2, 3, heads, -1).transpose(1, 0, 2, 3).reshape(b_qkv.shape)
    b_u = total[:2, ends[1] : ends[2]].reshape(b_up.shape)
    return (block_out, tokens_grad, gain_g, shift_g, bias_g, g_qkv, b_q, g_out, g_up, b_u, g_down)


def solution(mesh):
    in_specs = (
        P(("dp", "branch"), None),
        P("dp"),
        P("dp"),
        P(("dp", "branch"), None),
        P(("dp", "branch")),
        P(("dp", "branch")),
        P(("dp", "branch")),
        P(None, "dp", "branch"),
        P(None, "branch", "dp"),
        P("branch", "dp"),
        P("dp", "branch"),
        P("branch", "dp"),
        P("branch", "dp"),
    )
    out_specs = (
        P(("dp", "branch"), None),
        P(("dp", "branch"), None),
        P(("dp", "branch")),
        P(("dp", "branch")),
        P(("dp", "branch")),
        P(None, "dp", "branch"),
        P(None, "branch", "dp"),
        P("branch", "dp"),
        P("dp", "branch"),
        P("branch", "dp"),
        P("branch", "dp"),
    )
    body = functools.partial(local, mesh.shape["dp"], mesh.shape["branch"])
    return jax.shard_map(body, mesh=mesh, in_specs=in_specs, out_specs=out_specs, check_vma=False)
```

time: 641 us -> 503 us (0.78)
  matrix products: 104 us -> 0 us
  other arithmetic: 45.7 us -> 29.2 us
  waiting for transfers between devices: 15.3 us -> 8.15 us
    dot_general x8 -> x0, matrix products: 104 us -> none  [the longest x4 58.8 us: contract_cols(): lax.dot_general(left, right, (((1,), (1,)), ((), ())), preferred_element_...]
    pallas_call x0 -> x5, Pallas kernels: none -> 93.7 us  [row_call(): pl.pallas_call(kernel, grid=(tiles,), in_specs=in_specs, out_specs=[spec(...]
    pallas_call x1, Pallas kernels: 196 us -> 136 us  [scatter_all(): pl.pallas_call(functools.partial(scatter_kernel, dp_size, branch_size), o...]
    pallas_call x1, Pallas kernels: 159 us -> 124 us  [gather_all(): pl.pallas_call(functools.partial(gather_kernel, dp_size, branch_size, n_w...]
    unnamed x82 -> x91, local copies, waits for them, and re-layouts: 26.3 us -> 39.7 us
    reduce_sum x5 -> x2, other arithmetic: 10.6 us -> 0.64 us  [the longest x1 0.42 us: standardized(): jnp.mean(removed * removed, axis=-1, keepdims=True) + NORM_EPS]
    reduce_scatter x1, waiting for transfers between devices: 8.54 us -> 0.01 us  [local(): lax.psum_scatter(br, 'branch', scatter_dimension=0, tiled=True).astype(F32)]
    transpose x6 -> x2, local copies, waits for them, and re-layouts: 8.25 us -> 0.02 us  [the longest x1 0.01 us: local(): q_sums[0].reshape(3, heads, dp_size, -1).transpose(2, 0, 1, 3)]
  transfers between devices with their start and end apart: 3 -> 5, of which waited for: 2 -> 1; matrix products, arithmetic and copies ran while one was open for 21% -> 4% of each run, Pallas kernels for 29% -> 51%
where the time goes in v2:
time: 503 us; the launch traced here: 497 us
  Pallas kernels  395 us (79%)
  local copies, waits for them, and re-layouts  47.8 us (10%)
  other arithmetic  29.2 us (6%)
  between operations  14.8 us (3%)
  waiting for transfers between devices  8.15 us (2%)
    pallas_call x1, Pallas kernels, scatter_all(): pl.pallas_call(functools.partial(scatter_kernel, dp_size, branch_size), o...  136 us
    pallas_call x1, Pallas kernels, gather_all(): pl.pallas_call(functools.partial(gather_kernel, dp_size, branch_size, n_w...  124 us
    pallas_call x5, Pallas kernels, row_call(): pl.pallas_call(kernel, grid=(tiles,), in_specs=in_specs, out_specs=[spec(...  93.7 us
    unnamed x91, local copies, waits for them, and re-layouts  39.7 us
    pallas_call x1, Pallas kernels, attend_back(): pl.pallas_call(functools.partial(attend_back_kernel, min(256, toks)), gri...  21.8 us
    pallas_call x1, Pallas kernels, attend(): pl.pallas_call(functools.partial(attend_kernel, min(256, toks)), grid=(bl...  18.6 us
  transfers between devices with their start and end apart: 5, of which 1 were waited for; matrix products, arithmetic and copies ran while one was open for 4% of the time, Pallas kernels for 51%

profile of v2, /device:TPU:1, one launch (start us, length us, event | category | flops | bytes accessed | tf_op | source)
XLA Modules:
  0.0 497.1 jit_solution(1933213583499150355)
XLA Ops:
  10.8 1.1 convert_element_type.83
  12.0 1.7 copy.56
  13.8 1.2 copy.62.refs_1_
  14.9 1.8 copy.58
  17.2 2.7 convert_element_type.84
  19.9 1.6 copy.61
  22.8 3.1 convert_reduce_fusion.1
  26.0 1.1 copy-done.19
  27.2 124.5 %gather_all.1 = (bf16[2048,2048]{1,0:T(8,128)(2,1)}, bf16[2048,768]{1,0:T(8,128)(2,1)S(1)}, bf16[2048,1024]{1,0:T(8,128)(2,1)S(1)}, bf16[2048,256]{1,0:T(8,128)(...) custom-call(bf16[256,2048]{1,0:T(8,128)(2,1)S(1)} %copy-done.1, ...), custom_call_target="tpu_custom_call" | custom-call | flops 429496729600 | bytes 1048576 | tf_op jit(solution)/shard_map/gather_all/pallas_call | solution.py:206
  151.6 0.8 copy-done.22
  152.5 1.9 copy-done.23
  154.4 1.0 copy-done.24
  155.4 2.0 copy-done.28
  157.4 1.7 copy-done.29
  159.2 1.5 collective-permute-start
  160.7 1.0 slice.50
  163.3 1.9 copy-done.30
  165.2 30.2 %enter.1 = (bf16[2048,2048]{1,0:T(8,128)(2,1)}, f32[2048,768]{1,0:T(8,128)}, bf16[2048,1024]{1,0:T(8,128)(2,1)}, bf16[2048,1024]{1,0:T(8,128)(2,1)}) custom-call(bf16[2048,2048]{1,0:T(8,128)(2,1)} %get-tuple-element.45.tok_ref, f32[8,2048]{1,0:T(8,128)S(1)} %broadcast_in_dim.38.gain_ref, f32[8,2048]{1,0:T(8,128)S(1)} %broadcast_in_dim.40.shift_ref, ...), custom_call_target="tpu_custom_call" | custom-call | flops 15225323520 | bytes 55668736 | tf_op jit(solution)/shard_map/enter/pallas_call | solution.py:748
  196.1 3.8 fusion.14
  200.1 2.9 copy-done
  203.1 18.6 %attend.1 = (bf16[2048,256]{1,0:T(8,128)(2,1)S(1)}, bf16[2048,256]{1,0:T(8,128)(2,1)S(1)}, bf16[2048,256]{1,0:T(8,128)(2,1)S(1)}, bf16[2048,256]{1,0:T(8,128)(2,1)S(1)}, f32[2,2,2,1024]{3,2,1,0:T(2,128)S(1)}) custom-call(f32[2048,768]{1,0:T(8,128)S(1)} %copy-done, f32[2048,768]{1,0:T(8,128)S(1)} %copy-done, f32[2048,768]{1,0:T(8,128)S(1)} %copy-done, ...), custom_call_target="tpu_custom_call" | custom-call | tf_op jit(solution)/shard_map/attend/pallas_call | solution.py:628
  221.7 1.0 copy-done.11
  222.7 1.0 copy-done.13
  223.7 1.0 copy-done.15
  224.6 10.0 %branch_out.3 = bf16[1024,2048]{1,0:T(8,128)(2,1)} custom-call(bf16[2048,256]{1,0:T(8,128)(2,1)S(1)} %get-tuple-element.50.o_ref.refs_5_, bf16[2048,1024]{1,0:T(8,128)(2,1)} %get-tuple-element.56.u_ref.refs_6_, bf16[2048,256]{1,0:T(8,128)(2,1)S(1)} %copy-done.25, bf16[2048,1024]{1,0:T(8,128)(2,1)} %copy-done.23), custom_call_target="tpu_custom_call" | custom-call | flops 5368709120 | bytes 18874368 | tf_op jit(solution)/shard_map/branch_out/pallas_call | solution.py:748
  234.7 8.1 %all-gather.2.cloned.1.call-done.gm_ref.refs_1_ = bf16[1024,2048]{1,0:T(8,128)(2,1)} async-done(((bf16[256,2048]{1,0:T(8,128)(2,1)}), bf16[1024,2048]{1,0:T(8,128)(2,1)}) %all-gather.2.cloned.1.call-update) | async-done | bytes 4194320 | tf_op jit(solution)/shard_map/all_gather | solution.py:791
  243.4 1.2 copy-done.8
  244.7 1.2 copy-done.26
  245.9 9.6 %branch_out.2 = bf16[1024,2048]{1,0:T(8,128)(2,1)} custom-call(bf16[2048,256]{1,0:T(8,128)(2,1)S(1)} %copy-done.8, bf16[2048,1024]{1,0:T(8,128)(2,1)} %get-tuple-element.56.u_ref.refs_6_, bf16[2048,256]{1,0:T(8,128)(2,1)S(1)} %copy-done.26, bf16[2048,1024]{1,0:T(8,128)(2,1)} %copy-done.23), custom_call_target="tpu_custom_call" | custom-call | flops 5368709120 | bytes 18874368 | tf_op jit(solution)/shard_map/branch_out/pallas_call | solution.py:748
  255.5 7.7 %add_convert_fusion = bf16[1024,2048]{1,0:T(8,128)(2,1)} fusion(bf16[1024,2048]{1,0:T(8,128)(2,1)} %collective-permute-done.2, bf16[1024,2048]{1,0:T(8,128)(2,1)} %branch_out.2), kind=kLoop, calls=%fused_computation | loop fusion | flops 8388608 | bytes 12582912 | tf_op jit(solution)/shard_map/convert_element_type | solution.py:831
  263.2 1.2 copy-done.27
  264.4 16.8 %branch_grad.1 = (bf16[2048,256]{1,0:T(8,128)(2,1)S(1)}, bf16[2048,1024]{1,0:T(8,128)(2,1)}, f32[8,1024]{1,0:T(8,128)S(1)}) custom-call(bf16[1024,2048]{1,0:T(8,128)(2,1)} %all-gather.2.cloned.1.call-done.gm_ref.refs_1_, bf16[1024,2048]{1,0:T(8,128)(2,1)} %collective-permute-done.1.other_ref.refs_2_, bf16[2048,1024]{1,0:T(8,128)(2,1)} %get-tuple-element.52.slope_ref, ...), custom_call_target="tpu_custom_call" | custom-call | flops 10737418240 | bytes 28311552 | tf_op jit(solution)/shard_map/branch_grad/pallas_call | solution.py:748
  281.2 1.0 copy-done.17
  284.5 1.2 copy-done.12
  285.7 1.4 copy-done.14
  287.2 1.3 copy-done.16
  288.5 1.2 copy-done.18
  289.7 21.8 %attend_back.1.grad_ref.refs_3_ = bf16[3,2048,256]{2,1,0:T(8,128)(2,1)S(1)} custom-call(bf16[2048,256]{1,0:T(8,128)(2,1)S(1)} %copy-done.12, bf16[2048,256]{1,0:T(8,128)(2,1)S(1)} %copy-done.14, bf16[2048,256]{1,0:T(8,128)(2,1)S(1)} %copy-done.16, bf16[2048,256]{1,0:T(8,128)(2,1)S(1)} %copy-done.9, bf16[2048,256]{1,0:T(8,128)(2,1)S(1)} %copy-done.18, ...), custom_call_target="tpu_custom_call" | custom-call | tf_op jit(solution)/shard_map/attend_back/pallas_call | solution.py:644
  311.5 27.1 %leave.1 = (bf16[2048,2048]{1,0:T(8,128)(2,1)}, f32[8,2048]{1,0:T(8,128)S(1)}, f32[8,768]{1,0:T(8,128)S(1)}) custom-call(bf16[2048,2048]{1,0:T(8,128)(2,1)} %get-tuple-element.45.tok_ref, bf16[3,2048,256]{2,1,0:T(8,128)(2,1)S(1)} %attend_back.1.grad_ref.refs_3_, bf16[2048,1024]{1,0:T(8,128)(2,1)} %get-tuple-element.64.dz_ref.refs_4_, ...), custom_call_target="tpu_custom_call" | custom-call | flops 15032385536 | bytes 39845888 | tf_op jit(solution)/shard_map/leave/pallas_call | solution.py:748
  339.2 136.3 %scatter_all.1 = (f32[2048,256]{1,0:T(8,128)}, f32[512,256]{1,0:T(8,128)S(1)}, f32[256,2048]{1,0:T(8,128)}, f32[3,256,512]{2,1,0:T(8,128)S(1)}, bf16[256,2048]{1...) custom-call(bf16[2048,2048]{1,0:T(8,128)(2,1)} %get-tuple-element.58, ...), custom_call_target="tpu_custom_call" | custom-call | flops 25769803776 | bytes 4194304 | tf_op jit(solution)/shard_map/scatter_all/pallas_call | solution.py:492
  475.5 1.1 copy-done.5
  476.7 0.8 copy-done.20
  480.2 3.8 fusion.9
  484.1 1.1 copy.86
  485.5 0.8 copy.87
  486.4 1.3 copy.88
  487.7 1.0 copy-done.32
  488.8 1.3 copy.89
  (145 shorter events, 14.9 us)
Async XLA Ops:
  7.2 235.6 %all-gather.2.cloned.1.call-start = ((), (), s32[]{:S(2)}) async-start(), calls=%async_computation.1 | async-start | bytes 5242880 | tf_op jit(solution)/shard_map/all_gather | solution.py:791
  19.9 6.1 %copy-start.1 = (bf16[256,2048]{1,0:T(8,128)(2,1)S(1)}, bf16[256,2048]{1,0:T(8,128)(2,1)}, u32[]{:S(2)}) copy-start(bf16[256,2048]{1,0:T(8,128)(2,1)} %refs_0_.1) | copy-start | bytes 3145732
  22.2 0.6 copy-start.36
  26.0 1.1 copy-start.19
  27.2 132.0 %copy-start.35 = (s32[1024]{0:T(1024)S(1)}, s32[1024]{0:T(1024)}, u32[]{:S(2)}) copy-start(s32[1024]{0:T(1024)} %param.20) | copy-start | bytes 12292
  151.6 0.8 copy-start.22
  152.5 1.9 copy-start.23
  154.4 1.0 copy-start.24
  155.4 2.0 copy-start.28
  157.4 1.7 copy-start.29
  159.1 321.1 %reduce-scatter.2.cloned.1.call-start = ((), (), s32[]{:S(2)}) async-start(), calls=%async_computation.2 | async-start | bytes 5242880 | tf_op jit(solution)/shard_map/reduce_scatter | solution.py:841
  159.2 36.2 %collective-permute-start = (s32[1024]{0:T(1024)S(1)}, s32[1024]{0:T(1024)S(1)}, u32[]{:S(2)}, u32[]{:S(2)}) collective-permute-start(s32[1024]{0:T(1024)S(1)} %copy-done.35), channel_id=1, source_target_pairs={{0,4},{4,0},{8,12},{12,8},{16,20},{20,16},{24,28},{28,24},{1,5},{5... | collective-permute-start | bytes 12296 | tf_op jit(solution)/shard_map/ppermute | solution.py:804
  163.3 1.9 copy-start.30
  165.2 30.9 %copy-start.38 = (f32[128]{0:T(128)S(1)}, f32[128]{0:T(128)}, u32[]{:S(2)}) copy-start(f32[128]{0:T(128)} %constant.67) | copy-start | bytes 1540
  165.2 30.9 %copy-start.39 = (f32[128]{0:T(128)S(1)}, f32[128]{0:T(128)}, u32[]{:S(2)}) copy-start(f32[128]{0:T(128)} %constant.64.clone) | copy-start | bytes 1540
  165.2 30.9 %copy-start.40 = (f32[128]{0:T(128)S(1)}, f32[128]{0:T(128)}, u32[]{:S(2)}) copy-start(f32[128]{0:T(128)} %constant.63.clone) | copy-start | bytes 1540
  199.9 3.2 copy-start
  200.1 21.6 %copy-start.2 = (f32[2,1024,128]{2,1,0:T(8,128)}, f32[2,1024,128]{2,1,0:T(8,128)S(1)}, u32[]{:S(2)}) copy-start(f32[2,1024,128]{2,1,0:T(8,128)S(1)} %get-tuple-element.99.low_ref) | copy-start | bytes 3145732
  203.1 21.6 %copy-start.25 = (bf16[2048,256]{1,0:T(8,128)(2,1)S(1)}, bf16[2048,256]{1,0:T(8,128)(2,1)}, u32[]{:S(2)}) copy-start(bf16[2048,256]{1,0:T(8,128)(2,1)} %copy-done.24) | copy-start | bytes 3145732
  221.7 1.0 copy-start.11
  222.7 1.0 copy-start.13
  223.7 1.0 copy-start.15
  224.6 10.0 %copy-start.7 = (bf16[2048,256]{1,0:T(8,128)(2,1)}, bf16[2048,256]{1,0:T(8,128)(2,1)S(1)}, u32[]{:S(2)}) copy-start(bf16[2048,256]{1,0:T(8,128)(2,1)S(1)} %get-tuple-element.50.o_ref.refs_5_) | copy-start | bytes 3145732
  234.6 20.8 %collective-permute-start.2 = (bf16[1024,2048]{1,0:T(8,128)(2,1)}, bf16[1024,2048]{1,0:T(8,128)(2,1)}, u32[]{:S(2)}, u32[]{:S(2)}) collective-permute-start(bf16[1024,2048]{1,0:T(8,128)(2,1)} %branch_out.3), channel_id=1, source_target_pairs={{0,4},{4,0},{8,12},{12,8},{16,20},{20,16},{24,28},{28,24},{1,5},{5... | collective-permute-start | bytes 12582920 | tf_op jit(solution)/shard_map/ppermute | solution.py:830
  242.8 20.4 %collective-permute-start.1 = (bf16[1024,2048]{1,0:T(8,128)(2,1)}, bf16[1024,2048]{1,0:T(8,128)(2,1)}, u32[]{:S(2)}, u32[]{:S(2)}) collective-permute-start(bf16[1024,2048]{1,0:T(8,128)(2,1)} %all-gather.2.cloned.1.call-done.gm_ref.refs_1_), channel_id=1, source_target_pairs={{0,4},{4,0},{8,12},{12,8},{16,20},{20,16},{24,28},{28,24},{1,5},{5... | collective-permute-start | bytes 12582920 | tf_op jit(solution)/shard_map/ppermute | solution.py:819
  243.4 1.2 copy-start.8
  244.7 1.2 copy-start.26
  263.2 1.2 copy-start.27
  281.2 1.0 copy-start.17
  282.2 0.7 copy-start.34
  283.0 1.2 copy-start.3
  283.0 1.5 copy-start.9
  284.5 1.2 copy-start.12
  285.7 1.4 copy-start.14
  287.2 1.3 copy-start.16
  288.5 1.2 copy-start.18
  311.5 27.2 %copy-start.4 = (bf16[3,2048,256]{2,1,0:T(8,128)(2,1)}, bf16[3,2048,256]{2,1,0:T(8,128)(2,1)S(1)}, u32[]{:S(2)}) copy-start(bf16[3,2048,256]{2,1,0:T(8,128)(2,1)S(1)} %attend_back.1.grad_ref.refs_3_) | copy-start | bytes 9437188
  311.5 27.7 %copy-start.10 = (bf16[2048,256]{1,0:T(8,128)(2,1)S(1)}, bf16[2048,256]{1,0:T(8,128)(2,1)}, u32[]{:S(2)}) copy-start(bf16[2048,256]{1,0:T(8,128)(2,1)} %copy-done.7) | copy-start | bytes 3145732
  475.5 1.1 copy-start.5
  476.7 0.8 copy-start.20
  477.5 2.8 copy-start.31
  477.5 2.8 copy-start.37
  480.2 3.9 copy-start.6
  484.1 1.4 copy-start.21
  484.1 2.3 copy-start.33
  486.4 2.3 copy-start.32
Sparse Core Ops, SparseCore 0:
  159.2 83.4 all-gather.1
  282.3 74.7 reduce-scatter.1

commit v3 on v2

--- a/solution.py
+++ b/solution.py
@@ -17,8 +17,10 @@
 F32 = jnp.float32
 MESH = pl.DeviceIdType.MESH
 VMEM_LIMIT = 48 * 2**20
-ROW_TILE = 256
-GATHER_VMEM = 32 * 2**20
+ROW_TILE = 512
+ENTER_VMEM = 48 * 2**20
+FIRST_HOP = 2
+GATHER_VMEM = 48 * 2**20
 
 
 def ring_place(group):
@@ -75,6 +77,59 @@
     )
 
 
+class WeightRing:
+    def __init__(self, at, parts, fulls, sems):
+        self.at, self.parts, self.fulls = at, parts, fulls
+        self.send, self.recv, self.near_send, self.near_recv, self.local = sems
+
+    def rows(self, w, group, half):
+        return self.fulls[w].at[chunk_rows(group, half, self.parts[w].shape[1])]
+
+    def near(self, w):
+        at = self.at
+        here = self.rows(w, at.group, at.core)
+        return remote(self.parts[w].at[at.other], here, self.near_send.at[w], self.near_recv.at[w], at.sibling)
+
+    def own(self, w):
+        at = self.at
+        return pltpu.make_async_copy(self.parts[w].at[at.core], self.rows(w, at.group, at.core), self.local.at[w])
+
+    def hop(self, w, half, step):
+        at = self.at
+        shift = step if half == 0 else -step
+        part = self.rows(w, ring_group((at.place - shift + at.groups) % at.groups), half)
+        return remote(part, part, self.send.at[w, half, step], self.recv.at[w, half, step], at.ring[half])
+
+    def share(self):
+        for w in range(len(self.parts)):
+            self.near(w).start()
+            self.own(w).start()
+
+    def shared(self):
+        for w in range(len(self.parts)):
+            self.own(w).wait()
+            there = self.rows(w, self.at.group, self.at.other)
+            remote(there, there, self.near_send.at[w], self.near_recv.at[w], self.at.sibling).wait_recv()
+
+    def step(self, w, step):
+        at = self.at
+        for half in range(2):
+            if step > 0:
+                shift = step if half == 0 else -step
+                part = self.rows(w, ring_group((at.place - shift + at.groups) % at.groups), half)
+                sems = self.send.at[w, half, step - 1], self.recv.at[w, half, step - 1]
+                remote(part, part, *sems, at.ring[half]).wait_recv()
+            if step < at.groups - 1:
+                self.hop(w, half, step).start()
+
+    def drain(self):
+        for w in range(len(self.parts)):
+            self.near(w).wait_send()
+            for half in range(2):
+                for step in range(self.at.groups - 1):
+                    self.hop(w, half, step).wait_send()
+
+
 def gather_kernel(dp_size, branch_size, n_w, *refs):
     rows_ref = refs[0]
     w_refs = refs[1 : 1 + n_w]
@@ -103,40 +158,11 @@
     own = pltpu.make_async_copy(rows_ref, piece(0, at.branch), l_sem)
     own.start()
     waits.append((None, own.wait))
+    ring = WeightRing(at, w_refs, wf_refs, (w_send, w_recv, ws_send, ws_recv, wl_sem))
+    ring.share()
+    ring.shared()
     for w in range(n_w):
-        here = chunk_rows(at.group, at.core, w_refs[w].shape[1])
-        copy = remote(
-            w_refs[w].at[at.other], wf_refs[w].at[here], ws_send.at[w], ws_recv.at[w], at.sibling
-        )
-        copy.start()
-        waits.append((None, copy.wait_send))
-        own = pltpu.make_async_copy(w_refs[w].at[at.core], wf_refs[w].at[here], wl_sem.at[w])
-        own.start()
-
-    def ring_copy(w, half, step):
-        shift = step if half == 0 else -step
-        source = ring_group((at.place - shift + at.groups) % at.groups)
-        part = wf_refs[w].at[chunk_rows(source, half, w_refs[w].shape[1])]
-        return remote(part, part, w_send.at[w, half, step], w_recv.at[w, half, step], at.ring[half])
-
-    def ring_step(w, step):
-        if step == 0:
-            here = wf_refs[w].at[chunk_rows(at.group, at.core, w_refs[w].shape[1])]
-            pltpu.make_async_copy(w_refs[w].at[at.core], here, wl_sem.at[w]).wait()
-            there = wf_refs[w].at[chunk_rows(at.group, at.other, w_refs[w].shape[1])]
-            remote(there, there, ws_send.at[w], ws_recv.at[w], at.sibling).wait_recv()
-        for half in range(2):
-            if step > 0:
-                shift = step if half == 0 else -step
-                source = ring_group((at.place - shift + at.groups) % at.groups)
-                part = wf_refs[w].at[chunk_rows(source, half, w_refs[w].shape[1])]
-                remote(
-                    part, part, w_send.at[w, half, step - 1], w_recv.at[w, half, step - 1], at.ring[half]
-                ).wait_recv()
-            if step < at.groups - 1:
-                copy = ring_copy(w, half, step)
-                copy.start()
-                waits.append((None, copy.wait_send))
+        ring.step(w, 0)
 
     def line_step(step):
         for way in range(2):
@@ -163,17 +189,15 @@
 
             waits.append((None, both))
 
-    for w in range(n_w):
-        ring_step(w, 0)
     line_steps = list(range(1, branch_size))
     ring_steps = [(w, s) for s in range(1, at.groups) for w in range(n_w)]
     events = [(23.0 * e, 0, e) for e in line_steps]
-    events += [((i + 1.0) / len(ring_steps) * 103.0, 1, e) for i, e in enumerate(ring_steps)]
+    events += [((i + 1.0) / len(ring_steps) * 69.0, 1, e) for i, e in enumerate(ring_steps)]
     for _, kind, event in sorted(events, key=lambda e: e[:2]):
         if kind == 0:
             line_step(event)
         else:
-            ring_step(*event)
+            ring.step(*event)
     params = wf_refs[n_w - 1]
     own = pltpu.make_async_copy(params, small_out.at[at.branch], p_local)
     own.start()
@@ -188,6 +212,7 @@
     for branch in range(branch_size):
         part = piece(1, branch)
         remote(part, part, s_send.at[branch], s_recv.at[branch], at.sibling).wait_recv()
+    ring.drain()
     for cond, wait in waits:
         if cond is None:
             wait()
@@ -206,8 +231,8 @@
     return pl.pallas_call(
         functools.partial(gather_kernel, dp_size, branch_size, n_w),
         out_shape=out_shape,
-        in_specs=[pl.BlockSpec(memory_space=pl.ANY)] * (1 + n_w),
-        out_specs=[pl.BlockSpec(memory_space=pl.ANY)] * (2 + n_w),
+        in_specs=[pl.BlockSpec(memory_space=pltpu.HBM)] * (1 + n_w),
+        out_specs=[pl.BlockSpec(memory_space=pltpu.HBM)] * (2 + n_w),
         scratch_shapes=[
             dma((2, branch_size)),
             dma((branch_size,)),
@@ -478,7 +503,7 @@
     n_w = 4
     dma = pltpu.SemaphoreType.DMA
     vm = pl.BlockSpec(memory_space=pltpu.VMEM)
-    hb = pl.BlockSpec(memory_space=pl.ANY)
+    hb = pl.BlockSpec(memory_space=pltpu.HBM)
     shapes = [(widths[0], w_rows), (widths[1], w_rows), (w_rows, widths[2]), (w_rows, widths[3])]
     out_shape = [
         jax.ShapeDtypeStruct((2 * widths[0], w_rows), F32),
@@ -631,7 +656,7 @@
         in_specs=[cols(0), cols(1), cols(2), begin] + [table] * 3,
         out_specs=[cols(0)] * 4 + [lse],
         out_shape=[narrow] * 4 + [jax.ShapeDtypeStruct((blocks, pairs, 2, toks), F32)],
-        compiler_params=pltpu.CompilerParams(vmem_limit_bytes=GATHER_VMEM),
+        compiler_params=pltpu.CompilerParams(vmem_limit_bytes=60 * 2**20),
         name="attend",
     )(project, project, project, begins, *tables)
 
@@ -648,7 +673,7 @@
         out_specs=pl.BlockSpec((3, toks, 2 * HEAD_DIM), lambda i, j: (0, i, j)),
         out_shape=jax.ShapeDtypeStruct((3,) + queries.shape, BF),
         scratch_shapes=[acc, acc],
-        compiler_params=pltpu.CompilerParams(vmem_limit_bytes=GATHER_VMEM),
+        compiler_params=pltpu.CompilerParams(vmem_limit_bytes=60 * 2**20),
         name="attend_back",
     )(queries, keys, values, o, do, lse_rows, begins, *tables)
 
@@ -681,7 +706,23 @@
     return removed * inverse, inverse
 
 
-def enter_kernel(tok_ref, gain_ref, shift_ref, wq_ref, qb_ref, wu_ref, ub_ref, h_ref, project_ref, u_ref, slope_ref):
+def enter_kernel(
+    dp_size, branch_size, tok_ref, gain_ref, shift_ref, wq_ref, qb_ref, wu_ref, ub_ref, part_ref,
+    h_ref, project_ref, u_ref, slope_ref, full_ref, *sems,
+):
+    tile_at, tiles = pl.program_id(0), pl.num_programs(0)
+    at = Links(dp_size, branch_size)
+    ring = WeightRing(at, [part_ref], [full_ref], sems)
+
+    @pl.when(tile_at == 0)
+    def _():
+        at.meet()
+        ring.share()
+        ring.shared()
+        ring.step(0, 0)
+
+    pl.when(tile_at == FIRST_HOP)(lambda: ring.step(0, 1))
+
     h = (standardized(tok_ref[...])[0] * gain_ref[0:1] + shift_ref[0:1]).astype(BF)
     h_ref[...] = h
     project_ref[...] = jnp.dot(h, wq_ref[...], preferred_element_type=F32) + qb_ref[0:1]
@@ -694,9 +735,49 @@
     slope = half + 0.5 * z * (1.0 - bent * bent) * (scale * (1.0 + 3.0 * cubic * square))
     slope_ref[...] = slope.astype(BF)
 
-
-def branch_kernel(o_ref, u_ref, wo_ref, wd_ref, br_ref):
-    br_ref[...] = (dot_nt(o_ref[...], wo_ref[...]) + dot_nt(u_ref[...], wd_ref[...])).astype(BF)
+    @pl.when(tile_at == tiles - 1)
+    def _():
+        for step in range(2, at.groups):
+            ring.step(0, step)
+        ring.drain()
+
+
+def enter(dp_size, branch_size, tok_all, gain, shift, wqkv, qkv_b, wup, up_b, part):
+    total, width = tok_all.shape
+    groups = dp_size // 2
+    tile = ROW_TILE
+    dma = pltpu.SemaphoreType.DMA
+
+    def spec(width):
+        return pl.BlockSpec((tile, width), lambda i: (i, 0))
+
+    whole = (gain, shift, wqkv, qkv_b, wup, up_b)
+    outs = [(width, BF), (wqkv.shape[1], F32), (wup.shape[1], BF), (wup.shape[1], BF)]
+    far = pl.BlockSpec(memory_space=pltpu.HBM)
+    return pl.pallas_call(
+        functools.partial(enter_kernel, dp_size, branch_size),
+        grid=(total // tile,),
+        in_specs=[spec(width)] + [pl.BlockSpec(x.shape, lambda i: (0, 0)) for x in whole] + [far],
+        out_specs=[spec(w) for w, _ in outs] + [far],
+        out_shape=[jax.ShapeDtypeStruct((total, w), t) for w, t in outs]
+        + [jax.ShapeDtypeStruct((dp_size * part.shape[1], part.shape[2]), BF)],
+        scratch_shapes=[dma((1, 2, groups)), dma((1, 2, groups)), dma((1,)), dma((1,)), dma((1,))],
+        compiler_params=pltpu.CompilerParams(
+            collective_id=2, has_side_effects=True, vmem_limit_bytes=ENTER_VMEM
+        ),
+        cost_estimate=pl.CostEstimate(
+            flops=2 * total * (wqkv.size + wup.size), bytes_accessed=2 * total * width, transcendentals=0
+        ),
+        name="enter",
+    )(tok_all, *whole, part)
+
+
+def branch_kernel(o_ref, u_ref, *refs):
+    more, (wo_ref, wd_ref, br_ref) = refs[:-3], refs[-3:]
+    total = dot_nt(o_ref[...], wo_ref[...]) + dot_nt(u_ref[...], wd_ref[...])
+    for ref in more:
+        total = total + ref[...].astype(F32)
+    br_ref[...] = total.astype(BF)
 
 
 def grad_kernel(gm_ref, other_ref, slope_ref, wo_ref, wd_ref, do_ref, dz_ref, sum_ref):
@@ -752,7 +833,7 @@
         out_specs=[spec(w) for w, _ in outs] + [pl.BlockSpec((8, w), lambda i: (0, 0)) for w in sums],
         out_shape=[jax.ShapeDtypeStruct((tiles * tile, w), t) for w, t in outs]
         + [jax.ShapeDtypeStruct((8, w), F32) for w in sums],
-        compiler_params=pltpu.CompilerParams(vmem_limit_bytes=VMEM_LIMIT),
+        compiler_params=pltpu.CompilerParams(vmem_limit_bytes=60 * 2**20),
         cost_estimate=pl.CostEstimate(flops=flops, bytes_accessed=traffic, transcendentals=0),
         name=name,
     )(*[x for x, _ in tiled], *whole)
@@ -783,8 +864,8 @@
     small = jnp.pad(small, (0, -small.size % 128))
     small = jnp.broadcast_to(small[None, None], (2, 16, small.size))
 
-    tok_all, wqkv, wup, wot, wdt, _, params = gather_all(
-        dp_size, branch_size, tokens, (qkv_l, up_l, out_l, down_l, small)
+    tok_all, wqkv, wup, wot, _, params = gather_all(
+        dp_size, branch_size, tokens, (qkv_l, up_l, out_l, small)
     )
     swap = [(i, i + 1 - 2 * (i % 2)) for i in range(dp_size)]
     late_cot, tok_all = lax.optimization_barrier((masked_cot, tok_all))
@@ -807,9 +888,8 @@
         return jnp.broadcast_to(values[None], (8, values.size))
 
     tiles = 2 * toks // ROW_TILE
-    h, project, u, slope = row_call(
-        enter_kernel, "enter", tiles, [(tok_all, None)], [row(gain), row(shift), wqkv, row(qkv_b), wup, row(up_b)],
-        [(width, BF), (3 * cols, F32), (hid, BF), (hid, BF)], [],
+    h, project, u, slope, wdt = enter(
+        dp_size, branch_size, tok_all, row(gain), row(shift), wqkv, row(qkv_b), wup, row(up_b), down_l
     )
     found = [rotary_tables(ids[i]) for i in range(2)]
     begins = jnp.stack([t[0] for t in found])
@@ -819,16 +899,14 @@
     gm_other = lax.ppermute(gm_own, "dp", swap)
     half_tiles = tiles // 2
 
-    def branch_out(first):
+    def branch_out(first, *more):
         def later(width):
             return pl.BlockSpec((ROW_TILE, width), lambda i: (i + first, 0))
 
-        return row_call(
-            branch_kernel, "branch_out", half_tiles, [(o, later(cols)), (u, later(hid))], [wot, wdt], [(width, BF)], []
-        )[0]
+        tiled = [(o, later(cols)), (u, later(hid))] + [(x, None) for x in more]
+        return row_call(branch_kernel, "branch_out", half_tiles, tiled, [wot, wdt], [(width, BF)], [])[0]
 
     given = lax.ppermute(branch_out(half_tiles), "dp", swap)
-    br = (branch_out(0).astype(F32) + given.astype(F32)).astype(BF)
     xfloat = tokens.astype(F32)
 
     near = pl.BlockSpec((ROW_TILE, width), lambda i: (jnp.minimum(i, half_tiles - 1), 0))
@@ -837,6 +915,8 @@
         grad_kernel, "branch_grad", tiles, [(gm_own, near), (gm_other, far), (slope, None)], [wot, wdt],
         [(cols, BF), (hid, BF)], [hid],
     )
+    do, given = lax.optimization_barrier((do, given))
+    br = branch_out(0, given)
     do, br = lax.optimization_barrier((do, br))
     summed = lax.psum_scatter(br, "branch", scatter_dimension=0, tiled=True).astype(F32)
     dqkv = attend_back(queries, keys, values, o, do, lse_rows, begins, tables)

time: 503 us -> 466 us (0.926)
  local copies, waits for them, and re-layouts: 47.8 us -> 26.7 us
  waiting for transfers between devices: 8.15 us -> 0.05 us
  Pallas kernels: 395 us -> 389 us
  other arithmetic: 29.2 us -> 23.4 us
    pallas_call x0 -> x1, Pallas kernels: none -> 50.1 us  [enter(): pl.pallas_call(functools.partial(enter_kernel, dp_size, branch_size), gri...]
    pallas_call x1, Pallas kernels: 124 us -> 94 us  [gather_all(): pl.pallas_call(functools.partial(gather_kernel, dp_size, branch_size, n_w...]
    pallas_call x5 -> x4, Pallas kernels: 93.7 us -> 64.9 us  [row_call(): pl.pallas_call(kernel, grid=(tiles,), in_specs=in_specs, out_specs=[spec(...]
    unnamed x91 -> x47, local copies, waits for them, and re-layouts: 39.7 us -> 17.2 us
    all_gather x1, waiting for transfers between devices: 8.1 us -> 0.01 us  [local(): gm_own = lax.all_gather(late_cot, 'branch', axis=0, tiled=True)]
    convert_element_type x1 -> x0, other arithmetic: 7.71 us -> none  [local(): br = (branch_out(0).astype(F32) + given.astype(F32)).astype(BF)]
  transfers between devices with their start and end apart: 5 -> 5, of which waited for: 1 -> 0; matrix products, arithmetic and copies ran while one was open for 4% -> 4% of each run, Pallas kernels for 51% -> 62%
where the time goes in v3:
time: 466 us; the launch traced here: 461 us
  Pallas kernels  389 us (83%)
  local copies, waits for them, and re-layouts  26.7 us (6%)
  other arithmetic  23.4 us (5%)
  between operations  14.7 us (3%)
  starting transfers between devices  7.16 us (2%)
    pallas_call x1, Pallas kernels, scatter_all(): pl.pallas_call(functools.partial(scatter_kernel, dp_size, branch_size), o...  137 us
    pallas_call x1, Pallas kernels, gather_all(): pl.pallas_call(functools.partial(gather_kernel, dp_size, branch_size, n_w...  94 us
    pallas_call x4, Pallas kernels, row_call(): pl.pallas_call(kernel, grid=(tiles,), in_specs=in_specs, out_specs=[spec(...  64.9 us
    pallas_call x1, Pallas kernels, enter(): pl.pallas_call(functools.partial(enter_kernel, dp_size, branch_size), gri...  50.1 us
    pallas_call x1, Pallas kernels, attend_back(): pl.pallas_call(functools.partial(attend_back_kernel, min(256, toks)), gri...  23 us
    pallas_call x1, Pallas kernels, attend(): pl.pallas_call(functools.partial(attend_kernel, min(256, toks)), grid=(bl...  20.8 us
    unnamed x47, local copies, waits for them, and re-layouts  17.2 us
  transfers between devices with their start and end apart: 5, of which 0 were waited for; matrix products, arithmetic and copies ran while one was open for 4% of the time, Pallas kernels for 62%

profile of v3, /device:TPU:1, one launch (start us, length us, event | category | flops | bytes accessed | tf_op | source)
XLA Modules:
  0.0 461.4 jit_solution(3684982682328973459)
XLA Ops:
  7.2 0.7 convert.17
  7.9 0.7 convert.18
  8.5 0.7 convert.19
  9.2 0.7 convert.21
  10.0 0.7 convert.20
  10.8 1.1 convert_element_type.74
  12.0 1.7 copy.56
  14.0 2.5 copy.58
  16.6 1.6 copy.59
  18.2 0.8 dynamic-slice_convert_fusion
  19.5 3.1 convert_reduce_fusion.1
  22.7 94.0 %gather_all.1 = (bf16[2048,2048]{1,0:T(8,128)(2,1)}, bf16[2048,768]{1,0:T(8,128)(2,1)}, bf16[2048,1024]{1,0:T(8,128)(2,1)}, bf16[2048,256]{1,0:T(8,128)(2,1)S(1)...) custom-call(bf16[256,2048]{1,0:T(8,128)(2,1)S(1)} %copy-done, bf16[2,256,768]{2,1,0:T(8,128)(2,1)S(1)} %copy.61.refs_1_, ...), custom_call_target="tpu_custom_call" | custom-call | flops 429496729600 | bytes 1048576 | tf_op jit(solution)/shard_map/gather_all/pallas_call | solution.py:231
  116.7 0.8 copy-done.6
  117.5 1.0 copy-done.7
  118.9 4.7 %collective-permute-start = (s32[1024]{0:T(1024)S(1)}, s32[1024]{0:T(1024)S(1)}, u32[]{:S(2)}, u32[]{:S(2)}) collective-permute-start(s32[1024]{0:T(1024)S(1)} %copy-done.13), channel_id=1, source_target_pairs={{0,4},{4,0},{8,12},{12,8},{16,20},{20,16},{24,28},{28,24},{1,5},{5... | collective-permute-start | bytes 12296 | tf_op jit(solution)/shard_map/ppermute | solution.py:885
  123.6 1.0 slice.50
  124.8 1.7 convert_element_type.77
  127.8 0.6 select_reduce_fusion.1
  128.5 1.9 copy-done.8
  130.4 50.1 %enter.1 = (bf16[2048,2048]{1,0:T(8,128)(2,1)}, f32[2048,768]{1,0:T(8,128)}, bf16[2048,1024]{1,0:T(8,128)(2,1)}, bf16[2048,1024]{1,0:T(8,128)(2,1)}, bf16[2048,1024]{1,0:T(8,128)(2,1)}) custom-call(bf16[2048,2048]{1,0:T(8,128)(2,1)} %get-tuple-element.47.tok_ref, f32[8,2048]{1,0:T(8,128)S(1)} %broadcast_in_dim.38.gain_ref, ...), custom_call_target="tpu_custom_call" | custom-call | flops 15032385536 | bytes 8388608 | tf_op jit(solution)/shard_map/enter/pallas_call | solution.py:757
  180.5 0.6 select_reduce_fusion
  181.2 0.6 pad_add_fusion.begin_ref
  181.9 3.8 fusion.14
  185.6 1.0 pad_maximum_fusion.2.high_ref
  186.7 1.5 pad_maximum_fusion
  188.1 20.8 %attend.1 = (bf16[2048,256]{1,0:T(8,128)(2,1)}, bf16[2048,256]{1,0:T(8,128)(2,1)}, bf16[2048,256]{1,0:T(8,128)(2,1)}, bf16[2048,256]{1,0:T(8,128)(2,1)}, f32[2,2,2,1024]{3,2,1,0:T(2,128)}) custom-call(f32[2048,768]{1,0:T(8,128)} %get-tuple-element.51.q_ref.k_ref.v_ref, f32[2048,768]{1,0:T(8,128)} %get-tuple-element.51.q_ref.k_ref.v_ref, ...), custom_call_target="tpu_custom_call" | custom-call | tf_op jit(solution)/shard_map/attend/pallas_call | solution.py:653
  209.0 2.0 collective-permute-start.1
  211.0 10.1 %branch_out.2 = bf16[1024,2048]{1,0:T(8,128)(2,1)} custom-call(bf16[2048,256]{1,0:T(8,128)(2,1)} %get-tuple-element.52.o_ref.refs_5_, bf16[2048,1024]{1,0:T(8,128)(2,1)} %get-tuple-element.58.u_ref.refs_6_, bf16[2048,256]{1,0:T(8,128)(2,1)} %copy-done.7, bf16[2048,1024]{1,0:T(8,128)(2,1)} %get-tuple-element.56.wd_ref.refs_1_.refs_2_), custom_call_target="tpu_custom_call" | custom-call | flops 5368709120 | bytes 18874368 | tf_op jit(solution)/shard_map/branch_out/pallas_call | solution.py:829
  221.1 17.1 %branch_grad.1 = (bf16[2048,256]{1,0:T(8,128)(2,1)}, bf16[2048,1024]{1,0:T(8,128)(2,1)}, f32[8,1024]{1,0:T(8,128)}) custom-call(bf16[1024,2048]{1,0:T(8,128)(2,1)} %all-gather.2.cloned.1.call-done.gm_ref.refs_1_, bf16[1024,2048]{1,0:T(8,128)(2,1)} %collective-permute-done.1.other_ref.refs_2_, bf16[2048,1024]{1,0:T(8,128)(2,1)} %get-tuple-element.54.slope_ref, ...), custom_call_target="tpu_custom_call" | custom-call | flops 10737418240 | bytes 28311552 | tf_op jit(solution)/shard_map/branch_grad/pallas_call | solution.py:829
  238.3 11.2 %branch_out.3 = bf16[1024,2048]{1,0:T(8,128)(2,1)} custom-call(bf16[2048,256]{1,0:T(8,128)(2,1)} %get-tuple-element.52.o_ref.refs_5_, bf16[2048,1024]{1,0:T(8,128)(2,1)} %get-tuple-element.58.u_ref.refs_6_, bf16[1024,2048]{1,0:T(8,128)(2,1)} %collective-permute-done.2.refs_0_, bf16[2048,256]{1,0:T(8,128)(2,1)} %copy-done.7, ...), custom_call_target="tpu_custom_call" | custom-call | flops 5368709120 | bytes 23068672 | tf_op jit(solution)/shard_map/branch_out/pallas_call | solution.py:829
  249.5 0.7 copy-done.12
  250.9 23.0 %attend_back.1.grad_ref.refs_3_ = bf16[3,2048,256]{2,1,0:T(8,128)(2,1)} custom-call(bf16[2048,256]{1,0:T(8,128)(2,1)} %get-tuple-element.63.qr_ref, bf16[2048,256]{1,0:T(8,128)(2,1)} %get-tuple-element.64.kr_ref, bf16[2048,256]{1,0:T(8,128)(2,1)} %get-tuple-element.65.vr_ref, bf16[2048,256]{1,0:T(8,128)(2,1)} %get-tuple-element.52.o_ref.refs_5_, ...), custom_call_target="tpu_custom_call" | custom-call | tf_op jit(solution)/shard_map/attend_back/pallas_call | solution.py:669
  273.9 26.4 %leave.1 = (bf16[2048,2048]{1,0:T(8,128)(2,1)}, f32[8,2048]{1,0:T(8,128)}, f32[8,768]{1,0:T(8,128)}) custom-call(bf16[2048,2048]{1,0:T(8,128)(2,1)} %get-tuple-element.47.tok_ref, bf16[3,2048,256]{2,1,0:T(8,128)(2,1)} %attend_back.1.grad_ref.refs_3_, bf16[2048,1024]{1,0:T(8,128)(2,1)} %get-tuple-element.68.dz_ref.refs_4_, ...), custom_call_target="tpu_custom_call" | custom-call | flops 15032385536 | bytes 39845888 | tf_op jit(solution)/shard_map/leave/pallas_call | solution.py:829
  300.3 0.8 slice.44
  301.2 0.8 slice_reduce_fusion
  302.1 0.8 slice_reduce_fusion.2
  303.2 136.6 %scatter_all.1 = (f32[2048,256]{1,0:T(8,128)}, f32[512,256]{1,0:T(8,128)S(1)}, f32[256,2048]{1,0:T(8,128)}, f32[3,256,512]{2,1,0:T(8,128)S(1)}, bf16[256,2048]{1...) custom-call(bf16[2048,2048]{1,0:T(8,128)(2,1)} %get-tuple-element.62, ...), custom_call_target="tpu_custom_call" | custom-call | flops 25769803776 | bytes 4194304 | tf_op jit(solution)/shard_map/scatter_all/pallas_call | solution.py:517
  439.8 1.1 copy-done.1
  440.9 0.8 copy-done.4
  441.8 0.7 reshape.562
  442.6 0.6 copy.68
  443.3 0.6 fusion.11
  444.5 3.8 fusion.9
  448.3 1.1 copy.86
  449.7 0.8 copy.87
  450.7 1.3 copy.88
  452.0 1.0 copy-done.10
  453.0 1.3 copy.89
  (100 shorter events, 5.6 us)
Async XLA Ops:
  7.2 201.8 %all-gather.2.cloned.1.call-start = ((), (), s32[]{:S(2)}) async-start(), calls=%async_computation.1 | async-start | bytes 5242880 | tf_op jit(solution)/shard_map/all_gather | solution.py:872
  16.6 6.1 %copy-start = (bf16[256,2048]{1,0:T(8,128)(2,1)S(1)}, bf16[256,2048]{1,0:T(8,128)(2,1)}, u32[]{:S(2)}) copy-start(bf16[256,2048]{1,0:T(8,128)(2,1)} %refs_0_.1) | copy-start | bytes 3145732
  18.9 0.6 copy-start.14
  22.7 96.2 %copy-start.13 = (s32[1024]{0:T(1024)S(1)}, s32[1024]{0:T(1024)}, u32[]{:S(2)}) copy-start(s32[1024]{0:T(1024)} %param.20) | copy-start | bytes 12292
  116.7 0.8 copy-start.6
  117.5 1.0 copy-start.7
  118.6 325.9 %reduce-scatter.2.cloned.1.call-start = ((), (), s32[]{:S(2)}) async-start(), calls=%async_computation.2 | async-start | bytes 5242880 | tf_op jit(solution)/shard_map/reduce_scatter | solution.py:921
  118.9 61.6 %collective-permute-start = (s32[1024]{0:T(1024)S(1)}, s32[1024]{0:T(1024)S(1)}, u32[]{:S(2)}, u32[]{:S(2)}) collective-permute-start(s32[1024]{0:T(1024)S(1)} %copy-done.13), channel_id=1, source_target_pairs={{0,4},{4,0},{8,12},{12,8},{16,20},{20,16},{24,28},{28,24},{1,5},{5... | collective-permute-start | bytes 12296 | tf_op jit(solution)/shard_map/ppermute | solution.py:885
  128.5 1.9 copy-start.8
  130.4 51.5 %copy-start.16 = (f32[128]{0:T(128)S(1)}, f32[128]{0:T(128)}, u32[]{:S(2)}) copy-start(f32[128]{0:T(128)} %constant.67) | copy-start | bytes 1540
  130.4 51.5 %copy-start.17 = (f32[128]{0:T(128)S(1)}, f32[128]{0:T(128)}, u32[]{:S(2)}) copy-start(f32[128]{0:T(128)} %constant.64.clone) | copy-start | bytes 1540
  130.4 51.5 %copy-start.18 = (f32[128]{0:T(128)S(1)}, f32[128]{0:T(128)}, u32[]{:S(2)}) copy-start(f32[128]{0:T(128)} %constant.63.clone) | copy-start | bytes 1540
  209.0 12.2 %collective-permute-start.1 = (bf16[1024,2048]{1,0:T(8,128)(2,1)}, bf16[1024,2048]{1,0:T(8,128)(2,1)}, u32[]{:S(2)}, u32[]{:S(2)}) collective-permute-start(bf16[1024,2048]{1,0:T(8,128)(2,1)} %all-gather.2.cloned.1.call-done.gm_ref.refs_1_), channel_id=1, source_target_pairs={{0,4},{4,0},{8,12},{12,8},{16,20},{20,16},{24,28},{28,24},{1,5},{5... | collective-permute-start | bytes 12582920 | tf_op jit(solution)/shard_map/ppermute | solution.py:899
  221.1 17.2 %collective-permute-start.2 = (bf16[1024,2048]{1,0:T(8,128)(2,1)}, bf16[1024,2048]{1,0:T(8,128)(2,1)}, u32[]{:S(2)}, u32[]{:S(2)}) collective-permute-start(bf16[1024,2048]{1,0:T(8,128)(2,1)} %branch_out.2), channel_id=1, source_target_pairs={{0,4},{4,0},{8,12},{12,8},{16,20},{20,16},{24,28},{28,24},{1,5},{5... | collective-permute-start | bytes 12582920 | tf_op jit(solution)/shard_map/ppermute | solution.py:909
  249.5 0.7 copy-start.12
  273.9 29.3 %copy-start.3 = (bf16[2048,256]{1,0:T(8,128)(2,1)S(1)}, bf16[2048,256]{1,0:T(8,128)(2,1)}, u32[]{:S(2)}) copy-start(bf16[2048,256]{1,0:T(8,128)(2,1)} %get-tuple-element.52.o_ref.refs_5_) | copy-start | bytes 3145732
  439.8 1.1 copy-start.1
  440.9 0.8 copy-start.4
  441.7 2.8 copy-start.9
  441.7 2.8 copy-start.15
  444.5 3.9 copy-start.2
  448.3 1.4 copy-start.5
  448.3 2.3 copy-start.11
  450.7 2.3 copy-start.10
Sparse Core Ops, SparseCore 0:
  118.7 85.6 all-gather.1
  249.6 74.4 reduce-scatter.1

commit v4 on v3

--- a/solution.py
+++ b/solution.py
@@ -189,23 +189,31 @@
 
             waits.append((None, both))
 
+    def spread():
+        params = wf_refs[n_w - 1]
+        own = pltpu.make_async_copy(params, small_out.at[at.branch], p_local)
+        own.start()
+        waits.append((None, own.wait))
+        for k in range(1, branch_size):
+            copy = remote(params, small_out.at[at.branch], p_send.at[k], p_recv.at[k], at.peers[k - 1])
+            copy.start()
+            waits.append((None, copy.wait_send))
+
     line_steps = list(range(1, branch_size))
     ring_steps = [(w, s) for s in range(1, at.groups) for w in range(n_w)]
-    events = [(23.0 * e, 0, e) for e in line_steps]
-    events += [((i + 1.0) / len(ring_steps) * 69.0, 1, e) for i, e in enumerate(ring_steps)]
+    events = [(2.0 + 23.3 * e, 0, e) for e in line_steps]
+    size = [w_refs[w].shape[1] * w_refs[w].shape[2] for w in range(n_w)]
+    period = 34.0 * sum(size) / (256 * 3072)
+    due = [sum(size[: w + 1]) / sum(size) for w in range(n_w)]
+    due[-1] = 4.0 * size[-1] / sum(size)
+    events += [(5.0 + period * (s - 1 + due[w]), 1, (w, s)) for w, s in ring_steps]
     for _, kind, event in sorted(events, key=lambda e: e[:2]):
         if kind == 0:
             line_step(event)
         else:
             ring.step(*event)
-    params = wf_refs[n_w - 1]
-    own = pltpu.make_async_copy(params, small_out.at[at.branch], p_local)
-    own.start()
-    waits.append((None, own.wait))
-    for k in range(1, branch_size):
-        copy = remote(params, small_out.at[at.branch], p_send.at[k], p_recv.at[k], at.peers[k - 1])
-        copy.start()
-        waits.append((None, copy.wait_send))
+            if event == (n_w - 1, at.groups - 1):
+                spread()
     for k in range(1, branch_size):
         slot = small_out.at[(at.branch - k + branch_size) % branch_size]
         remote(slot, slot, p_send.at[k], p_recv.at[k], at.peers[k - 1]).wait_recv()

time: 466 us -> 461 us (0.989)
  starting transfers between devices: 7.16 us -> 2.05 us
where the time goes in v4:
time: 461 us; the launch traced here: 456 us
  Pallas kernels  389 us (84%)
  local copies, waits for them, and re-layouts  27.1 us (6%)
  other arithmetic  23.4 us (5%)
  between operations  14.7 us (3%)
    pallas_call x1, Pallas kernels, scatter_all(): pl.pallas_call(functools.partial(scatter_kernel, dp_size, branch_size), o...  136 us
    pallas_call x1, Pallas kernels, gather_all(): pl.pallas_call(functools.partial(gather_kernel, dp_size, branch_size, n_w...  94.4 us
    pallas_call x4, Pallas kernels, row_call(): pl.pallas_call(kernel, grid=(tiles,), in_specs=in_specs, out_specs=[spec(...  64.9 us
    pallas_call x1, Pallas kernels, enter(): pl.pallas_call(functools.partial(enter_kernel, dp_size, branch_size), gri...  49.8 us
    pallas_call x1, Pallas kernels, attend_back(): pl.pallas_call(functools.partial(attend_back_kernel, min(256, toks)), gri...  23 us
    pallas_call x1, Pallas kernels, attend(): pl.pallas_call(functools.partial(attend_kernel, min(256, toks)), grid=(bl...  20.8 us
    unnamed x47, local copies, waits for them, and re-layouts  17.5 us
  transfers between devices with their start and end apart: 5, of which 0 were waited for; matrix products, arithmetic and copies ran while one was open for 4% of the time, Pallas kernels for 62%

profile of v4, /device:TPU:1, one launch (start us, length us, event | category | flops | bytes accessed | tf_op | source)
XLA Modules:
  0.0 456.3 jit_solution(1768667078462351074)
XLA Ops:
  7.2 0.7 convert.17
  7.9 0.7 convert.18
  8.5 0.7 convert.19
  9.2 0.7 convert.21
  10.0 0.7 convert.20
  10.8 1.1 convert_element_type.74
  12.0 1.7 copy.56
  14.0 2.5 copy.58
  16.6 1.6 copy.59
  18.2 0.8 dynamic-slice_convert_fusion
  18.9 0.6 copy-done.14
  19.5 3.1 convert_reduce_fusion.1
  22.7 94.4 %gather_all.1 = (bf16[2048,2048]{1,0:T(8,128)(2,1)}, bf16[2048,768]{1,0:T(8,128)(2,1)}, bf16[2048,1024]{1,0:T(8,128)(2,1)}, bf16[2048,256]{1,0:T(8,128)(2,1)S(1)...) custom-call(bf16[256,2048]{1,0:T(8,128)(2,1)S(1)} %copy-done, bf16[2,256,768]{2,1,0:T(8,128)(2,1)S(1)} %copy.61.refs_1_, ...), custom_call_target="tpu_custom_call" | custom-call | flops 429496729600 | bytes 1048576 | tf_op jit(solution)/shard_map/gather_all/pallas_call | solution.py:239
  117.1 0.8 copy-done.6
  117.9 1.0 copy-done.7
  119.5 1.0 slice.50
  120.7 1.7 convert_element_type.77
  123.6 0.6 select_reduce_fusion.1
  124.3 2.2 copy-done.8
  126.6 49.8 %enter.1 = (bf16[2048,2048]{1,0:T(8,128)(2,1)}, f32[2048,768]{1,0:T(8,128)}, bf16[2048,1024]{1,0:T(8,128)(2,1)}, bf16[2048,1024]{1,0:T(8,128)(2,1)}, bf16[2048,1024]{1,0:T(8,128)(2,1)}) custom-call(bf16[2048,2048]{1,0:T(8,128)(2,1)} %get-tuple-element.47.tok_ref, f32[8,2048]{1,0:T(8,128)S(1)} %broadcast_in_dim.38.gain_ref, ...), custom_call_target="tpu_custom_call" | custom-call | flops 15032385536 | bytes 8388608 | tf_op jit(solution)/shard_map/enter/pallas_call | solution.py:765
  176.4 0.6 select_reduce_fusion
  177.0 0.6 pad_add_fusion.begin_ref
  177.7 3.8 fusion.14
  181.5 1.0 pad_maximum_fusion.2.high_ref
  182.5 1.5 pad_maximum_fusion
  184.0 20.8 %attend.1 = (bf16[2048,256]{1,0:T(8,128)(2,1)}, bf16[2048,256]{1,0:T(8,128)(2,1)}, bf16[2048,256]{1,0:T(8,128)(2,1)}, bf16[2048,256]{1,0:T(8,128)(2,1)}, f32[2,2,2,1024]{3,2,1,0:T(2,128)}) custom-call(f32[2048,768]{1,0:T(8,128)} %get-tuple-element.51.q_ref.k_ref.v_ref, f32[2048,768]{1,0:T(8,128)} %get-tuple-element.51.q_ref.k_ref.v_ref, ...), custom_call_target="tpu_custom_call" | custom-call | tf_op jit(solution)/shard_map/attend/pallas_call | solution.py:661
  204.8 1.5 collective-permute-start.1
  206.3 10.1 %branch_out.2 = bf16[1024,2048]{1,0:T(8,128)(2,1)} custom-call(bf16[2048,256]{1,0:T(8,128)(2,1)} %get-tuple-element.52.o_ref.refs_5_, bf16[2048,1024]{1,0:T(8,128)(2,1)} %get-tuple-element.58.u_ref.refs_6_, bf16[2048,256]{1,0:T(8,128)(2,1)} %copy-done.7, bf16[2048,1024]{1,0:T(8,128)(2,1)} %get-tuple-element.56.wd_ref.refs_1_.refs_2_), custom_call_target="tpu_custom_call" | custom-call | flops 5368709120 | bytes 18874368 | tf_op jit(solution)/shard_map/branch_out/pallas_call | solution.py:837
  216.4 17.1 %branch_grad.1 = (bf16[2048,256]{1,0:T(8,128)(2,1)}, bf16[2048,1024]{1,0:T(8,128)(2,1)}, f32[8,1024]{1,0:T(8,128)}) custom-call(bf16[1024,2048]{1,0:T(8,128)(2,1)} %all-gather.2.cloned.1.call-done.gm_ref.refs_1_, bf16[1024,2048]{1,0:T(8,128)(2,1)} %collective-permute-done.1.other_ref.refs_2_, bf16[2048,1024]{1,0:T(8,128)(2,1)} %get-tuple-element.54.slope_ref, ...), custom_call_target="tpu_custom_call" | custom-call | flops 10737418240 | bytes 28311552 | tf_op jit(solution)/shard_map/branch_grad/pallas_call | solution.py:837
  233.6 11.2 %branch_out.3 = bf16[1024,2048]{1,0:T(8,128)(2,1)} custom-call(bf16[2048,256]{1,0:T(8,128)(2,1)} %get-tuple-element.52.o_ref.refs_5_, bf16[2048,1024]{1,0:T(8,128)(2,1)} %get-tuple-element.58.u_ref.refs_6_, bf16[1024,2048]{1,0:T(8,128)(2,1)} %collective-permute-done.2.refs_0_, bf16[2048,256]{1,0:T(8,128)(2,1)} %copy-done.7, ...), custom_call_target="tpu_custom_call" | custom-call | flops 5368709120 | bytes 23068672 | tf_op jit(solution)/shard_map/branch_out/pallas_call | solution.py:837
  244.8 0.7 copy-done.12
  246.2 23.0 %attend_back.1.grad_ref.refs_3_ = bf16[3,2048,256]{2,1,0:T(8,128)(2,1)} custom-call(bf16[2048,256]{1,0:T(8,128)(2,1)} %get-tuple-element.63.qr_ref, bf16[2048,256]{1,0:T(8,128)(2,1)} %get-tuple-element.64.kr_ref, bf16[2048,256]{1,0:T(8,128)(2,1)} %get-tuple-element.65.vr_ref, bf16[2048,256]{1,0:T(8,128)(2,1)} %get-tuple-element.52.o_ref.refs_5_, ...), custom_call_target="tpu_custom_call" | custom-call | tf_op jit(solution)/shard_map/attend_back/pallas_call | solution.py:677
  269.2 26.4 %leave.1 = (bf16[2048,2048]{1,0:T(8,128)(2,1)}, f32[8,2048]{1,0:T(8,128)}, f32[8,768]{1,0:T(8,128)}) custom-call(bf16[2048,2048]{1,0:T(8,128)(2,1)} %get-tuple-element.47.tok_ref, bf16[3,2048,256]{2,1,0:T(8,128)(2,1)} %attend_back.1.grad_ref.refs_3_, bf16[2048,1024]{1,0:T(8,128)(2,1)} %get-tuple-element.68.dz_ref.refs_4_, ...), custom_call_target="tpu_custom_call" | custom-call | flops 15032385536 | bytes 39845888 | tf_op jit(solution)/shard_map/leave/pallas_call | solution.py:837
  295.6 0.8 slice.44
  296.5 0.8 slice_reduce_fusion
  297.4 0.8 slice_reduce_fusion.2
  298.5 136.2 %scatter_all.1 = (f32[2048,256]{1,0:T(8,128)}, f32[512,256]{1,0:T(8,128)S(1)}, f32[256,2048]{1,0:T(8,128)}, f32[3,256,512]{2,1,0:T(8,128)S(1)}, bf16[256,2048]{1...) custom-call(bf16[2048,2048]{1,0:T(8,128)(2,1)} %get-tuple-element.62, ...), custom_call_target="tpu_custom_call" | custom-call | flops 25769803776 | bytes 4194304 | tf_op jit(solution)/shard_map/scatter_all/pallas_call | solution.py:525
  434.7 1.1 copy-done.1
  435.8 0.8 copy-done.4
  436.7 0.7 reshape.562
  437.5 0.6 copy.68
  438.1 0.6 fusion.11
  439.4 3.8 fusion.9
  443.2 1.1 copy.86
  444.6 0.8 copy.87
  445.5 1.3 copy.88
  446.8 1.0 copy-done.10
  447.9 1.3 copy.89
  (100 shorter events, 5.2 us)
Async XLA Ops:
  7.2 197.6 %all-gather.2.cloned.1.call-start = ((), (), s32[]{:S(2)}) async-start(), calls=%async_computation.1 | async-start | bytes 5242880 | tf_op jit(solution)/shard_map/all_gather | solution.py:880
  16.6 6.1 %copy-start = (bf16[256,2048]{1,0:T(8,128)(2,1)S(1)}, bf16[256,2048]{1,0:T(8,128)(2,1)}, u32[]{:S(2)}) copy-start(bf16[256,2048]{1,0:T(8,128)(2,1)} %refs_0_.1) | copy-start | bytes 3145732
  18.9 0.6 copy-start.14
  22.7 96.6 %copy-start.13 = (s32[1024]{0:T(1024)S(1)}, s32[1024]{0:T(1024)}, u32[]{:S(2)}) copy-start(s32[1024]{0:T(1024)} %param.20) | copy-start | bytes 12292
  117.1 0.8 copy-start.6
  117.9 1.0 copy-start.7
  119.0 320.4 %reduce-scatter.2.cloned.1.call-start = ((), (), s32[]{:S(2)}) async-start(), calls=%async_computation.2 | async-start | bytes 5242880 | tf_op jit(solution)/shard_map/reduce_scatter | solution.py:929
  119.3 57.0 %collective-permute-start = (s32[1024]{0:T(1024)S(1)}, s32[1024]{0:T(1024)S(1)}, u32[]{:S(2)}, u32[]{:S(2)}) collective-permute-start(s32[1024]{0:T(1024)S(1)} %copy-done.13), channel_id=1, source_target_pairs={{0,4},{4,0},{8,12},{12,8},{16,20},{20,16},{24,28},{28,24},{1,5},{5... | collective-permute-start | bytes 12296 | tf_op jit(solution)/shard_map/ppermute | solution.py:893
  124.3 2.2 copy-start.8
  126.5 51.1 %copy-start.16 = (f32[128]{0:T(128)S(1)}, f32[128]{0:T(128)}, u32[]{:S(2)}) copy-start(f32[128]{0:T(128)} %constant.67) | copy-start | bytes 1540
  126.5 51.1 %copy-start.17 = (f32[128]{0:T(128)S(1)}, f32[128]{0:T(128)}, u32[]{:S(2)}) copy-start(f32[128]{0:T(128)} %constant.64.clone) | copy-start | bytes 1540
  126.6 51.1 %copy-start.18 = (f32[128]{0:T(128)S(1)}, f32[128]{0:T(128)}, u32[]{:S(2)}) copy-start(f32[128]{0:T(128)} %constant.63.clone) | copy-start | bytes 1540
  204.8 11.7 %collective-permute-start.1 = (bf16[1024,2048]{1,0:T(8,128)(2,1)}, bf16[1024,2048]{1,0:T(8,128)(2,1)}, u32[]{:S(2)}, u32[]{:S(2)}) collective-permute-start(bf16[1024,2048]{1,0:T(8,128)(2,1)} %all-gather.2.cloned.1.call-done.gm_ref.refs_1_), channel_id=1, source_target_pairs={{0,4},{4,0},{8,12},{12,8},{16,20},{20,16},{24,28},{28,24},{1,5},{5... | collective-permute-start | bytes 12582920 | tf_op jit(solution)/shard_map/ppermute | solution.py:907
  216.4 17.2 %collective-permute-start.2 = (bf16[1024,2048]{1,0:T(8,128)(2,1)}, bf16[1024,2048]{1,0:T(8,128)(2,1)}, u32[]{:S(2)}, u32[]{:S(2)}) collective-permute-start(bf16[1024,2048]{1,0:T(8,128)(2,1)} %branch_out.2), channel_id=1, source_target_pairs={{0,4},{4,0},{8,12},{12,8},{16,20},{20,16},{24,28},{28,24},{1,5},{5... | collective-permute-start | bytes 12582920 | tf_op jit(solution)/shard_map/ppermute | solution.py:917
  244.8 0.7 copy-start.12
  269.2 29.3 %copy-start.3 = (bf16[2048,256]{1,0:T(8,128)(2,1)S(1)}, bf16[2048,256]{1,0:T(8,128)(2,1)}, u32[]{:S(2)}) copy-start(bf16[2048,256]{1,0:T(8,128)(2,1)} %get-tuple-element.52.o_ref.refs_5_) | copy-start | bytes 3145732
  434.6 1.1 copy-start.1
  435.8 0.8 copy-start.4
  436.6 2.8 copy-start.9
  436.6 2.8 copy-start.15
  439.3 3.9 copy-start.2
  443.2 1.4 copy-start.5
  443.2 2.3 copy-start.11
  445.5 2.3 copy-start.10
Sparse Core Ops, SparseCore 0:
  119.1 79.2 all-gather.1
  244.9 74.6 reduce-scatter.1

commit v5 on v4

--- a/solution.py
+++ b/solution.py
@@ -735,6 +735,9 @@
     h_ref[...] = h
     project_ref[...] = jnp.dot(h, wq_ref[...], preferred_element_type=F32) + qb_ref[0:1]
     z = jnp.dot(h, wu_ref[...], preferred_element_type=F32) + ub_ref[0:1]
+    if at.groups > 2:
+        pl.when(tile_at == tiles - 1)(lambda: ring.step(0, 2))
+
     scale, cubic = math.sqrt(2.0 / math.pi), 0.044715
     square = z * z
     bent = jnp.tanh(scale * z * (1.0 + cubic * square))
@@ -745,7 +748,7 @@
 
     @pl.when(tile_at == tiles - 1)
     def _():
-        for step in range(2, at.groups):
+        for step in range(3, at.groups):
             ring.step(0, step)
         ring.drain()
 

time: 461 us -> 461 us (level)
  no operation moved by 1% of the time
where the time goes in v5:
time: 461 us; the launch traced here: 457 us
  Pallas kernels  389 us (84%)
  local copies, waits for them, and re-layouts  27.3 us (6%)
  other arithmetic  23.4 us (5%)
  between operations  14.7 us (3%)
    pallas_call x1, Pallas kernels, scatter_all(): pl.pallas_call(functools.partial(scatter_kernel, dp_size, branch_size), o...  136 us
    pallas_call x1, Pallas kernels, gather_all(): pl.pallas_call(functools.partial(gather_kernel, dp_size, branch_size, n_w...  94.4 us
    pallas_call x4, Pallas kernels, row_call(): pl.pallas_call(kernel, grid=(tiles,), in_specs=in_specs, out_specs=[spec(...  64.9 us
    pallas_call x1, Pallas kernels, enter(): pl.pallas_call(functools.partial(enter_kernel, dp_size, branch_size), gri...  49.8 us
    pallas_call x1, Pallas kernels, attend_back(): pl.pallas_call(functools.partial(attend_back_kernel, min(256, toks)), gri...  23 us
    pallas_call x1, Pallas kernels, attend(): pl.pallas_call(functools.partial(attend_kernel, min(256, toks)), grid=(bl...  20.8 us
    unnamed x47, local copies, waits for them, and re-layouts  17.5 us
  transfers between devices with their start and end apart: 5, of which 0 were waited for; matrix products, arithmetic and copies ran while one was open for 4% of the time, Pallas kernels for 62%

profile of v5, /device:TPU:1, one launch (start us, length us, event | category | flops | bytes accessed | tf_op | source)
XLA Modules:
  0.0 456.6 jit_solution(9335829139208258397)
XLA Ops:
  7.2 0.7 convert.17
  7.9 0.7 convert.18
  8.5 0.7 convert.19
  9.2 0.7 convert.21
  10.0 0.7 convert.20
  10.8 1.1 convert_element_type.74
  12.0 1.7 copy.56
  14.0 2.5 copy.58
  16.6 1.6 copy.59
  18.2 0.8 dynamic-slice_convert_fusion
  19.5 3.1 convert_reduce_fusion.1
  22.7 94.4 %gather_all.1 = (bf16[2048,2048]{1,0:T(8,128)(2,1)}, bf16[2048,768]{1,0:T(8,128)(2,1)}, bf16[2048,1024]{1,0:T(8,128)(2,1)}, bf16[2048,256]{1,0:T(8,128)(2,1)S(1)...) custom-call(bf16[256,2048]{1,0:T(8,128)(2,1)S(1)} %copy-done, bf16[2,256,768]{2,1,0:T(8,128)(2,1)S(1)} %copy.61.refs_1_, ...), custom_call_target="tpu_custom_call" | custom-call | flops 429496729600 | bytes 1048576 | tf_op jit(solution)/shard_map/gather_all/pallas_call | solution.py:239
  117.1 0.8 copy-done.6
  117.9 1.0 copy-done.7
  119.2 1.0 slice.50
  120.4 1.7 convert_element_type.77
  122.1 0.8 copy.65
  123.6 0.6 select_reduce_fusion.1
  124.3 2.2 copy-done.8
  126.6 49.8 %enter.1 = (bf16[2048,2048]{1,0:T(8,128)(2,1)}, f32[2048,768]{1,0:T(8,128)}, bf16[2048,1024]{1,0:T(8,128)(2,1)}, bf16[2048,1024]{1,0:T(8,128)(2,1)}, bf16[2048,1024]{1,0:T(8,128)(2,1)}) custom-call(bf16[2048,2048]{1,0:T(8,128)(2,1)} %get-tuple-element.47.tok_ref, f32[8,2048]{1,0:T(8,128)S(1)} %broadcast_in_dim.38.gain_ref, ...), custom_call_target="tpu_custom_call" | custom-call | flops 15032385536 | bytes 8388608 | tf_op jit(solution)/shard_map/enter/pallas_call | solution.py:768
  176.4 0.6 select_reduce_fusion
  177.0 0.6 pad_add_fusion.begin_ref
  177.7 3.8 fusion.14
  181.5 1.0 pad_maximum_fusion.2.high_ref
  182.5 1.5 pad_maximum_fusion
  184.0 20.8 %attend.1 = (bf16[2048,256]{1,0:T(8,128)(2,1)}, bf16[2048,256]{1,0:T(8,128)(2,1)}, bf16[2048,256]{1,0:T(8,128)(2,1)}, bf16[2048,256]{1,0:T(8,128)(2,1)}, f32[2,2,2,1024]{3,2,1,0:T(2,128)}) custom-call(f32[2048,768]{1,0:T(8,128)} %get-tuple-element.51.q_ref.k_ref.v_ref, f32[2048,768]{1,0:T(8,128)} %get-tuple-element.51.q_ref.k_ref.v_ref, ...), custom_call_target="tpu_custom_call" | custom-call | tf_op jit(solution)/shard_map/attend/pallas_call | solution.py:661
  204.8 1.5 collective-permute-start.1
  206.3 10.1 %branch_out.2 = bf16[1024,2048]{1,0:T(8,128)(2,1)} custom-call(bf16[2048,256]{1,0:T(8,128)(2,1)} %get-tuple-element.52.o_ref.refs_5_, bf16[2048,1024]{1,0:T(8,128)(2,1)} %get-tuple-element.58.u_ref.refs_6_, bf16[2048,256]{1,0:T(8,128)(2,1)} %copy-done.7, bf16[2048,1024]{1,0:T(8,128)(2,1)} %get-tuple-element.56.wd_ref.refs_1_.refs_2_), custom_call_target="tpu_custom_call" | custom-call | flops 5368709120 | bytes 18874368 | tf_op jit(solution)/shard_map/branch_out/pallas_call | solution.py:840
  216.4 17.1 %branch_grad.1 = (bf16[2048,256]{1,0:T(8,128)(2,1)}, bf16[2048,1024]{1,0:T(8,128)(2,1)}, f32[8,1024]{1,0:T(8,128)}) custom-call(bf16[1024,2048]{1,0:T(8,128)(2,1)} %all-gather.2.cloned.1.call-done.gm_ref.refs_1_, bf16[1024,2048]{1,0:T(8,128)(2,1)} %collective-permute-done.1.other_ref.refs_2_, bf16[2048,1024]{1,0:T(8,128)(2,1)} %get-tuple-element.54.slope_ref, ...), custom_call_target="tpu_custom_call" | custom-call | flops 10737418240 | bytes 28311552 | tf_op jit(solution)/shard_map/branch_grad/pallas_call | solution.py:840
  233.6 11.2 %branch_out.3 = bf16[1024,2048]{1,0:T(8,128)(2,1)} custom-call(bf16[2048,256]{1,0:T(8,128)(2,1)} %get-tuple-element.52.o_ref.refs_5_, bf16[2048,1024]{1,0:T(8,128)(2,1)} %get-tuple-element.58.u_ref.refs_6_, bf16[1024,2048]{1,0:T(8,128)(2,1)} %collective-permute-done.2.refs_0_, bf16[2048,256]{1,0:T(8,128)(2,1)} %copy-done.7, ...), custom_call_target="tpu_custom_call" | custom-call | flops 5368709120 | bytes 23068672 | tf_op jit(solution)/shard_map/branch_out/pallas_call | solution.py:840
  244.8 0.7 copy-done.12
  246.2 23.0 %attend_back.1.grad_ref.refs_3_ = bf16[3,2048,256]{2,1,0:T(8,128)(2,1)} custom-call(bf16[2048,256]{1,0:T(8,128)(2,1)} %get-tuple-element.63.qr_ref, bf16[2048,256]{1,0:T(8,128)(2,1)} %get-tuple-element.64.kr_ref, bf16[2048,256]{1,0:T(8,128)(2,1)} %get-tuple-element.65.vr_ref, bf16[2048,256]{1,0:T(8,128)(2,1)} %get-tuple-element.52.o_ref.refs_5_, ...), custom_call_target="tpu_custom_call" | custom-call | tf_op jit(solution)/shard_map/attend_back/pallas_call | solution.py:677
  269.2 26.4 %leave.1 = (bf16[2048,2048]{1,0:T(8,128)(2,1)}, f32[8,2048]{1,0:T(8,128)}, f32[8,768]{1,0:T(8,128)}) custom-call(bf16[2048,2048]{1,0:T(8,128)(2,1)} %get-tuple-element.47.tok_ref, bf16[3,2048,256]{2,1,0:T(8,128)(2,1)} %attend_back.1.grad_ref.refs_3_, bf16[2048,1024]{1,0:T(8,128)(2,1)} %get-tuple-element.68.dz_ref.refs_4_, ...), custom_call_target="tpu_custom_call" | custom-call | flops 15032385536 | bytes 39845888 | tf_op jit(solution)/shard_map/leave/pallas_call | solution.py:840
  295.6 0.8 slice.44
  296.5 0.8 slice_reduce_fusion
  297.4 0.8 slice_reduce_fusion.2
  298.5 136.4 %scatter_all.1 = (f32[2048,256]{1,0:T(8,128)}, f32[512,256]{1,0:T(8,128)S(1)}, f32[256,2048]{1,0:T(8,128)}, f32[3,256,512]{2,1,0:T(8,128)S(1)}, bf16[256,2048]{1...) custom-call(bf16[2048,2048]{1,0:T(8,128)(2,1)} %get-tuple-element.62, ...), custom_call_target="tpu_custom_call" | custom-call | flops 25769803776 | bytes 4194304 | tf_op jit(solution)/shard_map/scatter_all/pallas_call | solution.py:525
  434.9 1.1 copy-done.1
  436.0 0.8 copy-done.4
  437.0 0.7 reshape.562
  437.7 0.6 copy.68
  438.4 0.6 fusion.11
  439.6 3.8 fusion.9
  443.5 1.1 copy.86
  444.8 0.8 copy.87
  445.8 1.3 copy.88
  447.1 1.0 copy-done.10
  448.1 1.3 copy.89
  (100 shorter events, 4.9 us)
Async XLA Ops:
  7.2 197.6 %all-gather.2.cloned.1.call-start = ((), (), s32[]{:S(2)}) async-start(), calls=%async_computation.1 | async-start | bytes 5242880 | tf_op jit(solution)/shard_map/all_gather | solution.py:883
  16.6 6.1 %copy-start = (bf16[256,2048]{1,0:T(8,128)(2,1)S(1)}, bf16[256,2048]{1,0:T(8,128)(2,1)}, u32[]{:S(2)}) copy-start(bf16[256,2048]{1,0:T(8,128)(2,1)} %refs_0_.1) | copy-start | bytes 3145732
  18.9 0.6 copy-start.14
  22.7 96.3 %copy-start.13 = (s32[1024]{0:T(1024)S(1)}, s32[1024]{0:T(1024)}, u32[]{:S(2)}) copy-start(s32[1024]{0:T(1024)} %param.20) | copy-start | bytes 12292
  117.1 0.8 copy-start.6
  117.9 1.0 copy-start.7
  119.0 320.6 %reduce-scatter.2.cloned.1.call-start = ((), (), s32[]{:S(2)}) async-start(), calls=%async_computation.2 | async-start | bytes 5242880 | tf_op jit(solution)/shard_map/reduce_scatter | solution.py:932
  119.0 57.3 %collective-permute-start = (s32[1024]{0:T(1024)S(1)}, s32[1024]{0:T(1024)S(1)}, u32[]{:S(2)}, u32[]{:S(2)}) collective-permute-start(s32[1024]{0:T(1024)S(1)} %copy-done.13), channel_id=1, source_target_pairs={{0,4},{4,0},{8,12},{12,8},{16,20},{20,16},{24,28},{28,24},{1,5},{5... | collective-permute-start | bytes 12296 | tf_op jit(solution)/shard_map/ppermute | solution.py:896
  124.3 2.2 copy-start.8
  126.5 51.1 %copy-start.16 = (f32[128]{0:T(128)S(1)}, f32[128]{0:T(128)}, u32[]{:S(2)}) copy-start(f32[128]{0:T(128)} %constant.67) | copy-start | bytes 1540
  126.5 51.1 %copy-start.17 = (f32[128]{0:T(128)S(1)}, f32[128]{0:T(128)}, u32[]{:S(2)}) copy-start(f32[128]{0:T(128)} %constant.64.clone) | copy-start | bytes 1540
  126.5 51.1 %copy-start.18 = (f32[128]{0:T(128)S(1)}, f32[128]{0:T(128)}, u32[]{:S(2)}) copy-start(f32[128]{0:T(128)} %constant.63.clone) | copy-start | bytes 1540
  204.8 11.7 %collective-permute-start.1 = (bf16[1024,2048]{1,0:T(8,128)(2,1)}, bf16[1024,2048]{1,0:T(8,128)(2,1)}, u32[]{:S(2)}, u32[]{:S(2)}) collective-permute-start(bf16[1024,2048]{1,0:T(8,128)(2,1)} %all-gather.2.cloned.1.call-done.gm_ref.refs_1_), channel_id=1, source_target_pairs={{0,4},{4,0},{8,12},{12,8},{16,20},{20,16},{24,28},{28,24},{1,5},{5... | collective-permute-start | bytes 12582920 | tf_op jit(solution)/shard_map/ppermute | solution.py:910
  216.4 17.2 %collective-permute-start.2 = (bf16[1024,2048]{1,0:T(8,128)(2,1)}, bf16[1024,2048]{1,0:T(8,128)(2,1)}, u32[]{:S(2)}, u32[]{:S(2)}) collective-permute-start(bf16[1024,2048]{1,0:T(8,128)(2,1)} %branch_out.2), channel_id=1, source_target_pairs={{0,4},{4,0},{8,12},{12,8},{16,20},{20,16},{24,28},{28,24},{1,5},{5... | collective-permute-start | bytes 12582920 | tf_op jit(solution)/shard_map/ppermute | solution.py:920
  244.8 0.7 copy-start.12
  269.2 29.3 %copy-start.3 = (bf16[2048,256]{1,0:T(8,128)(2,1)S(1)}, bf16[2048,256]{1,0:T(8,128)(2,1)}, u32[]{:S(2)}) copy-start(bf16[2048,256]{1,0:T(8,128)(2,1)} %get-tuple-element.52.o_ref.refs_5_) | copy-start | bytes 3145732
  434.9 1.1 copy-start.1
  436.0 0.8 copy-start.4
  436.8 2.8 copy-start.9
  436.8 2.8 copy-start.15
  439.6 3.9 copy-start.2
  443.5 1.4 copy-start.5
  443.5 2.3 copy-start.11
  445.8 2.3 copy-start.10
Sparse Core Ops, SparseCore 0:
  119.1 79.2 all-gather.1
  244.9 74.6 reduce-scatter.1
